TPU v7x, 512 devices: a whole 4x4x16 slice. The times are simulated.
512 devices in a mesh: rep: 16 (over z_hi, y), shard: 32 (over x, z_lo, core).
Axes of the slice: x: 4, y: 4, z: 16 (z_hi: 4, z_lo: 4; z = z_hi * 4 + z_lo), core: 2. Of those that a mesh axis runs over, the one named last changes fastest.
Arguments:
- queries: bfloat16 [16, 4096, 256], P('rep', 'shard'), may hold values from -64 to 64
- targets: int32 [16, 4096], P('rep', 'shard'), may hold values from 0 to 16383, as said below
- samp_ids: int32 [16, 128], P('rep', 'shard'), may hold values from 0 to 5, as said below
- counts: int32 [16, 32], P('rep', 'shard'), may hold values from 1 to 4, as said below
- logq: float32 [16, 128], P('rep', 'shard'), may hold values from -9 to -5
- table: float32 [24576, 256], P('shard'), may hold values from -1 to 1
- first_moment: float32 [24576, 256], P('shard'), may hold values from -2 to 2
- second_moment: float32 [24576, 256], P('shard'), may hold values from 0.01 to 1
Outputs:
- loss: float32 [16, 4096], P('rep', 'shard')
- query_grad: float32 [16, 4096, 256], P('rep', 'shard')
- new_table: float32 [24576, 256], P('shard')
- new_first: float32 [24576, 256], P('shard')
- new_second: float32 [24576, 256], P('shard')
Inputs may be any that keep to these rules, and one draw needn't show every extreme that they name: In each group some device counts 4; when a device counts 4, the device of its group whose shard index differs in the lowest bit counts at most 2. `samp_ids`: the 4 numbers listed for one device are distinct. `targets`: the slot always lies in a live block of the query's group.
All inputs are finite; a program needn't handle non-finite values.
Results may differ from a plain program's by a relative error of at most 0.0085.
Values may be sent and summed in bfloat16 or wider, within the bound.
No kernel may reach another device: no remote copies, remote signals or barrier semaphores. Data moves between devices by JAX's collectives and lax.ppermute only.
A program may use at most 64 MiB of HBM per device.

v0:
```python
import jax
import jax.numpy as jnp
from jax import lax
from jax.sharding import PartitionSpec as P

BLOCK = 128


logit_scale = 2.0
beta_first = 0.9
beta_second = 0.99
learn_rate = 0.01
adam_eps = 1e-08
bias_first = 1.0 - 0.9**10
bias_second = 1.0 - 0.99**10
floor_value = -1e30


def adam_update(weights, first, second, gradient):
    first = beta_first * first + (1.0 - beta_first) * gradient
    second = beta_second * second + (1.0 - beta_second) * gradient * gradient
    weights = weights - learn_rate * (first / bias_first) / (
        jnp.sqrt(second / bias_second) + adam_eps
    )
    return (weights, first, second)


def add_totals(carry, scores, marked, active):
    run_top, run_sum, run_pick = carry
    masked = jnp.where(active, scores, floor_value)
    top = jnp.maximum(run_top, jnp.max(masked, axis=1))
    fresh = jnp.sum(jnp.where(active, jnp.exp(masked - top[:, None]), 0.0), axis=1)
    run_sum = run_sum * jnp.exp(run_top - top) + fresh
    run_pick = run_pick + jnp.sum(jnp.where(marked, scores, 0.0), axis=1)
    return (top, run_sum, run_pick)


def local(queries, targets, samp_ids, counts, logq, table, first_moment, second_moment):
    local_rows = queries.shape[1]
    slot_count = samp_ids.shape[1]
    shard_index = lax.axis_index("shard")
    every_query = lax.all_gather(queries[0], "shard", axis=0, tiled=True)
    every_target = lax.all_gather(targets[0], "shard", axis=0, tiled=True)
    group_rows = every_query.shape[0]
    table_half = table.astype(jnp.bfloat16)
    own_base = shard_index * (slot_count * BLOCK)
    columns = jnp.arange(BLOCK, dtype=jnp.int32)
    block_count = counts[0, 0]
    block_ids = samp_ids[0]
    block_shift = logq[0]

    def score_block(items, shift, base):
        product = lax.dot_general(
            every_query, items, (((1,), (1,)), ((), ())), preferred_element_type=jnp.float32
        )
        scores = logit_scale * product - shift
        marked = (every_target - base)[:, None] == columns[None, :]
        return (scores, marked)

    def local_block(number):
        items = lax.dynamic_slice_in_dim(table_half, block_ids[number] * BLOCK, BLOCK, 0)
        scores, marked = score_block(items, block_shift[number], own_base + number * BLOCK)
        return (items, scores, marked)

    start_carry = (
        jnp.full((group_rows,), floor_value, jnp.float32),
        jnp.zeros((group_rows,), jnp.float32),
        jnp.zeros((group_rows,), jnp.float32),
    )
    carry = start_carry
    for number in range(slot_count):
        first_items, first_scores, first_marked = local_block(number)
        carry = add_totals(carry, first_scores, first_marked, number < block_count)
    run_top, run_sum, run_pick = carry
    top = lax.pmax(run_top, "shard")
    total_sum, picked = lax.psum((run_sum * jnp.exp(run_top - top), run_pick), "shard")
    norm_total = top + jnp.log(total_sum)
    grad_carry = (jnp.zeros(table.shape, jnp.float32), jnp.zeros(every_query.shape, jnp.float32))
    for number in range(slot_count):
        second_gradients, second_query_acc = grad_carry
        second_items, second_scores, second_marked = local_block(number)
        probs = jnp.where(number < block_count, jnp.exp(second_scores - norm_total[:, None]), 0.0)
        dlogit = (probs - second_marked.astype(jnp.float32)).astype(jnp.bfloat16)
        item_part = logit_scale * lax.dot_general(
            dlogit, every_query, (((0,), (0,)), ((), ())), preferred_element_type=jnp.float32
        )
        query_part = logit_scale * jnp.dot(dlogit, second_items, preferred_element_type=jnp.float32)
        second_gradients = lax.dynamic_update_slice_in_dim(
            second_gradients, item_part, block_ids[number] * BLOCK, 0
        )
        grad_carry = (second_gradients, second_query_acc + query_part)
    gradients, query_acc = grad_carry
    query_grad = lax.psum_scatter(query_acc, "shard", scatter_dimension=0, tiled=True)
    own_loss = lax.dynamic_slice_in_dim(norm_total - picked, shard_index * local_rows, local_rows)
    summed = lax.psum(gradients, "rep")
    new_table, new_first, new_second = adam_update(table, first_moment, second_moment, summed)
    return (
        own_loss.reshape(1, local_rows),
        query_grad.reshape(1, local_rows, query_grad.shape[1]),
        new_table,
        new_first,
        new_second,
    )


def solution(mesh):
    in_specs = (
        P("rep", "shard", None),
        P("rep", "shard"),
        P("rep", "shard"),
        P("rep", "shard"),
        P("rep", "shard"),
        P("shard", None),
        P("shard", None),
        P("shard", None),
    )
    out_specs = (
        P("rep", "shard"),
        P("rep", "shard", None),
        P("shard", None),
        P("shard", None),
        P("shard", None),
    )
    return jax.shard_map(local, mesh=mesh, in_specs=in_specs, out_specs=out_specs, check_vma=False)
```

profile of v0, /device:TPU:1, one launch (start us, length us, event | category | flops | bytes accessed | tf_op | source)
XLA Modules:
  0.0 749.4 jit_solution(13756900587345434302)
XLA Ops:
  7.2 0.0 all-gather.4.cloned.1.call-start
  7.2 0.7 all-gather.4.cloned.1.call-update
  7.9 0.0 all-reduce.3.cloned.1.call-start
  7.9 1.4 fusion.68
  12.6 1.2 convert_element_type.27
  13.8 45.9 %all-gather.1 = s32[1,4096]{1,0:T(1,128)S(1)} all-gather(s32[1,128]{1,0:T(1,128)} %param.9), channel_id=3, replica_groups=mesh['rep'=16,'shard'=32] {'shard'}, dimensions={1}, use_global_device_ids=true | all-gather | bytes 16896 | tf_op jit(solution)/shard_map/all_gather | solution.py:43
  59.7 1.4 fusion.69
  61.2 19.4 %all-gather.4.cloned.1.call-done = bf16[1,4096,256]{2,1,0:T(8,128)(2,1)} async-done(((bf16[1,128,256]{2,1,0:T(8,128)(2,1)}), bf16[1,4096,256]{2,1,0:T(8,128)(2,1)}) %all-gather.4.cloned.1.call-update) | async-done | bytes 2097168 | tf_op jit(solution)/shard_map/all_gather | solution.py:42
  80.6 4.5 select_reduce_fusion.8
  85.1 0.0 copy-done
  85.1 2.8 select_reduce_fusion.9
  88.0 2.8 select_reduce_fusion.10
  90.8 2.9 select_reduce_fusion.11
  93.6 130.0 %pmax.7 = f32[4096]{0:T(1024)S(1)} all-reduce(f32[4096]{0:T(1024)S(1)} %get-tuple-element.18), channel_id=1, replica_groups=mesh['rep'=16,'shard'=32] {'shard'}, use_global_device_ids=true, to_apply=%region_4.5 | all-reduce | flops 4096 | bytes 32768 | tf_op jit(solution)/shard_map/pmax | solution.py:75
  223.7 3.9 select_reduce_fusion.4
  227.6 0.0 copy-done.1
  227.6 0.0 copy-done.6
  227.6 1.5 select_reduce_fusion.6
  229.1 133.2 %all-reduce = (f32[4096]{0:T(1024)S(1)}, f32[4096]{0:T(1024)S(1)}) all-reduce(f32[4096]{0:T(1024)S(1)} %add_add_fusion, f32[4096]{0:T(1024)S(1)} %exponential_multiply_fusion), channel_id=1, replica_groups=mesh['rep'=16,'shard'=32] {'shard'}, use_global_device_ids=true, to_apply=%region_14.15 | all-reduce | flops 8192 | bytes 65536 | tf_op jit(solution)/shard_map/psum | solution.py:76
  362.4 2.5 fusion.52
  364.9 0.0 copy-done.7
  364.9 0.0 copy-start.2
  364.9 2.8 convolution_add_fusion.2
  367.7 0.1 broadcast_in_dim.59
  367.8 0.0 copy-done.2
  367.8 0.7 fusion.24
  368.5 0.0 copy-start.5
  368.5 0.7 fusion.30
  369.3 0.9 copy-done.5
  370.1 0.7 fusion.36
  370.8 0.9 copy-done.3
  371.7 0.7 fusion.42
  372.4 0.0 copy-start.8
  372.4 0.9 copy-done.8
  373.3 0.0 all-reduce.3.cloned.1.call-update
  373.3 0.0 copy-start.4
  373.3 0.2 reduce-scatter.2.cloned.1.call-start
  373.5 3.8 convolution_add_fusion.1
  377.4 0.0 copy-done.4
  377.4 3.1 fusion
  380.5 0.0 reduce-scatter.2.cloned.1.call-update
  380.5 0.6 fusion.63
  381.1 193.0 %all-reduce.3.cloned.1.call-done = f32[768,256]{1,0:T(8,128)} async-done(((f32[768,256]{1,0:T(8,128)}), f32[768,256]{1,0:T(8,128)}) %all-reduce.3.cloned.1.call-update) | async-done | bytes 786448 | tf_op jit(solution)/shard_map/psum | solution.py:95
  574.1 0.0 copy-done.9
  574.1 0.0 copy-done.10
  574.1 0.0 copy-done.11
  574.1 2.8 divide_subtract_fusion
  576.9 165.9 %reduce-scatter.2.cloned.1.call-done = f32[128,256]{1,0:T(8,128)} async-done(((f32[4096,256]{1,0:T(8,128)}), f32[128,256]{1,0:T(8,128)}) %reduce-scatter.2.cloned.1.call-update) | async-done | bytes 131088 | tf_op jit(solution)/shard_map/reduce_scatter | solution.py:93
  (13 shorter events, 0.1 us)
Async XLA Ops:
  7.2 73.4 %all-gather.4.cloned.1.call-start = ((), (), s32[]{:S(2)}) async-start(), calls=%async_computation.3 | async-start | bytes 2162688 | tf_op jit(solution)/shard_map/all_gather | solution.py:42
  7.9 566.2 %all-reduce.3.cloned.1.call-start = ((), (), s32[]{:S(2)}) async-start(), calls=%async_computation.2 | async-start | bytes 1572864 | tf_op jit(solution)/shard_map/psum | solution.py:95
  80.6 4.5 copy-start
  223.7 3.9 copy-start.1
  223.7 3.9 copy-start.6
  362.4 2.5 copy-start.7
  364.9 2.9 copy-start.2
  368.5 1.6 copy-start.5
  370.1 1.6 copy-start.3
  372.4 0.9 copy-start.8
  373.3 4.1 copy-start.4
  373.3 369.5 %reduce-scatter.2.cloned.1.call-start = ((), (), s32[]{:S(2)}) async-start(), calls=%async_computation.1 | async-start | bytes 4325376 | tf_op jit(solution)/shard_map/reduce_scatter | solution.py:93
  380.5 193.6 %copy-start.9 = (f32[768,256]{1,0:T(8,128)S(1)}, f32[768,256]{1,0:T(8,128)}, u32[]{:S(2)}) copy-start(f32[768,256]{1,0:T(8,128)} %param.13) | copy-start | bytes 2359300
  380.5 193.6 %copy-start.10 = (f32[768,256]{1,0:T(8,128)S(1)}, f32[768,256]{1,0:T(8,128)}, u32[]{:S(2)}) copy-start(f32[768,256]{1,0:T(8,128)} %param.14) | copy-start | bytes 2359300
  380.5 193.6 %copy-start.11 = (f32[768,256]{1,0:T(8,128)S(1)}, f32[768,256]{1,0:T(8,128)}, u32[]{:S(2)}) copy-start(f32[768,256]{1,0:T(8,128)} %param.15) | copy-start | bytes 2359300
Sparse Core Ops, SparseCore 0:
  10.1 70.4 all-gather.3
  373.4 200.6 all-reduce.2
  577.5 165.3 reduce-scatter.1
where the time goes:
time: 754 us; the launch traced here: 749 us
  waiting for transfers between devices  379 us (50%)
  blocking collectives  309 us (41%)
  matrix products  28 us (4%)
  between operations  17.2 us (2%)
  other arithmetic  10 us (1%)
    psum x1, waiting for transfers between devices, local(): summed = lax.psum(gradients, 'rep')  193 us
    reduce_scatter x1, waiting for transfers between devices, local(): lax.psum_scatter(query_acc, 'shard', scatter_dimension=0, tiled=True)  166 us
    psum x1, blocking collectives, local(): lax.psum((run_sum * jnp.exp(run_top - top), run_pick), 'shard')  133 us
    pmax x1, blocking collectives, local(): top = lax.pmax(run_top, 'shard')  130 us
    all_gather x1, blocking collectives, local(): every_target = lax.all_gather(targets[0], 'shard', axis=0, tiled=True)  45.9 us
    all_gather x1, waiting for transfers between devices, local(): every_query = lax.all_gather(queries[0], 'shard', axis=0, tiled=True)  19.4 us
  transfers between devices with their start and end apart: 3, of which 3 were waited for; matrix products, arithmetic and copies ran while one was open for 2% of the time, Pallas kernels for 0%

commit v1 on v0

v1 whole, which is shorter than its diff:
```python
import jax
import jax.numpy as jnp
from jax import lax
from jax.experimental import pallas as pl
from jax.experimental.pallas import tpu as pltpu
from jax.sharding import Mesh, PartitionSpec as P

BLOCK = 128
D = 256
SLOTS_DEV = 4
BLOCKS_DEV = 6
NX = 4
NY = 4
NZ = 4
NC = 2
NQ = NZ * NC
SLOTS = NX * SLOTS_DEV
PART = BLOCK // NY
META = 16
CHUNK = 256
CHUNKS = NQ * BLOCK // CHUNK
QROWS = ("c", "zl")

logit_scale = 2.0
beta_first = 0.9
beta_second = 0.99
learn_rate = 0.01
adam_eps = 1e-08
bias_first = 1.0 - 0.9**10
bias_second = 1.0 - 0.99**10
floor_value = -1e30

f32 = jnp.float32
bf16 = jnp.bfloat16
i32 = jnp.int32


def vmem():
    return pl.BlockSpec(memory_space=pltpu.VMEM)


def smem():
    return pl.BlockSpec(memory_space=pltpu.SMEM)


def pack_kernel(ids, count, logq, table, queries, targets, item_out, query_out, rows, sems):
    copies = []
    for j in range(SLOTS_DEV):
        start = pl.multiple_of(ids[0, j] * BLOCK, BLOCK)
        copy = pltpu.make_async_copy(table.at[pl.ds(start, BLOCK), :], rows.at[j], sems.at[j])
        copy.start()
        copies.append(copy)
    row = lax.broadcasted_iota(i32, (META, D), 0)
    lane = lax.broadcasted_iota(i32, (META, D), 1)
    meta = jnp.where(row == 4, count[0, 0].astype(f32), 0.0)
    for j in range(SLOTS_DEV):
        whole = jnp.full((META, D), logq[0, j], f32)
        high = whole.astype(bf16).astype(f32)
        mid = (whole - high).astype(bf16).astype(f32)
        low = whole - high - mid
        ident = jnp.full((META, D), ids[0, j].astype(f32), f32)
        value = jnp.where(row == 0, high, jnp.where(row == 1, mid, jnp.where(row == 2, low, ident)))
        meta = jnp.where((lane == j) & (row < 4), value, meta)
    item_out[pl.ds(SLOTS_DEV * BLOCK, META), :] = meta.astype(bf16)
    slot = (targets[...] >> 7).astype(f32)
    item = (targets[...] & (BLOCK - 1)).astype(f32)
    both = jnp.concatenate([slot, item], axis=1)
    query_out[pl.ds(0, BLOCK), :] = queries[0]
    query_out[pl.ds(BLOCK, META), :] = jnp.broadcast_to(both, (META, D)).astype(bf16)
    for j in range(SLOTS_DEV):
        copies[j].wait()
        item_out[pl.ds(j * BLOCK, BLOCK), :] = rows[j].astype(bf16)


def slot_tables(items, live, shifts):
    lane = lax.broadcasted_iota(i32, (1, D), 1)
    number = jnp.int32(0)
    for x in range(NX):
        meta = items[x, pl.ds(SLOTS_DEV * BLOCK, META), :].astype(f32)
        row = meta[0:1] + meta[1:2] + meta[2:3]
        count = jnp.max(meta[4:5]).astype(i32)
        for j in range(SLOTS_DEV):
            shifts[x * SLOTS_DEV + j] = jnp.sum(jnp.where(lane == j, row, 0.0))
            live[number] = x * SLOTS_DEV + j
            number = number + (j < count).astype(i32)
    return number


def query_chunk(queries, b):
    return jnp.concatenate([queries[2 * b, pl.ds(0, BLOCK), :], queries[2 * b + 1, pl.ds(0, BLOCK), :]], axis=0)


def target_chunk(queries, b):
    first = queries[2 * b, pl.ds(BLOCK, META), :].astype(f32)[0:1]
    second = queries[2 * b + 1, pl.ds(BLOCK, META), :].astype(f32)[0:1]
    slot = jnp.concatenate([first[:, :BLOCK], second[:, :BLOCK]], axis=1)
    item = jnp.concatenate([first[:, BLOCK:], second[:, BLOCK:]], axis=1)
    return slot.astype(i32), item.astype(i32)


def slot_rows(items, slot):
    x = slot // SLOTS_DEV
    j = slot % SLOTS_DEV
    return items[x, pl.ds(pl.multiple_of(j * BLOCK, BLOCK), BLOCK), :]


def group_slot(place, slot):
    x = slot // SLOTS_DEV
    return x * (NQ * SLOTS_DEV) + place * SLOTS_DEV + slot % SLOTS_DEV


def products(rows, query_rows):
    return lax.dot_general(rows, query_rows, (((1,), (1,)), ((), ())), preferred_element_type=f32)


def totals_kernel(place, items, queries, out, live, shifts, tops, sums, picks):
    number = slot_tables(items, live, shifts)
    tops[...] = jnp.full(tops.shape, floor_value, f32)
    sums[...] = jnp.zeros(sums.shape, f32)
    picks[...] = jnp.zeros(picks.shape, f32)
    item_index = lax.broadcasted_iota(i32, (BLOCK, CHUNK), 0)

    def one_slot(i, carry):
        slot = live[i]
        shift = shifts[slot]
        rows = slot_rows(items, slot)
        mine = group_slot(place[0], slot)
        for b in range(CHUNKS):
            cols = pl.ds(b * CHUNK, CHUNK)
            target_slot, target_item = target_chunk(queries, b)
            wanted = jnp.where(target_slot == mine, target_item, -1)
            scores = logit_scale * products(rows, query_chunk(queries, b)) - shift
            split = scores.reshape(BLOCK // 8, 8, CHUNK)
            old = tops[:, cols]
            top = jnp.maximum(old, jnp.max(split, axis=0))
            fresh = jnp.sum(jnp.exp(split - top[None]), axis=0)
            sums[:, cols] = sums[:, cols] * jnp.exp(old - top) + fresh
            tops[:, cols] = top
            marked = jnp.where(item_index == wanted, scores, 0.0).reshape(BLOCK // 8, 8, CHUNK)
            picks[:, cols] = picks[:, cols] + jnp.sum(marked, axis=0)
        return carry

    lax.fori_loop(0, number, one_slot, 0)
    top = jnp.max(tops[...], axis=0, keepdims=True)
    total = jnp.sum(sums[...] * jnp.exp(tops[...] - top), axis=0, keepdims=True)
    norm = top + jnp.log(total)
    pick = jnp.sum(picks[...], axis=0, keepdims=True)
    norms = jnp.concatenate([norm[:, r * BLOCK : (r + 1) * BLOCK] for r in range(NQ)], axis=0)
    for d in range(NQ):
        out[d, pl.ds(0, NQ), :] = norms
        out[d, pl.ds(NQ, NQ), :] = jnp.broadcast_to(pick[:, d * BLOCK : (d + 1) * BLOCK], (NQ, BLOCK))


def grads_kernel(place, items, queries, stats, loss_out, item_out, query_out, live, shifts, gone, rows_all):
    number = slot_tables(items, live, shifts)
    item_out[...] = jnp.zeros(item_out.shape, bf16)
    for x in range(NX):
        meta = items[x, pl.ds(SLOTS_DEV * BLOCK, META), :]
        for y in range(NY):
            item_out[y * NX + x, pl.ds(SLOTS_DEV * PART, META), :] = meta
    top = stats[0, pl.ds(0, NQ), :]
    pick = stats[0, pl.ds(NQ, NQ), :]
    for r in range(1, NQ):
        top = jnp.maximum(top, stats[r, pl.ds(0, NQ), :])
        pick = pick + stats[r, pl.ds(NQ, NQ), :]
    total = jnp.zeros_like(top)
    for r in range(NQ):
        total = total + jnp.exp(stats[r, pl.ds(0, NQ), :] - top)
    norms = top + jnp.log(total)
    own = lax.broadcasted_iota(i32, norms.shape, 0) == place[1]
    loss_out[...] = jnp.sum(jnp.where(own, norms - pick, 0.0), axis=0, keepdims=True)
    item_index = lax.broadcasted_iota(i32, (BLOCK, CHUNK), 0)

    def one_slot(i, carry):
        slot = live[i]
        shift = shifts[slot]
        rows = slot_rows(items, slot)
        rows_all[i] = rows
        mine = group_slot(place[0], slot)
        part = jnp.zeros((BLOCK, D), f32)
        for b in range(CHUNKS):
            target_slot, target_item = target_chunk(queries, b)
            wanted = jnp.where(target_slot == mine, target_item, -1)
            norm = jnp.concatenate([norms[2 * b : 2 * b + 1], norms[2 * b + 1 : 2 * b + 2]], axis=1)
            query_rows = query_chunk(queries, b)
            scores = logit_scale * products(rows, query_rows) - shift
            probs = jnp.exp(scores - norm)
            dlogit = jnp.where(item_index == wanted, probs - 1.0, probs).astype(bf16)
            gone[i, :, pl.ds(b * CHUNK, CHUNK)] = dlogit
            part = part + jnp.dot(dlogit, query_rows, preferred_element_type=f32)
        part = (logit_scale * part).astype(bf16)
        x = slot // SLOTS_DEV
        j = slot % SLOTS_DEV
        for y in range(NY):
            item_out[y * NX + x, pl.ds(pl.multiple_of(j * PART, PART), PART), :] = part[y * PART : (y + 1) * PART]
        return carry

    lax.fori_loop(0, number, one_slot, 0)
    groups = (number + SLOTS_DEV - 1) // SLOTS_DEV

    def pad(i, carry):
        rows_all[i] = jnp.zeros((BLOCK, D), bf16)
        gone[i] = jnp.zeros((BLOCK, NQ * BLOCK), bf16)
        return carry

    lax.fori_loop(number, groups * SLOTS_DEV, pad, 0)
    for b in range(CHUNKS):

        def one_group(g, total):
            four = pl.ds(g * SLOTS_DEV, SLOTS_DEV)
            rows = rows_all[four].reshape(SLOTS_DEV * BLOCK, D)
            dlogit = gone[four, :, pl.ds(b * CHUNK, CHUNK)].reshape(SLOTS_DEV * BLOCK, CHUNK)
            return total + lax.dot_general(
                rows, dlogit, (((0,), (0,)), ((), ())), preferred_element_type=f32
            )

        total = lax.fori_loop(0, groups, one_group, jnp.zeros((D, CHUNK), f32))
        total = (logit_scale * total).astype(bf16)
        query_out[2 * b] = total[:, :BLOCK]
        query_out[2 * b + 1] = total[:, BLOCK:]


def gather_parts_kernel(parts, out, total):
    lane = lax.broadcasted_iota(i32, (1, D), 1)
    total[...] = jnp.zeros(total.shape, f32)
    for y in range(NY):
        meta = parts[y * NX, pl.ds(SLOTS_DEV * PART, META), :].astype(f32)
        for j in range(SLOTS_DEV):
            block = jnp.sum(jnp.where(lane == j, meta[3:4], 0.0)).astype(i32)
            piece = jnp.zeros((PART, D), f32)
            for x in range(NX):
                piece = piece + parts[y * NX + x, pl.ds(j * PART, PART), :].astype(f32)
            total[block] = total[block] + piece
    out[...] = total[...].astype(bf16)


def adam_kernel(gradient, table, first, second, table_out, first_out, second_out):
    grad = gradient[...].reshape(BLOCK, D)
    first_new = beta_first * first[...] + (1.0 - beta_first) * grad
    second_new = beta_second * second[...] + (1.0 - beta_second) * grad * grad
    first_out[...] = first_new
    second_out[...] = second_new
    table_out[...] = table[...] - learn_rate * (first_new / bias_first) / (
        jnp.sqrt(second_new / bias_second) + adam_eps
    )


def spread(value, axes, size):
    return lax.all_to_all(jnp.broadcast_to(value[None], (size,) + value.shape), axes, 0, 0, tiled=True)


def local(queries, targets, samp_ids, counts, logq, table, first_moment, second_moment):
    place = lax.axis_index("zl") * NC + lax.axis_index("c")
    own = lax.axis_index("c") * NZ + lax.axis_index("zl")
    where = jnp.stack([place, own]).astype(i32)
    item_rows, query_rows = pl.pallas_call(
        pack_kernel,
        out_shape=(
            jax.ShapeDtypeStruct((SLOTS_DEV * BLOCK + META, D), bf16),
            jax.ShapeDtypeStruct((BLOCK + META, D), bf16),
        ),
        in_specs=[smem(), smem(), smem(), pl.BlockSpec(memory_space=pl.ANY), vmem(), vmem()],
        out_specs=(vmem(), vmem()),
        scratch_shapes=[pltpu.VMEM((SLOTS_DEV, BLOCK, D), f32), pltpu.SemaphoreType.DMA((SLOTS_DEV,))],
        name="pack",
    )(samp_ids, counts, logq, table, queries, targets)

    every_query = spread(query_rows, "zl", NZ)
    every_query = lax.all_gather(every_query, "c", axis=0, tiled=True)
    every_item = spread(item_rows, "x", NX)

    tables = [pltpu.SMEM((SLOTS,), i32), pltpu.SMEM((SLOTS,), f32)]
    stats = pl.pallas_call(
        totals_kernel,
        out_shape=jax.ShapeDtypeStruct((NQ, 2 * NQ, BLOCK), f32),
        in_specs=[smem(), vmem(), vmem()],
        out_specs=vmem(),
        scratch_shapes=tables + [pltpu.VMEM((8, NQ * BLOCK), f32)] * 3,
        name="totals",
    )(where, every_item, every_query)
    stats = lax.all_to_all(stats, QROWS, 0, 0, tiled=True)

    loss, item_parts, query_parts = pl.pallas_call(
        grads_kernel,
        out_shape=(
            jax.ShapeDtypeStruct((1, BLOCK), f32),
            jax.ShapeDtypeStruct((NY * NX, SLOTS_DEV * PART + META, D), bf16),
            jax.ShapeDtypeStruct((NQ, D, BLOCK), bf16),
        ),
        in_specs=[smem(), vmem(), vmem(), vmem()],
        out_specs=(vmem(), vmem(), vmem()),
        scratch_shapes=tables
        + [pltpu.VMEM((SLOTS, BLOCK, NQ * BLOCK), bf16), pltpu.VMEM((SLOTS, BLOCK, D), bf16)],
        name="grads",
    )(where, every_item, every_query, stats)

    item_parts = lax.all_to_all(item_parts, ("y", "x"), 0, 0, tiled=True)
    rows_part = pl.pallas_call(
        gather_parts_kernel,
        out_shape=jax.ShapeDtypeStruct((BLOCKS_DEV, PART, D), bf16),
        in_specs=[vmem()],
        out_specs=vmem(),
        scratch_shapes=[pltpu.VMEM((BLOCKS_DEV, PART, D), f32)],
        name="gather_parts",
    )(item_parts)
    rows_part = jnp.sum(spread(rows_part, "zh", 4).astype(f32), axis=0)
    every_part = spread(rows_part, "y", NY)

    query_parts = lax.all_to_all(query_parts, QROWS, 0, 0, tiled=True)
    query_grad = jnp.sum(query_parts.astype(f32), axis=0).T

    block = pl.BlockSpec((BLOCK, D), lambda b: (b, 0))
    new_table, new_first, new_second = pl.pallas_call(
        adam_kernel,
        grid=(BLOCKS_DEV,),
        out_shape=(jax.ShapeDtypeStruct(table.shape, f32),) * 3,
        in_specs=[pl.BlockSpec((NY, None, PART, D), lambda b: (0, b, 0, 0)), block, block, block],
        out_specs=(block, block, block),
        name="adam",
    )(every_part, table, first_moment, second_moment)
    return loss, query_grad[None], new_table, new_first, new_second


def solution(mesh):
    fine = Mesh(mesh.devices.reshape(4, NY, NX, NZ, NC), ("zh", "y", "x", "zl", "c"))
    rep = ("zh", "y")
    shard = ("x", "zl", "c")
    in_specs = (
        P(rep, shard, None),
        P(rep, shard),
        P(rep, shard),
        P(rep, shard),
        P(rep, shard),
        P(shard, None),
        P(shard, None),
        P(shard, None),
    )
    out_specs = (
        P(rep, shard),
        P(rep, shard, None),
        P(shard, None),
        P(shard, None),
        P(shard, None),
    )
    return jax.shard_map(local, mesh=fine, in_specs=in_specs, out_specs=out_specs, check_vma=False)
```

time: 754 us -> 174 us (0.23)
  waiting for transfers between devices: 379 us -> 34.4 us
  blocking collectives: 309 us -> 83.6 us
  matrix products: 28 us -> 0 us
  Pallas kernels: 0 us -> 27.9 us
  starting transfers between devices: 0.3 us -> 17.6 us
  between operations: 17.2 us -> 1.33 us
  other arithmetic: 10 us -> 0.71 us
    psum x1 -> x0, waiting for transfers between devices: 193 us -> none  [local(): summed = lax.psum(gradients, 'rep')]
    reduce_scatter x1 -> x0, waiting for transfers between devices: 166 us -> none  [local(): lax.psum_scatter(query_acc, 'shard', scatter_dimension=0, tiled=True)]
    psum x1 -> x0, blocking collectives: 133 us -> none  [local(): lax.psum((run_sum * jnp.exp(run_top - top), run_pick), 'shard')]
    pmax x1 -> x0, blocking collectives: 130 us -> none  [local(): top = lax.pmax(run_top, 'shard')]
    all_to_all x0 -> x4, blocking collectives: none -> 79.4 us  [the longest x2 44.2 us: spread(): lax.all_to_all(jnp.broadcast_to(value[None], (size,) + value.shape), axes...]
    all_gather x1, blocking collectives: 45.9 us -> 4.24 us  [local(): every_query = lax.all_gather(every_query, 'c', axis=0, tiled=True)]
    all_to_all x0 -> x3, waiting for transfers between devices: none -> 34.4 us  [the longest x2 19.9 us: spread(): lax.all_to_all(jnp.broadcast_to(value[None], (size,) + value.shape), axes...]
    dot_general x12 -> x0, matrix products: 28 us -> none  [the longest x4 13 us: score_block(): lax.dot_general(every_query, items, (((1,), (1,)), ((), ())), preferred_e...]
  transfers between devices with their start and end apart: 3 -> 3, of which waited for: 3 -> 3; matrix products, arithmetic and copies ran while one was open for 2% -> 1% of each run, Pallas kernels for 0% -> 0%
where the time goes in v1:
time: 174 us; the launch traced here: 173 us
  blocking collectives  83.6 us (48%)
  waiting for transfers between devices  34.4 us (20%)
  Pallas kernels  27.9 us (16%)
  starting transfers between devices  17.6 us (10%)
  local copies, waits for them, and re-layouts  7.46 us (4%)
    all_to_all x2, blocking collectives, spread(): lax.all_to_all(jnp.broadcast_to(value[None], (size,) + value.shape), axes...  44.2 us
    all_to_all x1, blocking collectives, local(): item_parts = lax.all_to_all(item_parts, ('y', 'x'), 0, 0, tiled=True)  22.9 us
    all_to_all x2, waiting for transfers between devices, spread(): lax.all_to_all(jnp.broadcast_to(value[None], (size,) + value.shape), axes...  19.9 us
    all_to_all x1, waiting for transfers between devices, local(): query_parts = lax.all_to_all(query_parts, QROWS, 0, 0, tiled=True)  14.6 us
    all_to_all x1, blocking collectives, local(): stats = lax.all_to_all(stats, QROWS, 0, 0, tiled=True)  12.3 us
    pallas_call x1, Pallas kernels, local(): pl.pallas_call(grads_kernel, out_shape=(jax.ShapeDtypeStruct((1, BLOCK),...  11.6 us
    all_to_all x2, starting transfers between devices, spread(): lax.all_to_all(jnp.broadcast_to(value[None], (size,) + value.shape), axes...  9.43 us
    all_to_all x1, starting transfers between devices, local(): query_parts = lax.all_to_all(query_parts, QROWS, 0, 0, tiled=True)  8.21 us
  transfers between devices with their start and end apart: 3, of which 3 were waited for; matrix products, arithmetic and copies ran while one was open for 1% of the time, Pallas kernels for 0%

profile of v1, /device:TPU:1, one launch (start us, length us, event | category | flops | bytes accessed | tf_op | source)
XLA Modules:
  0.0 173.1 jit_solution(9565184439147991526)
XLA Ops:
  1.3 2.7 %pack.1 = (bf16[528,256]{1,0:T(8,128)(2,1)}, bf16[144,256]{1,0:T(8,128)(2,1)}) custom-call(s32[1,4]{1,0:T(1,128)} %ids.1, s32[1,1]{1,0:T(1,128)S(6)} %copy.15.count, f32[1,4]{1,0:T(1,128)} %logq.1, f32[768,256]{1,0:T(8,128)} %table.3, bf16[1,128,256]{2,1,0:T(8,128)(2,1)} %queries.1, s32[1,128]{1,0:T(1,128)} %targets.1), custom_call_target="tpu_custom_call" | custom-call | tf_op jit(solution)/shard_map/pack/pallas_call | solution.py:256
  4.0 0.9 broadcast_in_dim.11
  4.9 12.8 %all_to_all.35 = bf16[4,144,256]{2,1,0:T(8,128)(2,1)S(1)} all-to-all(bf16[4,144,256]{2,1,0:T(8,128)(2,1)S(1)} %broadcast_in_dim.11), channel_id=1, replica_groups=mesh['zh'=4,'y'=4,'x'=4,'zl'=4,'c'=2] {'zl'}, dimensions={0} | all-to-all | bytes 589824 | tf_op jit(solution)/shard_map/all_to_all | solution.py:249
  17.8 2.0 %broadcast_in_dim.10 = bf16[4,528,256]{2,1,0:T(8,128)(2,1)} broadcast(bf16[528,256]{1,0:T(8,128)(2,1)} %get-tuple-element.13), dimensions={1,2} | broadcast | bytes 1351680 | tf_op jit(solution)/shard_map/broadcast_in_dim | solution.py:249
  19.8 5.9 %all-to-all-start = ((bf16[4,528,256]{2,1,0:T(8,128)(2,1)}), bf16[4,528,256]{2,1,0:T(8,128)(2,1)S(1)}, u32[]{:S(2)}, u32[]{:S(2)}) async-start(bf16[4,528,256]{2,1,0:T(8,128)(2,1)} %broadcast_in_dim.10), calls=%async_computation | async-start | bytes 2162688 | tf_op jit(solution)/shard_map/all_to_all | solution.py:249
  25.7 0.6 pad_add_fusion.place
  26.3 4.2 %all_gather.3.queries = bf16[8,144,256]{2,1,0:T(8,128)(2,1)} all-gather(bf16[4,144,256]{2,1,0:T(8,128)(2,1)S(1)} %all_to_all.35), channel_id=1, replica_groups=mesh['zh'=4,'y'=4,'x'=4,'zl'=4,'c'=2] {'c'}, dimensions={0}, use_global_device_ids=true | all-gather | bytes 884736 | tf_op jit(solution)/shard_map/all_gather | solution.py:269
  30.5 8.5 %all-to-all-done.items = bf16[4,528,256]{2,1,0:T(8,128)(2,1)S(1)} async-done(((bf16[4,528,256]{2,1,0:T(8,128)(2,1)}), bf16[4,528,256]{2,1,0:T(8,128)(2,1)S(1)}, u32[]{:S(2)}, u32[]{:S(2)}) %all-to-all-start) | async-done | bytes 1081376 | tf_op jit(solution)/shard_map/all_to_all | solution.py:249
  39.0 0.0 copy-start
  39.0 1.0 copy-done
  40.0 6.3 %totals.1 = f32[8,16,128]{2,1,0:T(8,128)} custom-call(s32[2]{0:T(128)} %pad_add_fusion.place, bf16[4,528,256]{2,1,0:T(8,128)(2,1)} %copy-done, bf16[8,144,256]{2,1,0:T(8,128)(2,1)} %all_gather.3.queries), custom_call_target="tpu_custom_call" | custom-call | tf_op jit(solution)/shard_map/totals/pallas_call | solution.py:273
  46.3 12.3 %all_to_all.36.stats = f32[8,16,128]{2,1,0:T(8,128)} all-to-all(f32[8,16,128]{2,1,0:T(8,128)} %totals.1), channel_id=1, replica_groups=mesh['zh'=4,'y'=4,'x'=4,'zl'=4,'c'=2] {'c','zl'}, dimensions={0} | all-to-all | bytes 131072 | tf_op jit(solution)/shard_map/all_to_all | solution.py:281
  58.5 11.6 %grads.1 = (f32[1,128]{1,0:T(1,128)}, bf16[16,144,256]{2,1,0:T(8,128)(2,1)}, bf16[8,256,128]{2,1,0:T(8,128)(2,1)}) custom-call(s32[2]{0:T(128)} %pad_add_fusion.place, bf16[4,528,256]{2,1,0:T(8,128)(2,1)} %copy-done, bf16[8,144,256]{2,1,0:T(8,128)(2,1)} %all_gather.3.queries, f32[8,16,128]{2,1,0:T(8,128)} %all_to_all.36.stats), custom_call_target="tpu_custom_call" | custom-call | tf_op jit(solution)/shard_map/grads/pallas_call | solution.py:283
  70.1 22.9 %all_to_all.37.parts = bf16[16,144,256]{2,1,0:T(8,128)(2,1)} all-to-all(bf16[16,144,256]{2,1,0:T(8,128)(2,1)} %get-tuple-element.17), channel_id=1, replica_groups=mesh['zh'=4,'y'=4,'x'=4,'zl'=4,'c'=2] {'y','x'}, dimensions={0} | all-to-all | bytes 2359296 | tf_op jit(solution)/shard_map/all_to_all | solution.py:297
  93.1 2.2 %gather_parts.1 = bf16[6,32,256]{2,1,0:T(8,128)(2,1)} custom-call(bf16[16,144,256]{2,1,0:T(8,128)(2,1)} %all_to_all.37.parts), custom_call_target="tpu_custom_call" | custom-call | tf_op jit(solution)/shard_map/gather_parts/pallas_call | solution.py:298
  95.2 0.9 broadcast_in_dim.13
  96.2 31.3 %all_to_all.38 = bf16[4,6,32,256]{3,2,1,0:T(8,128)(2,1)S(1)} all-to-all(bf16[4,6,32,256]{3,2,1,0:T(8,128)(2,1)S(1)} %broadcast_in_dim.13), channel_id=1, replica_groups=mesh['zh'=4,'y'=4,'x'=4,'zl'=4,'c'=2] {'zh'}, dimensions={0} | all-to-all | bytes 786432 | tf_op jit(solution)/shard_map/all_to_all | solution.py:249
  127.5 8.2 %all-to-all-start.3 = ((bf16[8,256,128]{2,1,0:T(8,128)(2,1)}), bf16[8,256,128]{2,1,0:T(8,128)(2,1)S(1)}, u32[]{:S(2)}, u32[]{:S(2)}) async-start(bf16[8,256,128]{2,1,0:T(8,128)(2,1)} %get-tuple-element.16), calls=%async_computation.3 | async-start | bytes 1048576 | tf_op jit(solution)/shard_map/all_to_all | solution.py:309
  135.7 0.1 convert_reduce_fusion.1
  135.8 14.6 %all-to-all-done.3 = bf16[8,256,128]{2,1,0:T(8,128)(2,1)S(1)} async-done(((bf16[8,256,128]{2,1,0:T(8,128)(2,1)}), bf16[8,256,128]{2,1,0:T(8,128)(2,1)S(1)}, u32[]{:S(2)}, u32[]{:S(2)}) %all-to-all-start.3) | async-done | bytes 524320 | tf_op jit(solution)/shard_map/all_to_all | solution.py:309
  150.4 1.0 broadcast_in_dim.14
  151.3 3.5 %all-to-all-start.6 = ((f32[4,6,32,256]{3,2,1,0:T(8,128)}), f32[4,6,32,256]{3,2,1,0:T(8,128)S(1)}, u32[]{:S(2)}, u32[]{:S(2)}) async-start(f32[4,6,32,256]{3,2,1,0:T(8,128)} %broadcast_in_dim.14), calls=%async_computation.6 | async-start | bytes 1572864 | tf_op jit(solution)/shard_map/all_to_all | solution.py:249
  154.8 0.1 convert_reduce_fusion
  154.9 0.8 copy.14
  155.7 11.4 %all-to-all-done.6.gradient = f32[4,6,32,256]{3,2,1,0:T(8,128)S(1)} async-done(((f32[4,6,32,256]{3,2,1,0:T(8,128)}), f32[4,6,32,256]{3,2,1,0:T(8,128)S(1)}, u32[]{:S(2)}, u32[]{:S(2)}) %all-to-all-start.6) | async-done | bytes 786464 | tf_op jit(solution)/shard_map/all_to_all | solution.py:249
  167.1 0.0 copy-start.1
  167.1 0.9 copy-done.1
  168.0 5.2 %adam.1 = (f32[768,256]{1,0:T(8,128)}, f32[768,256]{1,0:T(8,128)}, f32[768,256]{1,0:T(8,128)}) custom-call(f32[4,6,32,256]{3,2,1,0:T(8,128)} %copy-done.1, f32[768,256]{1,0:T(8,128)} %table.3, f32[768,256]{1,0:T(8,128)} %first.1, f32[768,256]{1,0:T(8,128)} %second.1), custom_call_target="tpu_custom_call" | custom-call | tf_op jit(solution)/shard_map/adam/pallas_call | solution.py:313
Async XLA Ops:
  19.8 19.2 %all-to-all-start = ((bf16[4,528,256]{2,1,0:T(8,128)(2,1)}), bf16[4,528,256]{2,1,0:T(8,128)(2,1)S(1)}, u32[]{:S(2)}, u32[]{:S(2)}) async-start(bf16[4,528,256]{2,1,0:T(8,128)(2,1)} %broadcast_in_dim.10), calls=%async_computation | async-start | bytes 2162688 | tf_op jit(solution)/shard_map/all_to_all | solution.py:249
  39.0 1.0 copy-start
  127.5 22.9 %all-to-all-start.3 = ((bf16[8,256,128]{2,1,0:T(8,128)(2,1)}), bf16[8,256,128]{2,1,0:T(8,128)(2,1)S(1)}, u32[]{:S(2)}, u32[]{:S(2)}) async-start(bf16[8,256,128]{2,1,0:T(8,128)(2,1)} %get-tuple-element.16), calls=%async_computation.3 | async-start | bytes 1048576 | tf_op jit(solution)/shard_map/all_to_all | solution.py:309
  151.3 15.7 %all-to-all-start.6 = ((f32[4,6,32,256]{3,2,1,0:T(8,128)}), f32[4,6,32,256]{3,2,1,0:T(8,128)S(1)}, u32[]{:S(2)}, u32[]{:S(2)}) async-start(f32[4,6,32,256]{3,2,1,0:T(8,128)} %broadcast_in_dim.14), calls=%async_computation.6 | async-start | bytes 1572864 | tf_op jit(solution)/shard_map/all_to_all | solution.py:249
  167.1 0.9 copy-start.1

commit v2 on v1

v2 whole, which is shorter than its diff:
```python
import jax
import jax.numpy as jnp
from jax import lax
from jax.experimental import pallas as pl
from jax.experimental.pallas import tpu as pltpu
from jax.sharding import Mesh, PartitionSpec as P

BLOCK = 128
D = 256
SLOTS_DEV = 4
BLOCKS_DEV = 6
NX = 4
NY = 4
NZ = 4
NC = 2
NQ = NZ * NC
SLOTS = NX * SLOTS_DEV
PART = BLOCK // NY
META = 16
CHUNK = 256
CHUNKS = NQ * BLOCK // CHUNK
TOGETHER = 4
QROWS = ("c", "zl")

logit_scale = 2.0
beta_first = 0.9
beta_second = 0.99
learn_rate = 0.01
adam_eps = 1e-08
bias_first = 1.0 - 0.9**10
bias_second = 1.0 - 0.99**10
floor_value = -1e30

f32 = jnp.float32
bf16 = jnp.bfloat16
i32 = jnp.int32


def vmem():
    return pl.BlockSpec(memory_space=pltpu.VMEM)


def hbm():
    return pl.BlockSpec(memory_space=pltpu.HBM)


def smem():
    return pl.BlockSpec(memory_space=pltpu.SMEM)


def limit(mib):
    return pltpu.CompilerParams(vmem_limit_bytes=mib << 20)


def pack_kernel(ids, count, logq, table, queries, targets, item_out, query_out, rows, sems):
    copies = []
    for j in range(SLOTS_DEV):
        start = pl.multiple_of(ids[0, j] * BLOCK, BLOCK)
        copy = pltpu.make_async_copy(table.at[pl.ds(start, BLOCK), :], rows.at[j], sems.at[j])
        copy.start()
        copies.append(copy)
    slot = (targets[...] >> 7).astype(f32)
    item = (targets[...] & (BLOCK - 1)).astype(f32)
    both = jnp.broadcast_to(jnp.concatenate([slot, item], axis=1), (META, D)).astype(bf16)
    for z in range(NZ):
        query_out[z, pl.ds(0, BLOCK), :] = queries[0]
        query_out[z, pl.ds(BLOCK, META), :] = both
    row = lax.broadcasted_iota(i32, (META, D), 0)
    lane = lax.broadcasted_iota(i32, (META, D), 1)
    meta = jnp.where(row == 4, count[0, 0].astype(f32), 0.0)
    for j in range(SLOTS_DEV):
        whole = jnp.full((META, D), logq[0, j], f32)
        high = whole.astype(bf16).astype(f32)
        mid = (whole - high).astype(bf16).astype(f32)
        low = whole - high - mid
        ident = jnp.full((META, D), ids[0, j].astype(f32), f32)
        value = jnp.where(row == 0, high, jnp.where(row == 1, mid, jnp.where(row == 2, low, ident)))
        meta = jnp.where((lane == j) & (row < 4), value, meta)
    item_out[pl.ds(SLOTS_DEV * BLOCK, META), :] = meta.astype(bf16)
    for j in range(SLOTS_DEV):
        copies[j].wait()
        item_out[pl.ds(j * BLOCK, BLOCK), :] = (logit_scale * rows[j].astype(bf16).astype(f32)).astype(bf16)


def list_live(place, pieces, rows_all, live, shifts):
    lane = lax.broadcasted_iota(i32, (1, D), 1)
    number = jnp.int32(0)
    for k in range(NX):
        x = (place[2] - k) & (NX - 1)
        meta = pieces[k][pl.ds(SLOTS_DEV * BLOCK, META), :].astype(f32)
        row = meta[0:1] + meta[1:2] + meta[2:3]
        count = jnp.max(meta[4:5]).astype(i32)
        for j in range(SLOTS_DEV):
            shifts[number] = jnp.sum(jnp.where(lane == j, row, 0.0))
            live[number] = x * (NQ * SLOTS_DEV) + place[0] * SLOTS_DEV + j
            rows_all[number] = pieces[k][pl.ds(j * BLOCK, BLOCK), :]
            number = number + (j < count).astype(i32)
    return number


def query_chunk(queries, b):
    return jnp.concatenate([queries[2 * b, pl.ds(0, BLOCK), :], queries[2 * b + 1, pl.ds(0, BLOCK), :]], axis=0)


def target_chunk(queries, b):
    first = queries[2 * b, pl.ds(BLOCK, META), :].astype(f32)[0:1]
    second = queries[2 * b + 1, pl.ds(BLOCK, META), :].astype(f32)[0:1]
    slot = jnp.concatenate([first[:, :BLOCK], second[:, :BLOCK]], axis=1)
    item = jnp.concatenate([first[:, BLOCK:], second[:, BLOCK:]], axis=1)
    return slot.astype(i32), item.astype(i32)


def products(rows, query_rows):
    return lax.dot_general(rows, query_rows, (((1,), (1,)), ((), ())), preferred_element_type=f32)


def totals_kernel(place, own, one, two, three, queries, out, rows_all, live, shifts, tops, sums, picks):
    number = list_live(place, (own, one, two, three), rows_all, live, shifts)
    tops[...] = jnp.full(tops.shape, floor_value, f32)
    sums[...] = jnp.zeros(sums.shape, f32)
    picks[...] = jnp.zeros(picks.shape, f32)
    item_index = lax.broadcasted_iota(i32, (BLOCK, CHUNK), 0)

    def one_slot(i, carry):
        shift = shifts[i]
        rows = rows_all[i]
        mine = live[i]
        for b in range(CHUNKS):
            cols = pl.ds(b * CHUNK, CHUNK)
            target_slot, target_item = target_chunk(queries, b)
            wanted = jnp.where(target_slot == mine, target_item, -1)
            doubled = products(rows, query_chunk(queries, b))
            split = doubled.reshape(BLOCK // 8, 8, CHUNK)
            old = tops[:, cols]
            top = jnp.maximum(old, jnp.max(split, axis=0) - shift)
            base = top + shift
            fresh = jnp.sum(jnp.exp(split - base[None]), axis=0)
            sums[:, cols] = sums[:, cols] * jnp.exp(old - top) + fresh
            tops[:, cols] = top
            marked = jnp.where(item_index == wanted, doubled - shift, 0.0).reshape(BLOCK // 8, 8, CHUNK)
            picks[:, cols] = picks[:, cols] + jnp.sum(marked, axis=0)
        return carry

    lax.fori_loop(0, number, one_slot, 0)
    top = jnp.max(tops[...], axis=0, keepdims=True)
    total = jnp.sum(sums[...] * jnp.exp(tops[...] - top), axis=0, keepdims=True)
    norm = top + jnp.log(total)
    pick = jnp.sum(picks[...], axis=0, keepdims=True)
    norms = jnp.concatenate([norm[:, r * BLOCK : (r + 1) * BLOCK] for r in range(NQ)], axis=0)
    for d in range(NQ):
        out[d, pl.ds(0, NQ), :] = norms
        out[d, pl.ds(NQ, NQ), :] = jnp.broadcast_to(pick[:, d * BLOCK : (d + 1) * BLOCK], (NQ, BLOCK))


def item_kernel(
    place, own, one, two, three, queries, stats, number_out, loss_out, item_out, gone, rows_all, live, shifts
):
    pieces = (own, one, two, three)
    number = list_live(place, pieces, rows_all, live, shifts)
    number_out[0] = number
    item_out[...] = jnp.zeros(item_out.shape, bf16)
    for k in range(NX):
        x = (place[2] - k) & (NX - 1)
        meta = pieces[k][pl.ds(SLOTS_DEV * BLOCK, META), :]
        for y in range(NY):
            item_out[y * NX + x, pl.ds(SLOTS_DEV * PART, META), :] = meta
    top = stats[0, pl.ds(0, NQ), :]
    pick = stats[0, pl.ds(NQ, NQ), :]
    for r in range(1, NQ):
        top = jnp.maximum(top, stats[r, pl.ds(0, NQ), :])
        pick = pick + stats[r, pl.ds(NQ, NQ), :]
    total = jnp.zeros_like(top)
    for r in range(NQ):
        total = total + jnp.exp(stats[r, pl.ds(0, NQ), :] - top)
    norms = top + jnp.log(total)
    mine = lax.broadcasted_iota(i32, norms.shape, 0) == place[1]
    loss_out[...] = jnp.sum(jnp.where(mine, norms - pick, 0.0), axis=0, keepdims=True)
    item_index = lax.broadcasted_iota(i32, (BLOCK, CHUNK), 0)

    def one_slot(i, carry):
        shift = shifts[i]
        rows = rows_all[i]
        slot = live[i]
        part = jnp.zeros((BLOCK, D), f32)
        for b in range(CHUNKS):
            target_slot, target_item = target_chunk(queries, b)
            wanted = jnp.where(target_slot == slot, target_item, -1)
            norm = jnp.concatenate([norms[2 * b : 2 * b + 1], norms[2 * b + 1 : 2 * b + 2]], axis=1)
            query_rows = query_chunk(queries, b)
            probs = jnp.exp(products(rows, query_rows) - (norm + shift))
            dlogit = jnp.where(item_index == wanted, probs - 1.0, probs).astype(bf16)
            gone[i, :, pl.ds(b * CHUNK, CHUNK)] = dlogit
            part = part + jnp.dot(dlogit, query_rows, preferred_element_type=f32)
        part = (logit_scale * part).astype(bf16)
        x = slot // (NQ * SLOTS_DEV)
        j = slot % SLOTS_DEV
        for y in range(NY):
            item_out[y * NX + x, pl.ds(pl.multiple_of(j * PART, PART), PART), :] = part[y * PART : (y + 1) * PART]
        return carry

    lax.fori_loop(0, number, one_slot, 0)

    def pad(i, carry):
        rows_all[i] = jnp.zeros((BLOCK, D), bf16)
        gone[i] = jnp.zeros((BLOCK, NQ * BLOCK), bf16)
        return carry

    lax.fori_loop(number, (number + TOGETHER - 1) // TOGETHER * TOGETHER, pad, 0)


def query_kernel(number, rows_all, gone, out, total):
    total[...] = jnp.zeros(total.shape, f32)

    def one_group(g, carry):
        some = pl.ds(g * TOGETHER, TOGETHER)
        rows = rows_all[some].reshape(TOGETHER * BLOCK, D).T
        for b in range(CHUNKS):
            cols = pl.ds(b * CHUNK, CHUNK)
            dlogit = gone[some, :, cols].reshape(TOGETHER * BLOCK, CHUNK)
            total[:, cols] = total[:, cols] + jnp.dot(rows, dlogit, preferred_element_type=f32)
        return carry

    lax.fori_loop(0, (number[0] + TOGETHER - 1) // TOGETHER, one_group, 0)
    for r in range(NQ):
        out[r] = total[:, pl.ds(r * BLOCK, BLOCK)].astype(bf16)


def gather_parts_kernel(parts, out, total):
    lane = lax.broadcasted_iota(i32, (1, D), 1)
    total[...] = jnp.zeros(total.shape, f32)
    for y in range(NY):
        meta = parts[y * NX, pl.ds(SLOTS_DEV * PART, META), :].astype(f32)
        for j in range(SLOTS_DEV):
            block = jnp.sum(jnp.where(lane == j, meta[3:4], 0.0)).astype(i32)
            piece = jnp.zeros((PART, D), f32)
            for x in range(NX):
                piece = piece + parts[y * NX + x, pl.ds(j * PART, PART), :].astype(f32)
            total[block] = total[block] + piece
    out[...] = total[...].astype(bf16)


def adam_kernel(gradient, table, first, second, table_out, first_out, second_out, tables, firsts, seconds, sems):
    copies = []
    for b in range(BLOCKS_DEV):
        rows = pl.ds(b * BLOCK, BLOCK)
        grad = gradient[:, b].reshape(BLOCK, D)
        first_new = beta_first * first[rows, :] + (1.0 - beta_first) * grad
        second_new = beta_second * second[rows, :] + (1.0 - beta_second) * grad * grad
        firsts[rows, :] = first_new
        seconds[rows, :] = second_new
        tables[rows, :] = table[rows, :] - learn_rate * (first_new / bias_first) / (
            jnp.sqrt(second_new / bias_second) + adam_eps
        )
        for n, (value, out) in enumerate(((tables, table_out), (firsts, first_out), (seconds, second_out))):
            copy = pltpu.make_async_copy(value.at[rows, :], out.at[rows, :], sems.at[b, n])
            copy.start()
            copies.append(copy)
    for copy in copies:
        copy.wait()


def spread(value, axes, size):
    return lax.all_to_all(jnp.broadcast_to(value[None], (size,) + value.shape), axes, 0, 0, tiled=True)


def step(queries, targets, samp_ids, counts, logq, table, first_moment, second_moment):
    place = lax.axis_index("zl") * NC + lax.axis_index("c")
    own = lax.axis_index("c") * NZ + lax.axis_index("zl")
    where = jnp.stack([place, own, lax.axis_index("x")]).astype(i32)
    item_shape = jax.ShapeDtypeStruct((SLOTS_DEV * BLOCK + META, D), bf16)
    items, query_rows = pl.pallas_call(
        pack_kernel,
        out_shape=(item_shape, jax.ShapeDtypeStruct((NZ, BLOCK + META, D), bf16)),
        in_specs=[smem(), smem(), smem(), hbm(), vmem(), vmem()],
        out_specs=(vmem(), vmem()),
        scratch_shapes=[pltpu.VMEM((SLOTS_DEV, BLOCK, D), f32), pltpu.SemaphoreType.DMA((SLOTS_DEV,))],
        name="pack",
    )(samp_ids, counts, logq, table, queries, targets)

    every_query = lax.all_to_all(query_rows, "zl", 0, 0, tiled=True)
    pieces = [items]
    for k in range(1, NX):
        pieces.append(lax.ppermute(items, "x", [(i, (i + k) % NX) for i in range(NX)]))
    every_query = lax.all_gather(every_query, "c", axis=0, tiled=True)

    tables = [pltpu.SMEM((SLOTS + 1,), i32), pltpu.SMEM((SLOTS + 1,), f32)]
    rows_spec = pltpu.VMEM((SLOTS + 1, BLOCK, D), bf16)
    stats = pl.pallas_call(
        totals_kernel,
        out_shape=jax.ShapeDtypeStruct((NQ, 2 * NQ, BLOCK), f32),
        in_specs=[smem()] + [vmem()] * (NX + 1),
        out_specs=vmem(),
        scratch_shapes=[rows_spec] + tables + [pltpu.VMEM((8, NQ * BLOCK), f32)] * 3,
        compiler_params=limit(10),
        name="totals",
    )(where, *pieces, every_query)
    stats = lax.all_to_all(stats, QROWS, 0, 0, tiled=True)

    number, loss, item_parts, gone, rows_all = pl.pallas_call(
        item_kernel,
        out_shape=(
            jax.ShapeDtypeStruct((1,), i32),
            jax.ShapeDtypeStruct((1, BLOCK), f32),
            jax.ShapeDtypeStruct((NY * NX, SLOTS_DEV * PART + META, D), bf16),
            jax.ShapeDtypeStruct((SLOTS, BLOCK, NQ * BLOCK), bf16),
            jax.ShapeDtypeStruct((SLOTS + 1, BLOCK, D), bf16),
        ),
        in_specs=[smem()] + [vmem()] * (NX + 2),
        out_specs=(smem(), vmem(), vmem(), vmem(), vmem()),
        scratch_shapes=tables,
        compiler_params=limit(16),
        name="items",
    )(where, *pieces, every_query, stats)

    item_parts = lax.all_to_all(item_parts, ("y", "x"), 0, 0, tiled=True)
    query_parts = pl.pallas_call(
        query_kernel,
        out_shape=jax.ShapeDtypeStruct((NQ, D, BLOCK), bf16),
        in_specs=[smem(), vmem(), vmem()],
        out_specs=vmem(),
        scratch_shapes=[pltpu.VMEM((D, NQ * BLOCK), f32)],
        compiler_params=limit(12),
        cost_estimate=pl.CostEstimate(flops=1 << 30, bytes_accessed=6 << 20, transcendentals=0),
        name="query_parts",
    )(number, rows_all, gone)
    part = pl.pallas_call(
        gather_parts_kernel,
        out_shape=jax.ShapeDtypeStruct((BLOCKS_DEV, PART, D), bf16),
        in_specs=[vmem()],
        out_specs=vmem(),
        scratch_shapes=[pltpu.VMEM((BLOCKS_DEV, PART, D), f32)],
        compiler_params=limit(4),
        name="gather_parts",
    )(item_parts)
    other = lax.ppermute(part, "zh", [(0, 1), (1, 0), (2, 3), (3, 2)])
    part = lax.optimization_barrier((part.astype(f32) + other.astype(f32)).astype(bf16))
    other = lax.ppermute(part, "zh", [(1, 2), (2, 1), (3, 0), (0, 3)])
    part = part.astype(f32) + other.astype(f32)
    query_parts = lax.all_to_all(query_parts, QROWS, 0, 0, tiled=True)
    query_grad = jnp.sum(query_parts.astype(f32), axis=0).T
    every_part = spread(part, "y", NY)

    new_table, new_first, new_second = pl.pallas_call(
        adam_kernel,
        out_shape=(jax.ShapeDtypeStruct(table.shape, f32),) * 3,
        in_specs=[vmem()] * 4,
        out_specs=(hbm(),) * 3,
        scratch_shapes=[pltpu.VMEM(table.shape, f32)] * 3 + [pltpu.SemaphoreType.DMA((BLOCKS_DEV, 3))],
        compiler_params=limit(12),
        name="adam",
    )(every_part, table, first_moment, second_moment)
    return loss, query_grad[None], new_table, new_first, new_second


def solution(mesh):
    fine = Mesh(mesh.devices.reshape(4, NY, NX, NZ, NC), ("zh", "y", "x", "zl", "c"))
    rep = ("zh", "y")
    shard = ("x", "zl", "c")
    in_specs = (
        P(rep, shard, None),
        P(rep, shard),
        P(rep, shard),
        P(rep, shard),
        P(rep, shard),
        P(shard, None),
        P(shard, None),
        P(shard, None),
    )
    out_specs = (
        P(rep, shard),
        P(rep, shard, None),
        P(shard, None),
        P(shard, None),
        P(shard, None),
    )
    return jax.shard_map(step, mesh=fine, in_specs=in_specs, out_specs=out_specs, check_vma=False)
```

time: 174 us -> 139 us (0.80)
  the two profiles are of different devices: /device:TPU:1 before, /device:TPU:32 now
where the time goes in v2:
time: 139 us; the launch traced here: 138 us
  starting transfers between devices  51.5 us (37%)
  waiting for transfers between devices  47.2 us (34%)
  Pallas kernels  16.2 us (12%)
  blocking collectives  13.8 us (10%)
  local copies, waits for them, and re-layouts  6.65 us (5%)
  between operations  1.44 us (1%)
    all_to_all x1, waiting for transfers between devices, step(): item_parts = lax.all_to_all(item_parts, ('y', 'x'), 0, 0, tiled=True)  17.3 us
    ppermute x1, starting transfers between devices, step(): other = lax.ppermute(part, 'zh', [(1, 2), (2, 1), (3, 0), (0, 3)])  13.5 us
    all_to_all x1, blocking collectives, step(): stats = lax.all_to_all(stats, QROWS, 0, 0, tiled=True)  11.6 us
    all_to_all x1, waiting for transfers between devices, spread(): lax.all_to_all(jnp.broadcast_to(value[None], (size,) + value.shape), axes...  10.6 us
    ppermute x1, starting transfers between devices, step(): other = lax.ppermute(part, 'zh', [(0, 1), (1, 0), (2, 3), (3, 2)])  9.31 us
    all_to_all x1, starting transfers between devices, step(): every_query = lax.all_to_all(query_rows, 'zl', 0, 0, tiled=True)  9.02 us
    ppermute x3, waiting for transfers between devices, step(): lax.ppermute(items, 'x', [(i, (i + k) % NX) for i in range(NX)])  8.49 us
    ppermute x3, starting transfers between devices, step(): lax.ppermute(items, 'x', [(i, (i + k) % NX) for i in range(NX)])  7.75 us
  transfers between devices with their start and end apart: 9, of which 7 were waited for; matrix products, arithmetic and copies ran while one was open for 1% of the time, Pallas kernels for 2%

profile of v2, /device:TPU:32, one launch (start us, length us, event | category | flops | bytes accessed | tf_op | source)
XLA Modules:
  0.0 138.0 jit_solution(572802708563858510)
XLA Ops:
  1.3 2.8 %pack.1 = (bf16[528,256]{1,0:T(8,128)(2,1)}, bf16[4,144,256]{2,1,0:T(8,128)(2,1)}) custom-call(s32[1,4]{1,0:T(1,128)} %ids.1, s32[1,1]{1,0:T(1,128)S(6)} %copy.14.count, f32[1,4]{1,0:T(1,128)} %logq.1, f32[768,256]{1,0:T(8,128)} %table.3, bf16[1,128,256]{2,1,0:T(8,128)(2,1)} %queries.1, s32[1,128]{1,0:T(1,128)} %targets.1), custom_call_target="tpu_custom_call" | custom-call | tf_op jit(solution)/shard_map/pack/pallas_call | solution.py:271
  4.1 0.0 copy-start.3
  4.1 9.0 %all-to-all-start = ((bf16[4,144,256]{2,1,0:T(8,128)(2,1)}), bf16[4,144,256]{2,1,0:T(8,128)(2,1)S(1)}, u32[]{:S(2)}, u32[]{:S(2)}) async-start(bf16[4,144,256]{2,1,0:T(8,128)(2,1)} %get-tuple-element.16), calls=%async_computation | async-start | bytes 589824 | tf_op jit(solution)/shard_map/all_to_all | solution.py:280
  13.1 1.9 %collective-permute-start.2 = (bf16[528,256]{1,0:T(8,128)(2,1)}, bf16[528,256]{1,0:T(8,128)(2,1)S(1)}, u32[]{:S(2)}, u32[]{:S(2)}) collective-permute-start(bf16[528,256]{1,0:T(8,128)(2,1)} %get-tuple-element.15.own), channel_id=1, source_target_pairs={{0,24},{8,0},{16,8},{24,16},{1,25},{9,1},{17,9},{25,17},{2,26},{10... | collective-permute-start | bytes 811016 | tf_op jit(solution)/shard_map/ppermute | solution.py:283
  15.0 2.6 %collective-permute-start.1 = (bf16[528,256]{1,0:T(8,128)(2,1)}, bf16[528,256]{1,0:T(8,128)(2,1)S(1)}, u32[]{:S(2)}, u32[]{:S(2)}) collective-permute-start(bf16[528,256]{1,0:T(8,128)(2,1)} %get-tuple-element.15.own), channel_id=1, source_target_pairs={{0,16},{8,24},{16,0},{24,8},{1,17},{9,25},{17,1},{25,9},{2,18},{10... | collective-permute-start | bytes 811016 | tf_op jit(solution)/shard_map/ppermute | solution.py:283
  17.6 3.3 %collective-permute-start = (bf16[528,256]{1,0:T(8,128)(2,1)}, bf16[528,256]{1,0:T(8,128)(2,1)S(1)}, u32[]{:S(2)}, u32[]{:S(2)}) collective-permute-start(bf16[528,256]{1,0:T(8,128)(2,1)} %get-tuple-element.15.own), channel_id=1, source_target_pairs={{0,8},{8,16},{16,24},{24,0},{1,9},{9,17},{17,25},{25,1},{2,10},{10... | collective-permute-start | bytes 811016 | tf_op jit(solution)/shard_map/ppermute | solution.py:283
  20.9 0.1 pad_add_fusion.place
  21.0 0.0 all-to-all-done
  21.0 2.2 %all_gather.3.queries = bf16[8,144,256]{2,1,0:T(8,128)(2,1)S(1)} all-gather(bf16[4,144,256]{2,1,0:T(8,128)(2,1)S(1)} %all-to-all-done), channel_id=1, replica_groups=mesh['zh'=4,'y'=4,'x'=4,'zl'=4,'c'=2] {'c'}, dimensions={0}, use_global_device_ids=true | all-gather | bytes 884736 | tf_op jit(solution)/shard_map/all_gather | solution.py:284
  23.2 0.9 collective-permute-done.2.three
  24.0 4.0 %collective-permute-done.1.two = bf16[528,256]{1,0:T(8,128)(2,1)S(1)} collective-permute-done((bf16[528,256]{1,0:T(8,128)(2,1)}, bf16[528,256]{1,0:T(8,128)(2,1)S(1)}, u32[]{:S(2)}, u32[]{:S(2)}) %collective-permute-start.1) | collective-permute-done | bytes 270368 | tf_op jit(solution)/shard_map/ppermute | solution.py:283
  28.0 3.7 %collective-permute-done.one = bf16[528,256]{1,0:T(8,128)(2,1)S(1)} collective-permute-done((bf16[528,256]{1,0:T(8,128)(2,1)}, bf16[528,256]{1,0:T(8,128)(2,1)S(1)}, u32[]{:S(2)}, u32[]{:S(2)}) %collective-permute-start) | collective-permute-done | bytes 270368 | tf_op jit(solution)/shard_map/ppermute | solution.py:283
  31.7 0.0 copy-done.3
  31.7 3.5 %totals.1 = f32[8,16,128]{2,1,0:T(8,128)S(1)} custom-call(s32[3]{0:T(128)S(1)} %pad_add_fusion.place, bf16[528,256]{1,0:T(8,128)(2,1)S(1)} %copy-done.3, bf16[528,256]{1,0:T(8,128)(2,1)S(1)} %collective-permute-done.one, bf16[528,256]{1,0:T(8,128)(2,1)S(1)} %collective-permute-done.1.two, bf16[528,256]{1,0:T(8,128)(2,1)S(1)} %collective-permute-done.2.three, ...), custom_call_target="tpu_custom_call" | custom-call | tf_op jit(solution)/shard_map/totals/pallas_call | solution.py:288
  35.2 11.6 %all_to_all.25.stats = f32[8,16,128]{2,1,0:T(8,128)S(1)} all-to-all(f32[8,16,128]{2,1,0:T(8,128)S(1)} %totals.1), channel_id=1, replica_groups=mesh['zh'=4,'y'=4,'x'=4,'zl'=4,'c'=2] {'c','zl'}, dimensions={0} | all-to-all | bytes 131072 | tf_op jit(solution)/shard_map/all_to_all | solution.py:297
  46.8 5.5 %items.1 = (s32[1]{0:T(128)}, f32[1,128]{1,0:T(1,128)}, bf16[16,144,256]{2,1,0:T(8,128)(2,1)}, bf16[16,128,1024]{2,1,0:T(8,128)(2,1)S(1)}, bf16[17,128,256]{2,1,0:T(8,128)(2,1)S(1)}) custom-call(s32[3]{0:T(128)S(1)} %pad_add_fusion.place, bf16[528,256]{1,0:T(8,128)(2,1)S(1)} %copy-done.3, bf16[528,256]{1,0:T(8,128)(2,1)S(1)} %collective-permute-done.one, ...), custom_call_target="tpu_custom_call" | custom-call | tf_op jit(solution)/shard_map/items/pallas_call | solution.py:299
  52.2 0.0 copy-start
  52.3 1.9 %copy-done = bf16[16,128,1024]{2,1,0:T(8,128)(2,1)} copy-done((bf16[16,128,1024]{2,1,0:T(8,128)(2,1)}, bf16[16,128,1024]{2,1,0:T(8,128)(2,1)S(1)}, u32[]{:S(2)}) %copy-start) | copy-done | bytes 4194328
  54.2 4.1 %all-to-all-start.3 = ((bf16[16,144,256]{2,1,0:T(8,128)(2,1)}), bf16[16,144,256]{2,1,0:T(8,128)(2,1)S(1)}, u32[]{:S(2)}, u32[]{:S(2)}) async-start(bf16[16,144,256]{2,1,0:T(8,128)(2,1)} %get-tuple-element.21), calls=%async_computation.3 | async-start | bytes 2359296 | tf_op jit(solution)/shard_map/all_to_all | solution.py:315
  58.3 0.0 copy-start.1
  58.3 2.2 %copy-done.1 = bf16[16,128,1024]{2,1,0:T(8,128)(2,1)S(1)} copy-done((bf16[16,128,1024]{2,1,0:T(8,128)(2,1)S(1)}, bf16[16,128,1024]{2,1,0:T(8,128)(2,1)}, u32[]{:S(2)}) %copy-start.1) | copy-done | bytes 4194328
  60.5 2.5 %query_parts.1 = bf16[8,256,128]{2,1,0:T(8,128)(2,1)} custom-call(s32[1]{0:T(128)} %get-tuple-element.18.number, bf16[17,128,256]{2,1,0:T(8,128)(2,1)S(1)} %get-tuple-element.19.rows_all, bf16[16,128,1024]{2,1,0:T(8,128)(2,1)S(1)} %copy-done.1), custom_call_target="tpu_custom_call" | custom-call | flops 1073741824 | bytes 6291456 | tf_op jit(solution)/shard_map/query_parts/pallas_call | solution.py:316
  63.0 17.3 %all-to-all-done.3.parts = bf16[16,144,256]{2,1,0:T(8,128)(2,1)S(1)} async-done(((bf16[16,144,256]{2,1,0:T(8,128)(2,1)}), bf16[16,144,256]{2,1,0:T(8,128)(2,1)S(1)}, u32[]{:S(2)}, u32[]{:S(2)}) %all-to-all-start.3) | async-done | bytes 1179680 | tf_op jit(solution)/shard_map/all_to_all | solution.py:315
  80.3 4.2 %all-to-all-start.2 = ((bf16[8,256,128]{2,1,0:T(8,128)(2,1)}), bf16[8,256,128]{2,1,0:T(8,128)(2,1)S(1)}, u32[]{:S(2)}, u32[]{:S(2)}) async-start(bf16[8,256,128]{2,1,0:T(8,128)(2,1)} %query_parts.1), calls=%async_computation.2 | async-start | bytes 1048576 | tf_op jit(solution)/shard_map/all_to_all | solution.py:339
  84.5 0.2 gather_parts.1
  84.8 9.3 %collective-permute-start.3 = (bf16[6,32,256]{2,1,0:T(8,128)(2,1)S(1)}, bf16[6,32,256]{2,1,0:T(8,128)(2,1)S(1)}, u32[]{:S(2)}, u32[]{:S(2)}) collective-permute-start(bf16[6,32,256]{2,1,0:T(8,128)(2,1)S(1)} %gather_parts.1), channel_id=1, source_target_pairs={{0,128},{128,0},{256,384},{384,256},{1,129},{129,1},{257,385},{385... | collective-permute-start | bytes 294920 | tf_op jit(solution)/shard_map/ppermute | solution.py:335
  94.1 6.5 %collective-permute-done.3 = bf16[6,32,256]{2,1,0:T(8,128)(2,1)S(1)} collective-permute-done((bf16[6,32,256]{2,1,0:T(8,128)(2,1)S(1)}, bf16[6,32,256]{2,1,0:T(8,128)(2,1)S(1)}, u32[]{:S(2)}, u32[]{:S(2)}) %collective-permute-start.3) | collective-permute-done | bytes 98336 | tf_op jit(solution)/shard_map/ppermute | solution.py:335
  100.6 13.5 %collective-permute-start.4 = (bf16[6,32,256]{2,1,0:T(8,128)(2,1)S(1)}, bf16[6,32,256]{2,1,0:T(8,128)(2,1)S(1)}, u32[]{:S(2)}, u32[]{:S(2)}) collective-permute-start(bf16[6,32,256]{2,1,0:T(8,128)(2,1)S(1)} %add_convert_fusion), channel_id=1, source_target_pairs={{128,256},{256,128},{384,0},{0,384},{129,257},{257,129},{385,1},{1... | collective-permute-start | bytes 294920 | tf_op jit(solution)/shard_map/ppermute | solution.py:337
  114.1 4.3 %collective-permute-done.4 = bf16[6,32,256]{2,1,0:T(8,128)(2,1)S(1)} collective-permute-done((bf16[6,32,256]{2,1,0:T(8,128)(2,1)S(1)}, bf16[6,32,256]{2,1,0:T(8,128)(2,1)S(1)}, u32[]{:S(2)}, u32[]{:S(2)}) %collective-permute-start.4) | collective-permute-done | bytes 98336 | tf_op jit(solution)/shard_map/ppermute | solution.py:337
  118.4 0.0 all-to-all-done.2
  118.5 0.0 copy-start.6
  118.5 0.8 copy-done.6
  119.2 1.0 broadcast_in_dim.10
  120.2 0.0 copy-start.2
  120.2 0.0 copy-start.4
  120.2 0.0 copy-start.5
  120.2 3.6 %all-to-all-start.4 = ((f32[4,6,32,256]{3,2,1,0:T(8,128)}), f32[4,6,32,256]{3,2,1,0:T(8,128)S(1)}, u32[]{:S(2)}, u32[]{:S(2)}) async-start(f32[4,6,32,256]{3,2,1,0:T(8,128)} %broadcast_in_dim.10), calls=%async_computation.4 | async-start | bytes 1572864 | tf_op jit(solution)/shard_map/all_to_all | solution.py:263
  123.9 1.1 convert_reduce_fusion
  125.0 0.8 copy.13
  125.7 10.6 %all-to-all-done.4.gradient = f32[4,6,32,256]{3,2,1,0:T(8,128)S(1)} async-done(((f32[4,6,32,256]{3,2,1,0:T(8,128)}), f32[4,6,32,256]{3,2,1,0:T(8,128)S(1)}, u32[]{:S(2)}, u32[]{:S(2)}) %all-to-all-start.4) | async-done | bytes 786464 | tf_op jit(solution)/shard_map/all_to_all | solution.py:263
  136.3 0.0 copy-done.2
  136.3 0.0 copy-done.4
  136.3 0.0 copy-done.5
  136.3 1.6 %adam.1 = (f32[768,256]{1,0:T(8,128)}, f32[768,256]{1,0:T(8,128)}, f32[768,256]{1,0:T(8,128)}) custom-call(f32[4,6,32,256]{3,2,1,0:T(8,128)S(1)} %all-to-all-done.4.gradient, f32[768,256]{1,0:T(8,128)S(1)} %copy-done.2, f32[768,256]{1,0:T(8,128)S(1)} %copy-done.4, f32[768,256]{1,0:T(8,128)S(1)} %copy-done.5), custom_call_target="tpu_custom_call" | custom-call | tf_op jit(solution)/shard_map/adam/pallas_call | solution.py:343
  (2 shorter events, 0.1 us)
Async XLA Ops:
  4.1 27.6 %copy-start.3 = (bf16[528,256]{1,0:T(8,128)(2,1)S(1)}, bf16[528,256]{1,0:T(8,128)(2,1)}, u32[]{:S(2)}) copy-start(bf16[528,256]{1,0:T(8,128)(2,1)} %get-tuple-element.15.own) | copy-start | bytes 811012
  4.1 16.9 %all-to-all-start = ((bf16[4,144,256]{2,1,0:T(8,128)(2,1)}), bf16[4,144,256]{2,1,0:T(8,128)(2,1)S(1)}, u32[]{:S(2)}, u32[]{:S(2)}) async-start(bf16[4,144,256]{2,1,0:T(8,128)(2,1)} %get-tuple-element.16), calls=%async_computation | async-start | bytes 589824 | tf_op jit(solution)/shard_map/all_to_all | solution.py:280
  13.1 10.9 %collective-permute-start.2 = (bf16[528,256]{1,0:T(8,128)(2,1)}, bf16[528,256]{1,0:T(8,128)(2,1)S(1)}, u32[]{:S(2)}, u32[]{:S(2)}) collective-permute-start(bf16[528,256]{1,0:T(8,128)(2,1)} %get-tuple-element.15.own), channel_id=1, source_target_pairs={{0,24},{8,0},{16,8},{24,16},{1,25},{9,1},{17,9},{25,17},{2,26},{10... | collective-permute-start | bytes 811016 | tf_op jit(solution)/shard_map/ppermute | solution.py:283
  15.0 13.0 %collective-permute-start.1 = (bf16[528,256]{1,0:T(8,128)(2,1)}, bf16[528,256]{1,0:T(8,128)(2,1)S(1)}, u32[]{:S(2)}, u32[]{:S(2)}) collective-permute-start(bf16[528,256]{1,0:T(8,128)(2,1)} %get-tuple-element.15.own), channel_id=1, source_target_pairs={{0,16},{8,24},{16,0},{24,8},{1,17},{9,25},{17,1},{25,9},{2,18},{10... | collective-permute-start | bytes 811016 | tf_op jit(solution)/shard_map/ppermute | solution.py:283
  17.6 14.1 %collective-permute-start = (bf16[528,256]{1,0:T(8,128)(2,1)}, bf16[528,256]{1,0:T(8,128)(2,1)S(1)}, u32[]{:S(2)}, u32[]{:S(2)}) collective-permute-start(bf16[528,256]{1,0:T(8,128)(2,1)} %get-tuple-element.15.own), channel_id=1, source_target_pairs={{0,8},{8,16},{16,24},{24,0},{1,9},{9,17},{17,25},{25,1},{2,10},{10... | collective-permute-start | bytes 811016 | tf_op jit(solution)/shard_map/ppermute | solution.py:283
  52.2 1.9 %copy-start = (bf16[16,128,1024]{2,1,0:T(8,128)(2,1)}, bf16[16,128,1024]{2,1,0:T(8,128)(2,1)S(1)}, u32[]{:S(2)}) copy-start(bf16[16,128,1024]{2,1,0:T(8,128)(2,1)S(1)} %get-tuple-element.20.gone) | copy-start | bytes 12582916
  54.2 26.1 %all-to-all-start.3 = ((bf16[16,144,256]{2,1,0:T(8,128)(2,1)}), bf16[16,144,256]{2,1,0:T(8,128)(2,1)S(1)}, u32[]{:S(2)}, u32[]{:S(2)}) async-start(bf16[16,144,256]{2,1,0:T(8,128)(2,1)} %get-tuple-element.21), calls=%async_computation.3 | async-start | bytes 2359296 | tf_op jit(solution)/shard_map/all_to_all | solution.py:315
  58.3 2.2 %copy-start.1 = (bf16[16,128,1024]{2,1,0:T(8,128)(2,1)S(1)}, bf16[16,128,1024]{2,1,0:T(8,128)(2,1)}, u32[]{:S(2)}) copy-start(bf16[16,128,1024]{2,1,0:T(8,128)(2,1)} %copy-done) | copy-start | bytes 12582916
  80.3 38.2 %all-to-all-start.2 = ((bf16[8,256,128]{2,1,0:T(8,128)(2,1)}), bf16[8,256,128]{2,1,0:T(8,128)(2,1)S(1)}, u32[]{:S(2)}, u32[]{:S(2)}) async-start(bf16[8,256,128]{2,1,0:T(8,128)(2,1)} %query_parts.1), calls=%async_computation.2 | async-start | bytes 1048576 | tf_op jit(solution)/shard_map/all_to_all | solution.py:339
  84.8 15.8 %collective-permute-start.3 = (bf16[6,32,256]{2,1,0:T(8,128)(2,1)S(1)}, bf16[6,32,256]{2,1,0:T(8,128)(2,1)S(1)}, u32[]{:S(2)}, u32[]{:S(2)}) collective-permute-start(bf16[6,32,256]{2,1,0:T(8,128)(2,1)S(1)} %gather_parts.1), channel_id=1, source_target_pairs={{0,128},{128,0},{256,384},{384,256},{1,129},{129,1},{257,385},{385... | collective-permute-start | bytes 294920 | tf_op jit(solution)/shard_map/ppermute | solution.py:335
  100.6 17.8 %collective-permute-start.4 = (bf16[6,32,256]{2,1,0:T(8,128)(2,1)S(1)}, bf16[6,32,256]{2,1,0:T(8,128)(2,1)S(1)}, u32[]{:S(2)}, u32[]{:S(2)}) collective-permute-start(bf16[6,32,256]{2,1,0:T(8,128)(2,1)S(1)} %add_convert_fusion), channel_id=1, source_target_pairs={{128,256},{256,128},{384,0},{0,384},{129,257},{257,129},{385,1},{1... | collective-permute-start | bytes 294920 | tf_op jit(solution)/shard_map/ppermute | solution.py:337
  118.5 0.8 copy-start.6
  120.2 16.1 %copy-start.2 = (f32[768,256]{1,0:T(8,128)S(1)}, f32[768,256]{1,0:T(8,128)}, u32[]{:S(2)}) copy-start(f32[768,256]{1,0:T(8,128)} %table.3) | copy-start | bytes 2359300
  120.2 16.1 %copy-start.4 = (f32[768,256]{1,0:T(8,128)S(1)}, f32[768,256]{1,0:T(8,128)}, u32[]{:S(2)}) copy-start(f32[768,256]{1,0:T(8,128)} %first.1) | copy-start | bytes 2359300
  120.2 16.1 %copy-start.5 = (f32[768,256]{1,0:T(8,128)S(1)}, f32[768,256]{1,0:T(8,128)}, u32[]{:S(2)}) copy-start(f32[768,256]{1,0:T(8,128)} %second.1) | copy-start | bytes 2359300
  120.2 16.1 %all-to-all-start.4 = ((f32[4,6,32,256]{3,2,1,0:T(8,128)}), f32[4,6,32,256]{3,2,1,0:T(8,128)S(1)}, u32[]{:S(2)}, u32[]{:S(2)}) async-start(f32[4,6,32,256]{3,2,1,0:T(8,128)} %broadcast_in_dim.10), calls=%async_computation.4 | async-start | bytes 1572864 | tf_op jit(solution)/shard_map/all_to_all | solution.py:263

commit v3 on v2

--- a/solution.py
+++ b/solution.py
@@ -4,6 +4,7 @@
 from jax.experimental import pallas as pl
 from jax.experimental.pallas import tpu as pltpu
 from jax.sharding import Mesh, PartitionSpec as P
+
 
 BLOCK = 128
 D = 256
@@ -114,11 +115,12 @@
     return lax.dot_general(rows, query_rows, (((1,), (1,)), ((), ())), preferred_element_type=f32)
 
 
-def totals_kernel(place, own, one, two, three, queries, out, rows_all, live, shifts, tops, sums, picks):
+def totals_kernel(place, own, one, two, three, queries, out, rows_all, live, shifts, taken, tops, sums, picks):
     number = list_live(place, (own, one, two, three), rows_all, live, shifts)
     tops[...] = jnp.full(tops.shape, floor_value, f32)
     sums[...] = jnp.zeros(sums.shape, f32)
     picks[...] = jnp.zeros(picks.shape, f32)
+    taken[...] = jnp.zeros(taken.shape, f32)
     item_index = lax.broadcasted_iota(i32, (BLOCK, CHUNK), 0)
 
     def one_slot(i, carry):
@@ -137,15 +139,16 @@
             fresh = jnp.sum(jnp.exp(split - base[None]), axis=0)
             sums[:, cols] = sums[:, cols] * jnp.exp(old - top) + fresh
             tops[:, cols] = top
-            marked = jnp.where(item_index == wanted, doubled - shift, 0.0).reshape(BLOCK // 8, 8, CHUNK)
+            marked = jnp.where(item_index == wanted, doubled, 0.0).reshape(BLOCK // 8, 8, CHUNK)
             picks[:, cols] = picks[:, cols] + jnp.sum(marked, axis=0)
+            taken[:, cols] = taken[:, cols] + jnp.where(target_slot == mine, shift, 0.0)
         return carry
 
     lax.fori_loop(0, number, one_slot, 0)
     top = jnp.max(tops[...], axis=0, keepdims=True)
     total = jnp.sum(sums[...] * jnp.exp(tops[...] - top), axis=0, keepdims=True)
     norm = top + jnp.log(total)
-    pick = jnp.sum(picks[...], axis=0, keepdims=True)
+    pick = jnp.sum(picks[...], axis=0, keepdims=True) - taken[...]
     norms = jnp.concatenate([norm[:, r * BLOCK : (r + 1) * BLOCK] for r in range(NQ)], axis=0)
     for d in range(NQ):
         out[d, pl.ds(0, NQ), :] = norms
@@ -153,7 +156,8 @@
 
 
 def item_kernel(
-    place, own, one, two, three, queries, stats, number_out, loss_out, item_out, gone, rows_all, live, shifts
+    place, own, one, two, three, queries, stats,
+    number_out, loss_out, item_out, gone_out, rows_all, live, shifts, gone, sems
 ):
     pieces = (own, one, two, three)
     number = list_live(place, pieces, rows_all, live, shifts)
@@ -196,6 +200,7 @@
         j = slot % SLOTS_DEV
         for y in range(NY):
             item_out[y * NX + x, pl.ds(pl.multiple_of(j * PART, PART), PART), :] = part[y * PART : (y + 1) * PART]
+        pltpu.make_async_copy(gone.at[i], gone_out.at[i], sems.at[i]).start()
         return carry
 
     lax.fori_loop(0, number, one_slot, 0)
@@ -203,15 +208,35 @@
     def pad(i, carry):
         rows_all[i] = jnp.zeros((BLOCK, D), bf16)
         gone[i] = jnp.zeros((BLOCK, NQ * BLOCK), bf16)
-        return carry
-
-    lax.fori_loop(number, (number + TOGETHER - 1) // TOGETHER * TOGETHER, pad, 0)
-
-
-def query_kernel(number, rows_all, gone, out, total):
+        pltpu.make_async_copy(gone.at[i], gone_out.at[i], sems.at[i]).start()
+        return carry
+
+    padded = (number + TOGETHER - 1) // TOGETHER * TOGETHER
+    lax.fori_loop(number, padded, pad, 0)
+
+    def finish(i, carry):
+        pltpu.make_async_copy(gone.at[i], gone_out.at[i], sems.at[i]).wait()
+        return carry
+
+    lax.fori_loop(0, padded, finish, 0)
+
+
+def query_kernel(number, rows_all, gone_in, out, total, gone, sems):
+    groups = (number[0] + TOGETHER - 1) // TOGETHER
+
+    def fetch(g):
+        some = pl.ds(g * TOGETHER, TOGETHER)
+        return pltpu.make_async_copy(gone_in.at[some], gone.at[some], sems.at[g])
+
+    def begin(g, carry):
+        fetch(g).start()
+        return carry
+
+    lax.fori_loop(0, groups, begin, 0)
     total[...] = jnp.zeros(total.shape, f32)
 
     def one_group(g, carry):
+        fetch(g).wait()
         some = pl.ds(g * TOGETHER, TOGETHER)
         rows = rows_all[some].reshape(TOGETHER * BLOCK, D).T
         for b in range(CHUNKS):
@@ -220,7 +245,7 @@
             total[:, cols] = total[:, cols] + jnp.dot(rows, dlogit, preferred_element_type=f32)
         return carry
 
-    lax.fori_loop(0, (number[0] + TOGETHER - 1) // TOGETHER, one_group, 0)
+    lax.fori_loop(0, groups, one_group, 0)
     for r in range(NQ):
         out[r] = total[:, pl.ds(r * BLOCK, BLOCK)].astype(bf16)
 
@@ -239,34 +264,41 @@
     out[...] = total[...].astype(bf16)
 
 
-def adam_kernel(gradient, table, first, second, table_out, first_out, second_out, tables, firsts, seconds, sems):
+def adam_kernel(place, own, one, two, three, table, first, second, *rest):
+    outs, results, sems = rest[:3], rest[3:6], rest[6]
     copies = []
     for b in range(BLOCKS_DEV):
-        rows = pl.ds(b * BLOCK, BLOCK)
-        grad = gradient[:, b].reshape(BLOCK, D)
-        first_new = beta_first * first[rows, :] + (1.0 - beta_first) * grad
-        second_new = beta_second * second[rows, :] + (1.0 - beta_second) * grad * grad
-        firsts[rows, :] = first_new
-        seconds[rows, :] = second_new
-        tables[rows, :] = table[rows, :] - learn_rate * (first_new / bias_first) / (
-            jnp.sqrt(second_new / bias_second) + adam_eps
-        )
-        for n, (value, out) in enumerate(((tables, table_out), (firsts, first_out), (seconds, second_out))):
-            copy = pltpu.make_async_copy(value.at[rows, :], out.at[rows, :], sems.at[b, n])
+        for k, piece in enumerate((own, one, two, three)):
+            y = (place[3] - k) & (NY - 1)
+            rows = pl.ds(pl.multiple_of(b * BLOCK + y * PART, PART), PART)
+            grad = piece[b]
+            first_new = beta_first * first[rows, :] + (1.0 - beta_first) * grad
+            second_new = beta_second * second[rows, :] + (1.0 - beta_second) * grad * grad
+            results[1][rows, :] = first_new
+            results[2][rows, :] = second_new
+            results[0][rows, :] = table[rows, :] - learn_rate * (first_new / bias_first) / (
+                jnp.sqrt(second_new / bias_second) + adam_eps
+            )
+        block = pl.ds(b * BLOCK, BLOCK)
+        for n in range(3):
+            copy = pltpu.make_async_copy(results[n].at[block, :], outs[n].at[block, :], sems.at[b, n])
             copy.start()
             copies.append(copy)
     for copy in copies:
         copy.wait()
 
 
-def spread(value, axes, size):
-    return lax.all_to_all(jnp.broadcast_to(value[None], (size,) + value.shape), axes, 0, 0, tiled=True)
+def query_sum_kernel(parts, out):
+    total = parts[0].astype(f32)
+    for r in range(1, NQ):
+        total = total + parts[r].astype(f32)
+    out[0] = total.T
 
 
 def step(queries, targets, samp_ids, counts, logq, table, first_moment, second_moment):
     place = lax.axis_index("zl") * NC + lax.axis_index("c")
     own = lax.axis_index("c") * NZ + lax.axis_index("zl")
-    where = jnp.stack([place, own, lax.axis_index("x")]).astype(i32)
+    where = jnp.stack([place, own, lax.axis_index("x"), lax.axis_index("y")]).astype(i32)
     item_shape = jax.ShapeDtypeStruct((SLOTS_DEV * BLOCK + META, D), bf16)
     items, query_rows = pl.pallas_call(
         pack_kernel,
@@ -290,7 +322,7 @@
         out_shape=jax.ShapeDtypeStruct((NQ, 2 * NQ, BLOCK), f32),
         in_specs=[smem()] + [vmem()] * (NX + 1),
         out_specs=vmem(),
-        scratch_shapes=[rows_spec] + tables + [pltpu.VMEM((8, NQ * BLOCK), f32)] * 3,
+        scratch_shapes=[rows_spec] + tables + [pltpu.VMEM((1, NQ * BLOCK), f32)] + [pltpu.VMEM((8, NQ * BLOCK), f32)] * 3,
         compiler_params=limit(10),
         name="totals",
     )(where, *pieces, every_query)
@@ -306,8 +338,9 @@
             jax.ShapeDtypeStruct((SLOTS + 1, BLOCK, D), bf16),
         ),
         in_specs=[smem()] + [vmem()] * (NX + 2),
-        out_specs=(smem(), vmem(), vmem(), vmem(), vmem()),
-        scratch_shapes=tables,
+        out_specs=(smem(), vmem(), vmem(), hbm(), vmem()),
+        scratch_shapes=tables
+        + [pltpu.VMEM((SLOTS, BLOCK, NQ * BLOCK), bf16), pltpu.SemaphoreType.DMA((SLOTS,))],
         compiler_params=limit(16),
         name="items",
     )(where, *pieces, every_query, stats)
@@ -316,9 +349,13 @@
     query_parts = pl.pallas_call(
         query_kernel,
         out_shape=jax.ShapeDtypeStruct((NQ, D, BLOCK), bf16),
-        in_specs=[smem(), vmem(), vmem()],
+        in_specs=[smem(), vmem(), hbm()],
         out_specs=vmem(),
-        scratch_shapes=[pltpu.VMEM((D, NQ * BLOCK), f32)],
+        scratch_shapes=[
+            pltpu.VMEM((D, NQ * BLOCK), f32),
+            pltpu.VMEM((SLOTS, BLOCK, NQ * BLOCK), bf16),
+            pltpu.SemaphoreType.DMA((SLOTS // TOGETHER,)),
+        ],
         compiler_params=limit(12),
         cost_estimate=pl.CostEstimate(flops=1 << 30, bytes_accessed=6 << 20, transcendentals=0),
         name="query_parts",
@@ -337,19 +374,28 @@
     other = lax.ppermute(part, "zh", [(1, 2), (2, 1), (3, 0), (0, 3)])
     part = part.astype(f32) + other.astype(f32)
     query_parts = lax.all_to_all(query_parts, QROWS, 0, 0, tiled=True)
-    query_grad = jnp.sum(query_parts.astype(f32), axis=0).T
-    every_part = spread(part, "y", NY)
+    query_grad = pl.pallas_call(
+        query_sum_kernel,
+        out_shape=jax.ShapeDtypeStruct((1, BLOCK, D), f32),
+        in_specs=[vmem()],
+        out_specs=vmem(),
+        compiler_params=limit(4),
+        name="query_sum",
+    )(query_parts)
+    grads = [part]
+    for k in range(1, NY):
+        grads.append(lax.ppermute(part, "y", [(i, (i + k) % NY) for i in range(NY)]))
 
     new_table, new_first, new_second = pl.pallas_call(
         adam_kernel,
         out_shape=(jax.ShapeDtypeStruct(table.shape, f32),) * 3,
-        in_specs=[vmem()] * 4,
+        in_specs=[smem()] + [vmem()] * (NY + 3),
         out_specs=(hbm(),) * 3,
         scratch_shapes=[pltpu.VMEM(table.shape, f32)] * 3 + [pltpu.SemaphoreType.DMA((BLOCKS_DEV, 3))],
         compiler_params=limit(12),
         name="adam",
-    )(every_part, table, first_moment, second_moment)
-    return loss, query_grad[None], new_table, new_first, new_second
+    )(where, *grads, table, first_moment, second_moment)
+    return loss, query_grad, new_table, new_first, new_second
 
 
 def solution(mesh):

time: 139 us -> 141 us (1.014)
  the two profiles are of different devices: /device:TPU:32 before, /device:TPU:97 now
where the time goes in v3:
time: 141 us; the launch traced here: 140 us
  waiting for transfers between devices  50.3 us (36%)
  starting transfers between devices  49.4 us (35%)
  Pallas kernels  20.4 us (14%)
  blocking collectives  14.1 us (10%)
  local copies, waits for them, and re-layouts  4.13 us (3%)
  between operations  1.46 us (1%)
    ppermute x1, waiting for transfers between devices, step(): other = lax.ppermute(part, 'zh', [(1, 2), (2, 1), (3, 0), (0, 3)])  12.9 us
    all_to_all x1, starting transfers between devices, step(): query_parts = lax.all_to_all(query_parts, QROWS, 0, 0, tiled=True)  11.3 us
    all_to_all x1, waiting for transfers between devices, step(): item_parts = lax.all_to_all(item_parts, ('y', 'x'), 0, 0, tiled=True)  10.7 us
    ppermute x3, waiting for transfers between devices, step(): lax.ppermute(part, 'y', [(i, (i + k) % NY) for i in range(NY)])  9.89 us
    all_to_all x1, blocking collectives, step(): stats = lax.all_to_all(stats, QROWS, 0, 0, tiled=True)  9.69 us
    ppermute x3, starting transfers between devices, step(): lax.ppermute(items, 'x', [(i, (i + k) % NX) for i in range(NX)])  9.32 us
    ppermute x1, starting transfers between devices, step(): other = lax.ppermute(part, 'zh', [(0, 1), (1, 0), (2, 3), (3, 2)])  9.16 us
    ppermute x1, waiting for transfers between devices, step(): other = lax.ppermute(part, 'zh', [(0, 1), (1, 0), (2, 3), (3, 2)])  9.14 us
  transfers between devices with their start and end apart: 11, of which 8 were waited for; matrix products, arithmetic and copies ran while one was open for 0% of the time, Pallas kernels for 4%

profile of v3, /device:TPU:97, one launch (start us, length us, event | category | flops | bytes accessed | tf_op | source)
XLA Modules:
  0.0 139.9 jit_solution(17607925994420192910)
XLA Ops:
  1.3 2.8 %pack.1 = (bf16[528,256]{1,0:T(8,128)(2,1)}, bf16[4,144,256]{2,1,0:T(8,128)(2,1)}) custom-call(s32[1,4]{1,0:T(1,128)} %ids.1, s32[1,1]{1,0:T(1,128)S(6)} %copy.13.count, f32[1,4]{1,0:T(1,128)} %logq.1, f32[768,256]{1,0:T(8,128)} %table.3, bf16[1,128,256]{2,1,0:T(8,128)(2,1)} %queries.1, s32[1,128]{1,0:T(1,128)} %targets.1), custom_call_target="tpu_custom_call" | custom-call | tf_op jit(solution)/shard_map/pack/pallas_call | solution.py:303
  4.1 0.0 copy-start.3
  4.1 4.7 %all-to-all-start = ((bf16[4,144,256]{2,1,0:T(8,128)(2,1)}), bf16[4,144,256]{2,1,0:T(8,128)(2,1)S(1)}, u32[]{:S(2)}, u32[]{:S(2)}) async-start(bf16[4,144,256]{2,1,0:T(8,128)(2,1)} %get-tuple-element.16), calls=%async_computation | async-start | bytes 589824 | tf_op jit(solution)/shard_map/all_to_all | solution.py:312
  8.8 4.4 %collective-permute-start.2 = (bf16[528,256]{1,0:T(8,128)(2,1)}, bf16[528,256]{1,0:T(8,128)(2,1)S(1)}, u32[]{:S(2)}, u32[]{:S(2)}) collective-permute-start(bf16[528,256]{1,0:T(8,128)(2,1)} %get-tuple-element.15.own), channel_id=1, source_target_pairs={{0,24},{8,0},{16,8},{24,16},{1,25},{9,1},{17,9},{25,17},{2,26},{10... | collective-permute-start | bytes 811016 | tf_op jit(solution)/shard_map/ppermute | solution.py:315
  13.1 2.4 %collective-permute-start.1 = (bf16[528,256]{1,0:T(8,128)(2,1)}, bf16[528,256]{1,0:T(8,128)(2,1)S(1)}, u32[]{:S(2)}, u32[]{:S(2)}) collective-permute-start(bf16[528,256]{1,0:T(8,128)(2,1)} %get-tuple-element.15.own), channel_id=1, source_target_pairs={{0,16},{8,24},{16,0},{24,8},{1,17},{9,25},{17,1},{25,9},{2,18},{10... | collective-permute-start | bytes 811016 | tf_op jit(solution)/shard_map/ppermute | solution.py:315
  15.6 2.5 %collective-permute-start = (bf16[528,256]{1,0:T(8,128)(2,1)}, bf16[528,256]{1,0:T(8,128)(2,1)S(1)}, u32[]{:S(2)}, u32[]{:S(2)}) collective-permute-start(bf16[528,256]{1,0:T(8,128)(2,1)} %get-tuple-element.15.own), channel_id=1, source_target_pairs={{0,8},{8,16},{16,24},{24,0},{1,9},{9,17},{17,25},{25,1},{2,10},{10... | collective-permute-start | bytes 811016 | tf_op jit(solution)/shard_map/ppermute | solution.py:315
  18.1 0.1 pad_add_fusion.place
  18.2 0.0 all-to-all-done
  18.2 4.4 %all_gather.3.queries = bf16[8,144,256]{2,1,0:T(8,128)(2,1)S(1)} all-gather(bf16[4,144,256]{2,1,0:T(8,128)(2,1)S(1)} %all-to-all-done), channel_id=1, replica_groups=mesh['zh'=4,'y'=4,'x'=4,'zl'=4,'c'=2] {'c'}, dimensions={0}, use_global_device_ids=true | all-gather | bytes 884736 | tf_op jit(solution)/shard_map/all_gather | solution.py:316
  22.6 0.0 collective-permute-done.2.three
  22.6 0.6 collective-permute-done.1.two
  23.2 7.1 %collective-permute-done.one = bf16[528,256]{1,0:T(8,128)(2,1)S(1)} collective-permute-done((bf16[528,256]{1,0:T(8,128)(2,1)}, bf16[528,256]{1,0:T(8,128)(2,1)S(1)}, u32[]{:S(2)}, u32[]{:S(2)}) %collective-permute-start) | collective-permute-done | bytes 270368 | tf_op jit(solution)/shard_map/ppermute | solution.py:315
  30.3 0.0 copy-done.3
  30.3 4.2 %totals.1 = f32[8,16,128]{2,1,0:T(8,128)S(1)} custom-call(s32[4]{0:T(128)S(1)} %pad_add_fusion.place, bf16[528,256]{1,0:T(8,128)(2,1)S(1)} %copy-done.3, bf16[528,256]{1,0:T(8,128)(2,1)S(1)} %collective-permute-done.one, bf16[528,256]{1,0:T(8,128)(2,1)S(1)} %collective-permute-done.1.two, bf16[528,256]{1,0:T(8,128)(2,1)S(1)} %collective-permute-done.2.three, ...), custom_call_target="tpu_custom_call" | custom-call | tf_op jit(solution)/shard_map/totals/pallas_call | solution.py:320
  34.5 9.7 %all_to_all.20.stats = f32[8,16,128]{2,1,0:T(8,128)S(1)} all-to-all(f32[8,16,128]{2,1,0:T(8,128)S(1)} %totals.1), channel_id=1, replica_groups=mesh['zh'=4,'y'=4,'x'=4,'zl'=4,'c'=2] {'c','zl'}, dimensions={0} | all-to-all | bytes 131072 | tf_op jit(solution)/shard_map/all_to_all | solution.py:329
  44.2 7.0 %items.1 = (s32[1]{0:T(128)}, f32[1,128]{1,0:T(1,128)}, bf16[16,144,256]{2,1,0:T(8,128)(2,1)}, bf16[16,128,1024]{2,1,0:T(8,128)(2,1)S(1)}, bf16[17,128,256]{2,1,0:T(8,128)(2,1)S(1)}) custom-call(s32[4]{0:T(128)S(1)} %pad_add_fusion.place, bf16[528,256]{1,0:T(8,128)(2,1)S(1)} %copy-done.3, bf16[528,256]{1,0:T(8,128)(2,1)S(1)} %collective-permute-done.one, ...), custom_call_target="tpu_custom_call" | custom-call | tf_op jit(solution)/shard_map/items/pallas_call | solution.py:331
  51.2 0.0 copy-start
  51.2 1.9 %copy-done = bf16[16,128,1024]{2,1,0:T(8,128)(2,1)} copy-done((bf16[16,128,1024]{2,1,0:T(8,128)(2,1)}, bf16[16,128,1024]{2,1,0:T(8,128)(2,1)S(1)}, u32[]{:S(2)}) %copy-start) | copy-done | bytes 4194328
  53.1 3.7 %all-to-all-start.3 = ((bf16[16,144,256]{2,1,0:T(8,128)(2,1)}), bf16[16,144,256]{2,1,0:T(8,128)(2,1)S(1)}, u32[]{:S(2)}, u32[]{:S(2)}) async-start(bf16[16,144,256]{2,1,0:T(8,128)(2,1)} %get-tuple-element.21), calls=%async_computation.3 | async-start | bytes 2359296 | tf_op jit(solution)/shard_map/all_to_all | solution.py:348
  56.8 0.0 copy-start.1
  56.8 2.2 %copy-done.1 = bf16[16,128,1024]{2,1,0:T(8,128)(2,1)S(1)} copy-done((bf16[16,128,1024]{2,1,0:T(8,128)(2,1)S(1)}, bf16[16,128,1024]{2,1,0:T(8,128)(2,1)}, u32[]{:S(2)}) %copy-start.1) | copy-done | bytes 4194328
  59.0 3.2 %query_parts.1 = bf16[8,256,128]{2,1,0:T(8,128)(2,1)} custom-call(s32[1]{0:T(128)} %get-tuple-element.18.number, bf16[17,128,256]{2,1,0:T(8,128)(2,1)S(1)} %get-tuple-element.19.rows_all, bf16[16,128,1024]{2,1,0:T(8,128)(2,1)S(1)} %copy-done.1), custom_call_target="tpu_custom_call" | custom-call | flops 1073741824 | bytes 6291456 | tf_op jit(solution)/shard_map/query_parts/pallas_call | solution.py:349
  62.3 10.7 %all-to-all-done.3.parts = bf16[16,144,256]{2,1,0:T(8,128)(2,1)S(1)} async-done(((bf16[16,144,256]{2,1,0:T(8,128)(2,1)}), bf16[16,144,256]{2,1,0:T(8,128)(2,1)S(1)}, u32[]{:S(2)}, u32[]{:S(2)}) %all-to-all-start.3) | async-done | bytes 1179680 | tf_op jit(solution)/shard_map/all_to_all | solution.py:348
  73.0 0.0 copy-start.5
  73.0 11.3 %all-to-all-start.2 = ((bf16[8,256,128]{2,1,0:T(8,128)(2,1)}), bf16[8,256,128]{2,1,0:T(8,128)(2,1)S(1)}, u32[]{:S(2)}, u32[]{:S(2)}) async-start(bf16[8,256,128]{2,1,0:T(8,128)(2,1)} %query_parts.1), calls=%async_computation.2 | async-start | bytes 1048576 | tf_op jit(solution)/shard_map/all_to_all | solution.py:376
  84.3 0.0 copy-start.2
  84.3 0.0 copy-start.4
  84.3 0.2 gather_parts.1
  84.5 9.2 %collective-permute-start.3 = (bf16[6,32,256]{2,1,0:T(8,128)(2,1)S(1)}, bf16[6,32,256]{2,1,0:T(8,128)(2,1)S(1)}, u32[]{:S(2)}, u32[]{:S(2)}) collective-permute-start(bf16[6,32,256]{2,1,0:T(8,128)(2,1)S(1)} %gather_parts.1), channel_id=1, source_target_pairs={{0,128},{128,0},{256,384},{384,256},{1,129},{129,1},{257,385},{385... | collective-permute-start | bytes 294920 | tf_op jit(solution)/shard_map/ppermute | solution.py:372
  93.7 9.1 %collective-permute-done.3 = bf16[6,32,256]{2,1,0:T(8,128)(2,1)S(1)} collective-permute-done((bf16[6,32,256]{2,1,0:T(8,128)(2,1)S(1)}, bf16[6,32,256]{2,1,0:T(8,128)(2,1)S(1)}, u32[]{:S(2)}, u32[]{:S(2)}) %collective-permute-start.3) | collective-permute-done | bytes 98336 | tf_op jit(solution)/shard_map/ppermute | solution.py:372
  102.9 3.7 %collective-permute-start.4 = (bf16[6,32,256]{2,1,0:T(8,128)(2,1)S(1)}, bf16[6,32,256]{2,1,0:T(8,128)(2,1)S(1)}, u32[]{:S(2)}, u32[]{:S(2)}) collective-permute-start(bf16[6,32,256]{2,1,0:T(8,128)(2,1)S(1)} %add_convert_fusion), channel_id=1, source_target_pairs={{128,256},{256,128},{384,0},{0,384},{129,257},{257,129},{385,1},{1... | collective-permute-start | bytes 294920 | tf_op jit(solution)/shard_map/ppermute | solution.py:374
  106.6 12.9 %collective-permute-done.4 = bf16[6,32,256]{2,1,0:T(8,128)(2,1)S(1)} collective-permute-done((bf16[6,32,256]{2,1,0:T(8,128)(2,1)S(1)}, bf16[6,32,256]{2,1,0:T(8,128)(2,1)S(1)}, u32[]{:S(2)}, u32[]{:S(2)}) %collective-permute-start.4) | collective-permute-done | bytes 98336 | tf_op jit(solution)/shard_map/ppermute | solution.py:374
  119.5 3.1 %collective-permute-start.7 = (f32[6,32,256]{2,1,0:T(8,128)S(1)}, f32[6,32,256]{2,1,0:T(8,128)S(1)}, u32[]{:S(2)}, u32[]{:S(2)}) collective-permute-start(f32[6,32,256]{2,1,0:T(8,128)S(1)} %convert_add_fusion.own), channel_id=1, source_target_pairs={{0,96},{32,0},{64,32},{96,64},{1,97},{33,1},{65,33},{97,65},{2,98}... | collective-permute-start | bytes 589832 | tf_op jit(solution)/shard_map/ppermute | solution.py:387
  122.6 2.2 %collective-permute-start.6 = (f32[6,32,256]{2,1,0:T(8,128)S(1)}, f32[6,32,256]{2,1,0:T(8,128)S(1)}, u32[]{:S(2)}, u32[]{:S(2)}) collective-permute-start(f32[6,32,256]{2,1,0:T(8,128)S(1)} %convert_add_fusion.own), channel_id=1, source_target_pairs={{0,64},{32,96},{64,0},{96,32},{1,65},{33,97},{65,1},{97,33},{2,66}... | collective-permute-start | bytes 589832 | tf_op jit(solution)/shard_map/ppermute | solution.py:387
  124.8 2.2 %collective-permute-start.5 = (f32[6,32,256]{2,1,0:T(8,128)S(1)}, f32[6,32,256]{2,1,0:T(8,128)S(1)}, u32[]{:S(2)}, u32[]{:S(2)}) collective-permute-start(f32[6,32,256]{2,1,0:T(8,128)S(1)} %convert_add_fusion.own), channel_id=1, source_target_pairs={{0,32},{32,64},{64,96},{96,0},{1,33},{33,65},{65,97},{97,1},{2,34}... | collective-permute-start | bytes 589832 | tf_op jit(solution)/shard_map/ppermute | solution.py:387
  127.0 0.3 collective-permute-done.7.three
  127.4 4.3 %collective-permute-done.6.two = f32[6,32,256]{2,1,0:T(8,128)S(1)} collective-permute-done((f32[6,32,256]{2,1,0:T(8,128)S(1)}, f32[6,32,256]{2,1,0:T(8,128)S(1)}, u32[]{:S(2)}, u32[]{:S(2)}) %collective-permute-start.6) | collective-permute-done | bytes 196640 | tf_op jit(solution)/shard_map/ppermute | solution.py:387
  131.7 5.2 %collective-permute-done.5.one = f32[6,32,256]{2,1,0:T(8,128)S(1)} collective-permute-done((f32[6,32,256]{2,1,0:T(8,128)S(1)}, f32[6,32,256]{2,1,0:T(8,128)S(1)}, u32[]{:S(2)}, u32[]{:S(2)}) %collective-permute-start.5) | collective-permute-done | bytes 196640 | tf_op jit(solution)/shard_map/ppermute | solution.py:387
  136.9 0.0 copy-done.5
  136.9 0.0 copy-done.2
  136.9 0.0 copy-done.4
  136.9 2.2 %adam.1 = (f32[768,256]{1,0:T(8,128)}, f32[768,256]{1,0:T(8,128)}, f32[768,256]{1,0:T(8,128)}) custom-call(s32[4]{0:T(128)S(1)} %pad_add_fusion.place, f32[6,32,256]{2,1,0:T(8,128)S(1)} %convert_add_fusion.own, f32[6,32,256]{2,1,0:T(8,128)S(1)} %collective-permute-done.5.one, f32[6,32,256]{2,1,0:T(8,128)S(1)} %collective-permute-done.6.two, ...), custom_call_target="tpu_custom_call" | custom-call | tf_op jit(solution)/shard_map/adam/pallas_call | solution.py:389
  139.1 0.0 all-to-all-done.2.parts
  139.2 0.8 query_sum.1
  (2 shorter events, 0.0 us)
Async XLA Ops:
  4.1 26.2 %copy-start.3 = (bf16[528,256]{1,0:T(8,128)(2,1)S(1)}, bf16[528,256]{1,0:T(8,128)(2,1)}, u32[]{:S(2)}) copy-start(bf16[528,256]{1,0:T(8,128)(2,1)} %get-tuple-element.15.own) | copy-start | bytes 811012
  4.1 14.1 %all-to-all-start = ((bf16[4,144,256]{2,1,0:T(8,128)(2,1)}), bf16[4,144,256]{2,1,0:T(8,128)(2,1)S(1)}, u32[]{:S(2)}, u32[]{:S(2)}) async-start(bf16[4,144,256]{2,1,0:T(8,128)(2,1)} %get-tuple-element.16), calls=%async_computation | async-start | bytes 589824 | tf_op jit(solution)/shard_map/all_to_all | solution.py:312
  8.8 13.8 %collective-permute-start.2 = (bf16[528,256]{1,0:T(8,128)(2,1)}, bf16[528,256]{1,0:T(8,128)(2,1)S(1)}, u32[]{:S(2)}, u32[]{:S(2)}) collective-permute-start(bf16[528,256]{1,0:T(8,128)(2,1)} %get-tuple-element.15.own), channel_id=1, source_target_pairs={{0,24},{8,0},{16,8},{24,16},{1,25},{9,1},{17,9},{25,17},{2,26},{10... | collective-permute-start | bytes 811016 | tf_op jit(solution)/shard_map/ppermute | solution.py:315
  13.1 10.0 %collective-permute-start.1 = (bf16[528,256]{1,0:T(8,128)(2,1)}, bf16[528,256]{1,0:T(8,128)(2,1)S(1)}, u32[]{:S(2)}, u32[]{:S(2)}) collective-permute-start(bf16[528,256]{1,0:T(8,128)(2,1)} %get-tuple-element.15.own), channel_id=1, source_target_pairs={{0,16},{8,24},{16,0},{24,8},{1,17},{9,25},{17,1},{25,9},{2,18},{10... | collective-permute-start | bytes 811016 | tf_op jit(solution)/shard_map/ppermute | solution.py:315
  15.6 14.7 %collective-permute-start = (bf16[528,256]{1,0:T(8,128)(2,1)}, bf16[528,256]{1,0:T(8,128)(2,1)S(1)}, u32[]{:S(2)}, u32[]{:S(2)}) collective-permute-start(bf16[528,256]{1,0:T(8,128)(2,1)} %get-tuple-element.15.own), channel_id=1, source_target_pairs={{0,8},{8,16},{16,24},{24,0},{1,9},{9,17},{17,25},{25,1},{2,10},{10... | collective-permute-start | bytes 811016 | tf_op jit(solution)/shard_map/ppermute | solution.py:315
  51.2 1.9 %copy-start = (bf16[16,128,1024]{2,1,0:T(8,128)(2,1)}, bf16[16,128,1024]{2,1,0:T(8,128)(2,1)S(1)}, u32[]{:S(2)}) copy-start(bf16[16,128,1024]{2,1,0:T(8,128)(2,1)S(1)} %get-tuple-element.20.gone_in) | copy-start | bytes 12582916
  53.1 19.9 %all-to-all-start.3 = ((bf16[16,144,256]{2,1,0:T(8,128)(2,1)}), bf16[16,144,256]{2,1,0:T(8,128)(2,1)S(1)}, u32[]{:S(2)}, u32[]{:S(2)}) async-start(bf16[16,144,256]{2,1,0:T(8,128)(2,1)} %get-tuple-element.21), calls=%async_computation.3 | async-start | bytes 2359296 | tf_op jit(solution)/shard_map/all_to_all | solution.py:348
  56.8 2.2 %copy-start.1 = (bf16[16,128,1024]{2,1,0:T(8,128)(2,1)S(1)}, bf16[16,128,1024]{2,1,0:T(8,128)(2,1)}, u32[]{:S(2)}) copy-start(bf16[16,128,1024]{2,1,0:T(8,128)(2,1)} %copy-done) | copy-start | bytes 12582916
  73.0 63.9 %copy-start.5 = (f32[768,256]{1,0:T(8,128)S(1)}, f32[768,256]{1,0:T(8,128)}, u32[]{:S(2)}) copy-start(f32[768,256]{1,0:T(8,128)} %second.1) | copy-start | bytes 2359300
  73.0 66.1 %all-to-all-start.2 = ((bf16[8,256,128]{2,1,0:T(8,128)(2,1)}), bf16[8,256,128]{2,1,0:T(8,128)(2,1)S(1)}, u32[]{:S(2)}, u32[]{:S(2)}) async-start(bf16[8,256,128]{2,1,0:T(8,128)(2,1)} %query_parts.1), calls=%async_computation.2 | async-start | bytes 1048576 | tf_op jit(solution)/shard_map/all_to_all | solution.py:376
  84.3 52.7 %copy-start.2 = (f32[768,256]{1,0:T(8,128)S(1)}, f32[768,256]{1,0:T(8,128)}, u32[]{:S(2)}) copy-start(f32[768,256]{1,0:T(8,128)} %table.3) | copy-start | bytes 2359300
  84.3 52.7 %copy-start.4 = (f32[768,256]{1,0:T(8,128)S(1)}, f32[768,256]{1,0:T(8,128)}, u32[]{:S(2)}) copy-start(f32[768,256]{1,0:T(8,128)} %first.1) | copy-start | bytes 2359300
  84.5 18.3 %collective-permute-start.3 = (bf16[6,32,256]{2,1,0:T(8,128)(2,1)S(1)}, bf16[6,32,256]{2,1,0:T(8,128)(2,1)S(1)}, u32[]{:S(2)}, u32[]{:S(2)}) collective-permute-start(bf16[6,32,256]{2,1,0:T(8,128)(2,1)S(1)} %gather_parts.1), channel_id=1, source_target_pairs={{0,128},{128,0},{256,384},{384,256},{1,129},{129,1},{257,385},{385... | collective-permute-start | bytes 294920 | tf_op jit(solution)/shard_map/ppermute | solution.py:372
  102.9 16.6 %collective-permute-start.4 = (bf16[6,32,256]{2,1,0:T(8,128)(2,1)S(1)}, bf16[6,32,256]{2,1,0:T(8,128)(2,1)S(1)}, u32[]{:S(2)}, u32[]{:S(2)}) collective-permute-start(bf16[6,32,256]{2,1,0:T(8,128)(2,1)S(1)} %add_convert_fusion), channel_id=1, source_target_pairs={{128,256},{256,128},{384,0},{0,384},{129,257},{257,129},{385,1},{1... | collective-permute-start | bytes 294920 | tf_op jit(solution)/shard_map/ppermute | solution.py:374
  119.5 7.9 %collective-permute-start.7 = (f32[6,32,256]{2,1,0:T(8,128)S(1)}, f32[6,32,256]{2,1,0:T(8,128)S(1)}, u32[]{:S(2)}, u32[]{:S(2)}) collective-permute-start(f32[6,32,256]{2,1,0:T(8,128)S(1)} %convert_add_fusion.own), channel_id=1, source_target_pairs={{0,96},{32,0},{64,32},{96,64},{1,97},{33,1},{65,33},{97,65},{2,98}... | collective-permute-start | bytes 589832 | tf_op jit(solution)/shard_map/ppermute | solution.py:387
  122.6 9.1 %collective-permute-start.6 = (f32[6,32,256]{2,1,0:T(8,128)S(1)}, f32[6,32,256]{2,1,0:T(8,128)S(1)}, u32[]{:S(2)}, u32[]{:S(2)}) collective-permute-start(f32[6,32,256]{2,1,0:T(8,128)S(1)} %convert_add_fusion.own), channel_id=1, source_target_pairs={{0,64},{32,96},{64,0},{96,32},{1,65},{33,97},{65,1},{97,33},{2,66}... | collective-permute-start | bytes 589832 | tf_op jit(solution)/shard_map/ppermute | solution.py:387
  124.8 12.1 %collective-permute-start.5 = (f32[6,32,256]{2,1,0:T(8,128)S(1)}, f32[6,32,256]{2,1,0:T(8,128)S(1)}, u32[]{:S(2)}, u32[]{:S(2)}) collective-permute-start(f32[6,32,256]{2,1,0:T(8,128)S(1)} %convert_add_fusion.own), channel_id=1, source_target_pairs={{0,32},{32,64},{64,96},{96,0},{1,33},{33,65},{65,97},{97,1},{2,34}... | collective-permute-start | bytes 589832 | tf_op jit(solution)/shard_map/ppermute | solution.py:387

commit v4 on v3

v4 whole, which is shorter than its diff:
```python
import jax
import jax.numpy as jnp
from jax import lax
from jax.experimental import pallas as pl
from jax.experimental.pallas import tpu as pltpu
from jax.sharding import Mesh, PartitionSpec as P


BLOCK = 128
D = 256
SLOTS_DEV = 4
BLOCKS_DEV = 6
NX = 4
NY = 4
NZ = 4
NC = 2
NQ = NZ * NC
SLOTS = NX * SLOTS_DEV
PART = BLOCK // NY
META = 16
CHUNK = 256
CHUNKS = NQ * BLOCK // CHUNK
TOGETHER = 4
QROWS = ("c", "zl")

logit_scale = 2.0
beta_first = 0.9
beta_second = 0.99
learn_rate = 0.01
adam_eps = 1e-08
bias_first = 1.0 - 0.9**10
bias_second = 1.0 - 0.99**10
floor_value = -1e30

f32 = jnp.float32
bf16 = jnp.bfloat16
i32 = jnp.int32


def vmem():
    return pl.BlockSpec(memory_space=pltpu.VMEM)


def hbm():
    return pl.BlockSpec(memory_space=pltpu.HBM)


def smem():
    return pl.BlockSpec(memory_space=pltpu.SMEM)


def limit(mib):
    return pltpu.CompilerParams(vmem_limit_bytes=mib << 20)


def pack_kernel(ids, count, logq, table, queries, targets, item_out, query_out):
    slot = (targets[...] >> 7).astype(f32)
    item = (targets[...] & (BLOCK - 1)).astype(f32)
    both = jnp.broadcast_to(jnp.concatenate([slot, item], axis=1), (META, D)).astype(bf16)
    for z in range(NZ):
        query_out[z, pl.ds(0, BLOCK), :] = queries[0]
        query_out[z, pl.ds(BLOCK, META), :] = both
    row = lax.broadcasted_iota(i32, (META, D), 0)
    lane = lax.broadcasted_iota(i32, (META, D), 1)
    meta = jnp.where(row == 4, count[0, 0].astype(f32), 0.0)
    for j in range(SLOTS_DEV):
        whole = jnp.full((META, D), logq[0, j], f32)
        high = whole.astype(bf16).astype(f32)
        mid = (whole - high).astype(bf16).astype(f32)
        low = whole - high - mid
        ident = jnp.full((META, D), ids[0, j].astype(f32), f32)
        value = jnp.where(row == 0, high, jnp.where(row == 1, mid, jnp.where(row == 2, low, ident)))
        meta = jnp.where((lane == j) & (row < 4), value, meta)
    item_out[pl.ds(SLOTS_DEV * BLOCK, META), :] = meta.astype(bf16)
    for j in range(SLOTS_DEV):
        rows = table[pl.ds(pl.multiple_of(ids[0, j] * BLOCK, BLOCK), BLOCK), :]
        item_out[pl.ds(j * BLOCK, BLOCK), :] = (logit_scale * rows.astype(bf16).astype(f32)).astype(bf16)


def query_chunk(queries, b):
    return jnp.concatenate([queries[2 * b, pl.ds(0, BLOCK), :], queries[2 * b + 1, pl.ds(0, BLOCK), :]], axis=0)


def target_codes(queries):
    parts = []
    for r in range(NQ):
        row = queries[r, pl.ds(BLOCK, META), :].astype(f32)[0:1]
        parts.append((row[:, :BLOCK] * BLOCK + row[:, BLOCK:]).astype(i32))
    return jnp.concatenate(parts, axis=1)


def totals_kernel(
    place, own, one, two, three, queries,
    out, rows_all, metas, live, shifts, scores, tops, sums,
):
    lane = lax.broadcasted_iota(i32, (1, D), 1)
    number = jnp.int32(0)
    for k, piece in enumerate((own, one, two, three)):
        x = (place[2] - k) & (NX - 1)
        raw = piece[pl.ds(SLOTS_DEV * BLOCK, META), :]
        metas[x] = raw
        meta = raw.astype(f32)
        row = meta[0:1] + meta[1:2] + meta[2:3]
        count = jnp.max(meta[4:5]).astype(i32)
        for j in range(SLOTS_DEV):
            shifts[number] = jnp.sum(jnp.where(lane == j, row, 0.0))
            live[number] = x * (NQ * SLOTS_DEV) + place[0] * SLOTS_DEV + j
            rows_all[number] = piece[pl.ds(j * BLOCK, BLOCK), :]
            number = number + (j < count).astype(i32)
    live[SLOTS + 1] = number

    def pad(i, carry):
        rows_all[i] = jnp.zeros((BLOCK, D), bf16)
        shifts[i] = -floor_value
        live[i] = -1
        return carry

    lax.fori_loop(number, (number + TOGETHER - 1) // TOGETHER * TOGETHER, pad, 0)
    pairs = (number + 1) // 2
    tops[...] = jnp.full(tops.shape, floor_value, f32)
    sums[...] = jnp.zeros(sums.shape, f32)

    def score(p, carry):
        rows = rows_all[pl.ds(2 * p, 2)].reshape(2 * BLOCK, D)
        for b in range(CHUNKS):
            cols = pl.ds(b * CHUNK, CHUNK)
            doubled = pair_products(rows, queries, b)
            top = tops[:, cols]
            for h in range(2):
                half = doubled[h * BLOCK : (h + 1) * BLOCK]
                scores[2 * p + h, :, cols] = half
                top = jnp.maximum(top, jnp.max(half.reshape(BLOCK // 8, 8, CHUNK), axis=0) - shifts[2 * p + h])
            tops[:, cols] = top
        return carry

    lax.fori_loop(0, pairs, score, 0)
    top_row = jnp.max(tops[...], axis=0, keepdims=True)

    def weigh(p, carry):
        for h in range(2):
            i = 2 * p + h
            for b in range(CHUNKS):
                cols = pl.ds(b * CHUNK, CHUNK)
                base = top_row[:, b * CHUNK : (b + 1) * CHUNK] + shifts[i]
                weight = jnp.exp(scores[i, :, cols] - base)
                sums[:, cols] = sums[:, cols] + jnp.sum(weight.reshape(BLOCK // 8, 8, CHUNK), axis=0)
        return carry

    lax.fori_loop(0, pairs, weigh, 0)
    norm = top_row + jnp.log(jnp.sum(sums[...], axis=0, keepdims=True))
    norms = jnp.concatenate([norm[:, r * BLOCK : (r + 1) * BLOCK] for r in range(NQ)], axis=0)
    for d in range(NQ):
        out[d] = norms


def pair_products(rows, queries, b):
    return lax.dot_general(rows, query_chunk(queries, b), (((1,), (1,)), ((), ())), preferred_element_type=f32)


def dlogits(doubled, norm, codes, live, shifts, i):
    probs = jnp.exp(doubled - (norm + shifts[i]))
    item_index = lax.broadcasted_iota(i32, (BLOCK, CHUNK), 0)
    return jnp.where(item_index == codes - live[i] * BLOCK, probs - 1.0, probs).astype(bf16)


def item_kernel(place, live, shifts, rows_all, metas, queries, stats, item_out, norm_out, held):
    top = stats[0]
    for r in range(1, NQ):
        top = jnp.maximum(top, stats[r])
    total = jnp.zeros_like(top)
    for r in range(NQ):
        total = total + jnp.exp(stats[r] - top)
    norms = top + jnp.log(total)
    norm_row = jnp.concatenate([norms[r : r + 1] for r in range(NQ)], axis=1)
    norm_out[...] = norm_row
    codes = target_codes(queries)
    item_out[...] = jnp.zeros(item_out.shape, bf16)
    for x in range(NX):
        for y in range(NY):
            item_out[y * NX + x, pl.ds(SLOTS_DEV * PART, META), :] = metas[x]
    number = live[SLOTS + 1]

    def one_pair(p, carry):
        rows = rows_all[pl.ds(2 * p, 2)].reshape(2 * BLOCK, D)
        for b in range(CHUNKS):
            doubled = pair_products(rows, queries, b)
            norm = norm_row[:, b * CHUNK : (b + 1) * CHUNK]
            code = codes[:, b * CHUNK : (b + 1) * CHUNK]
            for h in range(2):
                half = pl.ds(h * BLOCK, BLOCK)
                held[half, pl.ds(b * CHUNK, CHUNK)] = dlogits(
                    doubled[h * BLOCK : (h + 1) * BLOCK], norm, code, live, shifts, 2 * p + h
                )
        every = jnp.concatenate([query_chunk(queries, b) for b in range(CHUNKS)], axis=0)
        total = jnp.dot(held[...], every, preferred_element_type=f32)
        for h in range(2):
            i = 2 * p + h
            part = (logit_scale * total[h * BLOCK : (h + 1) * BLOCK]).astype(bf16)

            @pl.when(i < number)
            def _():
                x = live[i] // (NQ * SLOTS_DEV)
                rows = pl.ds(pl.multiple_of(live[i] % SLOTS_DEV * PART, PART), PART)
                for y in range(NY):
                    item_out[y * NX + x, rows, :] = part[y * PART : (y + 1) * PART]

        return carry

    lax.fori_loop(0, (number + 1) // 2, one_pair, 0)


def query_kernel(live, shifts, rows_all, queries, norms, out, total, picks, taken):
    codes = target_codes(queries)
    norm_row = norms[...]
    total[...] = jnp.zeros(total.shape, f32)
    picks[...] = jnp.zeros(picks.shape, f32)
    taken[...] = jnp.zeros(taken.shape, f32)
    item_index = lax.broadcasted_iota(i32, (BLOCK, CHUNK), 0)

    def one_group(g, carry):
        rows = rows_all[pl.ds(g * TOGETHER, TOGETHER)].reshape(TOGETHER * BLOCK, D)
        turned = rows.T
        for b in range(CHUNKS):
            cols = pl.ds(b * CHUNK, CHUNK)
            doubled = pair_products(rows, queries, b)
            norm = norm_row[:, b * CHUNK : (b + 1) * CHUNK]
            code = codes[:, b * CHUNK : (b + 1) * CHUNK]
            parts = []
            for h in range(TOGETHER):
                i = g * TOGETHER + h
                block = doubled[h * BLOCK : (h + 1) * BLOCK]
                wanted = code - live[i] * BLOCK
                match = item_index == wanted
                marked = jnp.where(match, block, 0.0)
                picks[:, cols] = picks[:, cols] + jnp.sum(marked.reshape(BLOCK // 8, 8, CHUNK), axis=0)
                here = (wanted >= 0) & (wanted < BLOCK)
                taken[:, cols] = taken[:, cols] + jnp.where(here, shifts[i], 0.0)
                probs = jnp.exp(block - (norm + shifts[i]))
                parts.append(jnp.where(match, probs - 1.0, probs).astype(bf16))
            total[:, cols] = total[:, cols] + jnp.dot(
                turned, jnp.concatenate(parts, axis=0), preferred_element_type=f32
            )
        return carry

    lax.fori_loop(0, (live[SLOTS + 1] + TOGETHER - 1) // TOGETHER, one_group, 0)
    row = lax.broadcasted_iota(i32, (META, BLOCK), 0)
    for r in range(NQ):
        cols = pl.ds(r * BLOCK, BLOCK)
        out[r, pl.ds(0, D), :] = total[:, cols].astype(bf16)
        pick = jnp.sum(picks[:, cols], axis=0, keepdims=True) - taken[:, cols]
        pick = jnp.broadcast_to(pick, (META, BLOCK))
        high = pick.astype(bf16).astype(f32)
        mid = (pick - high).astype(bf16).astype(f32)
        low = pick - high - mid
        three = jnp.where(row == 0, high, jnp.where(row == 1, mid, jnp.where(row == 2, low, 0.0)))
        out[r, pl.ds(D, META), :] = three.astype(bf16)


def gather_parts_kernel(parts, out, total):
    lane = lax.broadcasted_iota(i32, (1, D), 1)
    total[...] = jnp.zeros(total.shape, f32)
    for y in range(NY):
        meta = parts[y * NX, pl.ds(SLOTS_DEV * PART, META), :].astype(f32)
        for j in range(SLOTS_DEV):
            block = jnp.sum(jnp.where(lane == j, meta[3:4], 0.0)).astype(i32)
            piece = jnp.zeros((PART, D), f32)
            for x in range(NX):
                piece = piece + parts[y * NX + x, pl.ds(j * PART, PART), :].astype(f32)
            total[block] = total[block] + piece
    out[...] = total[...].astype(bf16)


def adam_kernel(place, own, one, two, three, table, first, second, *rest):
    outs, results, sems = rest[:3], rest[3:6], rest[6]
    copies = []
    for b in range(BLOCKS_DEV):
        for k, piece in enumerate((own, one, two, three)):
            y = (place[3] - k) & (NY - 1)
            rows = pl.ds(pl.multiple_of(b * BLOCK + y * PART, PART), PART)
            grad = piece[b]
            first_new = beta_first * first[rows, :] + (1.0 - beta_first) * grad
            second_new = beta_second * second[rows, :] + (1.0 - beta_second) * grad * grad
            results[1][rows, :] = first_new
            results[2][rows, :] = second_new
            results[0][rows, :] = table[rows, :] - learn_rate * (first_new / bias_first) / (
                jnp.sqrt(second_new / bias_second) + adam_eps
            )
        block = pl.ds(b * BLOCK, BLOCK)
        for n in range(3):
            copy = pltpu.make_async_copy(results[n].at[block, :], outs[n].at[block, :], sems.at[b, n])
            copy.start()
            copies.append(copy)
    for copy in copies:
        copy.wait()


def query_sum_kernel(place, norms, parts, loss_out, out):
    total = parts[0].astype(f32)
    for r in range(1, NQ):
        total = total + parts[r].astype(f32)
    out[0] = total[:D].T
    pick = jnp.sum(total[D : D + META], axis=0, keepdims=True)
    loss_out[...] = norms[:, pl.ds(pl.multiple_of(place[1] * BLOCK, BLOCK), BLOCK)] - pick


def step(queries, targets, samp_ids, counts, logq, table, first_moment, second_moment):
    place = lax.axis_index("zl") * NC + lax.axis_index("c")
    own = lax.axis_index("c") * NZ + lax.axis_index("zl")
    where = jnp.stack([place, own, lax.axis_index("x"), lax.axis_index("y")]).astype(i32)
    item_shape = jax.ShapeDtypeStruct((SLOTS_DEV * BLOCK + META, D), bf16)
    items, query_rows = pl.pallas_call(
        pack_kernel,
        out_shape=(item_shape, jax.ShapeDtypeStruct((NZ, BLOCK + META, D), bf16)),
        in_specs=[smem(), smem(), smem(), vmem(), vmem(), vmem()],
        out_specs=(vmem(), vmem()),
        name="pack",
    )(samp_ids, counts, logq, table, queries, targets)

    every_query = lax.all_to_all(query_rows, "zl", 0, 0, tiled=True)
    pieces = [items]
    for k in range(1, NX):
        pieces.append(lax.ppermute(items, "x", [(i, (i + k) % NX) for i in range(NX)]))
    every_query = lax.all_gather(every_query, "c", axis=0, tiled=True)

    wide = NQ * BLOCK
    stats, rows_all, metas, live, shifts = pl.pallas_call(
        totals_kernel,
        out_shape=(
            jax.ShapeDtypeStruct((NQ, NQ, BLOCK), f32),
            jax.ShapeDtypeStruct((SLOTS + 1, BLOCK, D), bf16),
            jax.ShapeDtypeStruct((NX, META, D), bf16),
            jax.ShapeDtypeStruct((SLOTS + 2,), i32),
            jax.ShapeDtypeStruct((SLOTS + 1,), f32),
        ),
        in_specs=[smem()] + [vmem()] * (NX + 1),
        out_specs=(vmem(),) * 3 + (smem(), smem()),
        scratch_shapes=[pltpu.VMEM((SLOTS, BLOCK, wide), f32)]
        + [pltpu.VMEM((8, wide), f32)] * 2,
        compiler_params=limit(16),
        name="totals",
    )(where, *pieces, every_query)
    stats = lax.all_to_all(stats, QROWS, 0, 0, tiled=True)
    item_parts, norms = pl.pallas_call(
        item_kernel,
        out_shape=(
            jax.ShapeDtypeStruct((NY * NX, SLOTS_DEV * PART + META, D), bf16),
            jax.ShapeDtypeStruct((1, wide), f32),
        ),
        in_specs=[smem()] * 3 + [vmem()] * 4,
        out_specs=(vmem(),) * 2,
        scratch_shapes=[pltpu.VMEM((2 * BLOCK, wide), bf16)],
        compiler_params=limit(12),
        name="items",
    )(where, live, shifts, rows_all, metas, every_query, stats)

    item_parts = lax.all_to_all(item_parts, ("y", "x"), 0, 0, tiled=True)
    query_parts = pl.pallas_call(
        query_kernel,
        out_shape=jax.ShapeDtypeStruct((NQ, D + META, BLOCK), bf16),
        in_specs=[smem(), smem()] + [vmem()] * 3,
        out_specs=vmem(),
        scratch_shapes=[pltpu.VMEM((D, wide), f32), pltpu.VMEM((8, wide), f32), pltpu.VMEM((1, wide), f32)],
        compiler_params=limit(8),
        cost_estimate=pl.CostEstimate(flops=1 << 31, bytes_accessed=6 << 20, transcendentals=0),
        name="query_parts",
    )(live, shifts, rows_all, every_query, norms)
    part = pl.pallas_call(
        gather_parts_kernel,
        out_shape=jax.ShapeDtypeStruct((BLOCKS_DEV, PART, D), bf16),
        in_specs=[vmem()],
        out_specs=vmem(),
        scratch_shapes=[pltpu.VMEM((BLOCKS_DEV, PART, D), f32)],
        compiler_params=limit(4),
        name="gather_parts",
    )(item_parts)
    other = lax.ppermute(part, "zh", [(0, 1), (1, 0), (2, 3), (3, 2)])
    part = lax.optimization_barrier((part.astype(f32) + other.astype(f32)).astype(bf16))
    other = lax.ppermute(part, "zh", [(1, 2), (2, 1), (3, 0), (0, 3)])
    part = part.astype(f32) + other.astype(f32)
    query_parts = lax.all_to_all(query_parts, QROWS, 0, 0, tiled=True)
    loss, query_grad = pl.pallas_call(
        query_sum_kernel,
        out_shape=(jax.ShapeDtypeStruct((1, BLOCK), f32), jax.ShapeDtypeStruct((1, BLOCK, D), f32)),
        in_specs=[smem(), vmem(), vmem()],
        out_specs=(vmem(), vmem()),
        compiler_params=limit(4),
        name="query_sum",
    )(where, norms, query_parts)
    grads = [part]
    for k in range(1, NY):
        grads.append(lax.ppermute(part, "y", [(i, (i + k) % NY) for i in range(NY)]))

    new_table, new_first, new_second = pl.pallas_call(
        adam_kernel,
        out_shape=(jax.ShapeDtypeStruct(table.shape, f32),) * 3,
        in_specs=[smem()] + [vmem()] * (NY + 3),
        out_specs=(hbm(),) * 3,
        scratch_shapes=[pltpu.VMEM(table.shape, f32)] * 3 + [pltpu.SemaphoreType.DMA((BLOCKS_DEV, 3))],
        compiler_params=limit(12),
        name="adam",
    )(where, *grads, table, first_moment, second_moment)
    return loss, query_grad, new_table, new_first, new_second


def solution(mesh):
    fine = Mesh(mesh.devices.reshape(4, NY, NX, NZ, NC), ("zh", "y", "x", "zl", "c"))
    rep = ("zh", "y")
    shard = ("x", "zl", "c")
    in_specs = (
        P(rep, shard, None),
        P(rep, shard),
        P(rep, shard),
        P(rep, shard),
        P(rep, shard),
        P(shard, None),
        P(shard, None),
        P(shard, None),
    )
    out_specs = (
        P(rep, shard),
        P(rep, shard, None),
        P(shard, None),
        P(shard, None),
        P(shard, None),
    )
    return jax.shard_map(step, mesh=fine, in_specs=in_specs, out_specs=out_specs, check_vma=False)
```

time: 141 us -> 136 us (0.965)
  the two profiles are of different devices: /device:TPU:97 before, /device:TPU:64 now
where the time goes in v4:
time: 136 us; the launch traced here: 135 us
  waiting for transfers between devices  56.6 us (42%)
  starting transfers between devices  47.7 us (35%)
  Pallas kernels  17.3 us (13%)
  blocking collectives  11.8 us (9%)
  between operations  1.41 us (1%)
    all_to_all x1, waiting for transfers between devices, step(): item_parts = lax.all_to_all(item_parts, ('y', 'x'), 0, 0, tiled=True)  17.2 us
    ppermute x1, waiting for transfers between devices, step(): other = lax.ppermute(part, 'zh', [(0, 1), (1, 0), (2, 3), (3, 2)])  16.2 us
    ppermute x3, starting transfers between devices, step(): lax.ppermute(part, 'y', [(i, (i + k) % NY) for i in range(NY)])  10 us
    all_to_all x1, blocking collectives, step(): stats = lax.all_to_all(stats, QROWS, 0, 0, tiled=True)  9.63 us
    ppermute x1, starting transfers between devices, step(): other = lax.ppermute(part, 'zh', [(0, 1), (1, 0), (2, 3), (3, 2)])  9.03 us
    all_to_all x1, starting transfers between devices, step(): every_query = lax.all_to_all(query_rows, 'zl', 0, 0, tiled=True)  8.55 us
    ppermute x3, waiting for transfers between devices, step(): lax.ppermute(items, 'x', [(i, (i + k) % NX) for i in range(NX)])  8.49 us
    ppermute x3, starting transfers between devices, step(): lax.ppermute(items, 'x', [(i, (i + k) % NX) for i in range(NX)])  7.75 us
  transfers between devices with their start and end apart: 11, of which 9 were waited for; matrix products, arithmetic and copies ran while one was open for 0% of the time, Pallas kernels for 5%

profile of v4, /device:TPU:64, one launch (start us, length us, event | category | flops | bytes accessed | tf_op | source)
XLA Modules:
  0.0 135.0 jit_solution(8754121854352254097)
XLA Ops:
  1.3 2.0 %pack.1 = (bf16[528,256]{1,0:T(8,128)(2,1)}, bf16[4,144,256]{2,1,0:T(8,128)(2,1)}) custom-call(s32[1,4]{1,0:T(1,128)} %ids.1, s32[1,1]{1,0:T(1,128)S(6)} %copy.13.count, f32[1,4]{1,0:T(1,128)} %logq.1, f32[768,256]{1,0:T(8,128)} %table.3, bf16[1,128,256]{2,1,0:T(8,128)(2,1)} %queries.1, s32[1,128]{1,0:T(1,128)} %targets.1), custom_call_target="tpu_custom_call" | custom-call | tf_op jit(solution)/shard_map/pack/pallas_call | solution.py:311
  3.3 0.0 copy-start.3
  3.3 8.6 %all-to-all-start = ((bf16[4,144,256]{2,1,0:T(8,128)(2,1)}), bf16[4,144,256]{2,1,0:T(8,128)(2,1)S(1)}, u32[]{:S(2)}, u32[]{:S(2)}) async-start(bf16[4,144,256]{2,1,0:T(8,128)(2,1)} %get-tuple-element.20), calls=%async_computation | async-start | bytes 589824 | tf_op jit(solution)/shard_map/all_to_all | solution.py:319
  11.8 1.9 %collective-permute-start.2 = (bf16[528,256]{1,0:T(8,128)(2,1)}, bf16[528,256]{1,0:T(8,128)(2,1)S(1)}, u32[]{:S(2)}, u32[]{:S(2)}) collective-permute-start(bf16[528,256]{1,0:T(8,128)(2,1)} %get-tuple-element.19.own), channel_id=1, source_target_pairs={{0,24},{8,0},{16,8},{24,16},{1,25},{9,1},{17,9},{25,17},{2,26},{10... | collective-permute-start | bytes 811016 | tf_op jit(solution)/shard_map/ppermute | solution.py:322
  13.8 2.6 %collective-permute-start.1 = (bf16[528,256]{1,0:T(8,128)(2,1)}, bf16[528,256]{1,0:T(8,128)(2,1)S(1)}, u32[]{:S(2)}, u32[]{:S(2)}) collective-permute-start(bf16[528,256]{1,0:T(8,128)(2,1)} %get-tuple-element.19.own), channel_id=1, source_target_pairs={{0,16},{8,24},{16,0},{24,8},{1,17},{9,25},{17,1},{25,9},{2,18},{10... | collective-permute-start | bytes 811016 | tf_op jit(solution)/shard_map/ppermute | solution.py:322
  16.3 3.3 %collective-permute-start = (bf16[528,256]{1,0:T(8,128)(2,1)}, bf16[528,256]{1,0:T(8,128)(2,1)S(1)}, u32[]{:S(2)}, u32[]{:S(2)}) collective-permute-start(bf16[528,256]{1,0:T(8,128)(2,1)} %get-tuple-element.19.own), channel_id=1, source_target_pairs={{0,8},{8,16},{16,24},{24,0},{1,9},{9,17},{17,25},{25,1},{2,10},{10... | collective-permute-start | bytes 811016 | tf_op jit(solution)/shard_map/ppermute | solution.py:322
  19.6 0.1 pad_add_fusion.place
  19.7 0.0 all-to-all-done
  19.7 2.2 %all_gather.3.queries = bf16[8,144,256]{2,1,0:T(8,128)(2,1)S(1)} all-gather(bf16[4,144,256]{2,1,0:T(8,128)(2,1)S(1)} %all-to-all-done), channel_id=1, replica_groups=mesh['zh'=4,'y'=4,'x'=4,'zl'=4,'c'=2] {'c'}, dimensions={0}, use_global_device_ids=true | all-gather | bytes 884736 | tf_op jit(solution)/shard_map/all_gather | solution.py:323
  21.9 0.9 collective-permute-done.2.three
  22.8 4.0 %collective-permute-done.1.two = bf16[528,256]{1,0:T(8,128)(2,1)S(1)} collective-permute-done((bf16[528,256]{1,0:T(8,128)(2,1)}, bf16[528,256]{1,0:T(8,128)(2,1)S(1)}, u32[]{:S(2)}, u32[]{:S(2)}) %collective-permute-start.1) | collective-permute-done | bytes 270368 | tf_op jit(solution)/shard_map/ppermute | solution.py:322
  26.7 3.7 %collective-permute-done.one = bf16[528,256]{1,0:T(8,128)(2,1)S(1)} collective-permute-done((bf16[528,256]{1,0:T(8,128)(2,1)}, bf16[528,256]{1,0:T(8,128)(2,1)S(1)}, u32[]{:S(2)}, u32[]{:S(2)}) %collective-permute-start) | collective-permute-done | bytes 270368 | tf_op jit(solution)/shard_map/ppermute | solution.py:322
  30.4 0.0 copy-done.3
  30.4 3.3 %totals.1 = (f32[8,8,128]{2,1,0:T(8,128)S(1)}, bf16[17,128,256]{2,1,0:T(8,128)(2,1)S(1)}, bf16[4,16,256]{2,1,0:T(8,128)(2,1)S(1)}, s32[18]{0:T(128)S(1)}, f32[17]{0:T(128)S(1)}) custom-call(s32[4]{0:T(128)S(1)} %pad_add_fusion.place, bf16[528,256]{1,0:T(8,128)(2,1)S(1)} %copy-done.3, bf16[528,256]{1,0:T(8,128)(2,1)S(1)} %collective-permute-done.one, ...), custom_call_target="tpu_custom_call" | custom-call | tf_op jit(solution)/shard_map/totals/pallas_call | solution.py:326
  33.7 9.6 %all_to_all.20.stats = f32[8,8,128]{2,1,0:T(8,128)S(1)} all-to-all(f32[8,8,128]{2,1,0:T(8,128)S(1)} %get-tuple-element.25), channel_id=1, replica_groups=mesh['zh'=4,'y'=4,'x'=4,'zl'=4,'c'=2] {'c','zl'}, dimensions={0} | all-to-all | bytes 65536 | tf_op jit(solution)/shard_map/all_to_all | solution.py:342
  43.3 4.1 %items.1 = (bf16[16,144,256]{2,1,0:T(8,128)(2,1)}, f32[1,1024]{1,0:T(1,128)S(1)}) custom-call(s32[4]{0:T(128)S(1)} %pad_add_fusion.place, s32[18]{0:T(128)S(1)} %get-tuple-element.21.live, f32[17]{0:T(128)S(1)} %get-tuple-element.22.shifts, bf16[17,128,256]{2,1,0:T(8,128)(2,1)S(1)} %get-tuple-element.23.rows_all, ...), custom_call_target="tpu_custom_call" | custom-call | tf_op jit(solution)/shard_map/items/pallas_call | solution.py:343
  47.5 4.9 %all-to-all-start.3 = ((bf16[16,144,256]{2,1,0:T(8,128)(2,1)}), bf16[16,144,256]{2,1,0:T(8,128)(2,1)S(1)}, u32[]{:S(2)}, u32[]{:S(2)}) async-start(bf16[16,144,256]{2,1,0:T(8,128)(2,1)} %get-tuple-element.29), calls=%async_computation.3 | async-start | bytes 2359296 | tf_op jit(solution)/shard_map/all_to_all | solution.py:356
  52.4 4.1 %query_parts.1 = bf16[8,272,128]{2,1,0:T(8,128)(2,1)} custom-call(s32[18]{0:T(128)S(1)} %get-tuple-element.21.live, f32[17]{0:T(128)S(1)} %get-tuple-element.22.shifts, bf16[17,128,256]{2,1,0:T(8,128)(2,1)S(1)} %get-tuple-element.23.rows_all, bf16[8,144,256]{2,1,0:T(8,128)(2,1)S(1)} %all_gather.3.queries, f32[1,1024]{1,0:T(1,128)S(1)} %get-tuple-element.26.norms), custom_call_target="tpu_custom_call" | custom-call | flops 2147483648 | bytes 6291456 | tf_op jit(solution)/shard_map/query_parts/pallas_call | solution.py:357
  56.5 17.2 %all-to-all-done.3.parts = bf16[16,144,256]{2,1,0:T(8,128)(2,1)S(1)} async-done(((bf16[16,144,256]{2,1,0:T(8,128)(2,1)}), bf16[16,144,256]{2,1,0:T(8,128)(2,1)S(1)}, u32[]{:S(2)}, u32[]{:S(2)}) %all-to-all-start.3) | async-done | bytes 1179680 | tf_op jit(solution)/shard_map/all_to_all | solution.py:356
  73.7 0.0 copy-start.2
  73.7 4.3 %all-to-all-start.2 = ((bf16[8,272,128]{2,1,0:T(8,128)(2,1)}), bf16[8,272,128]{2,1,0:T(8,128)(2,1)S(1)}, u32[]{:S(2)}, u32[]{:S(2)}) async-start(bf16[8,272,128]{2,1,0:T(8,128)(2,1)} %query_parts.1), calls=%async_computation.2 | async-start | bytes 1114112 | tf_op jit(solution)/shard_map/all_to_all | solution.py:380
  78.0 0.0 copy-start
  78.0 0.0 copy-start.1
  78.1 0.2 gather_parts.1
  78.3 9.0 %collective-permute-start.3 = (bf16[6,32,256]{2,1,0:T(8,128)(2,1)S(1)}, bf16[6,32,256]{2,1,0:T(8,128)(2,1)S(1)}, u32[]{:S(2)}, u32[]{:S(2)}) collective-permute-start(bf16[6,32,256]{2,1,0:T(8,128)(2,1)S(1)} %gather_parts.1), channel_id=1, source_target_pairs={{0,128},{128,0},{256,384},{384,256},{1,129},{129,1},{257,385},{385... | collective-permute-start | bytes 294920 | tf_op jit(solution)/shard_map/ppermute | solution.py:376
  87.3 16.2 %collective-permute-done.3 = bf16[6,32,256]{2,1,0:T(8,128)(2,1)S(1)} collective-permute-done((bf16[6,32,256]{2,1,0:T(8,128)(2,1)S(1)}, bf16[6,32,256]{2,1,0:T(8,128)(2,1)S(1)}, u32[]{:S(2)}, u32[]{:S(2)}) %collective-permute-start.3) | collective-permute-done | bytes 98336 | tf_op jit(solution)/shard_map/ppermute | solution.py:376
  103.5 3.1 %collective-permute-start.4 = (bf16[6,32,256]{2,1,0:T(8,128)(2,1)S(1)}, bf16[6,32,256]{2,1,0:T(8,128)(2,1)S(1)}, u32[]{:S(2)}, u32[]{:S(2)}) collective-permute-start(bf16[6,32,256]{2,1,0:T(8,128)(2,1)S(1)} %add_convert_fusion), channel_id=1, source_target_pairs={{128,256},{256,128},{384,0},{0,384},{129,257},{257,129},{385,1},{1... | collective-permute-start | bytes 294920 | tf_op jit(solution)/shard_map/ppermute | solution.py:378
  106.6 7.3 %collective-permute-done.4 = bf16[6,32,256]{2,1,0:T(8,128)(2,1)S(1)} collective-permute-done((bf16[6,32,256]{2,1,0:T(8,128)(2,1)S(1)}, bf16[6,32,256]{2,1,0:T(8,128)(2,1)S(1)}, u32[]{:S(2)}, u32[]{:S(2)}) %collective-permute-start.4) | collective-permute-done | bytes 98336 | tf_op jit(solution)/shard_map/ppermute | solution.py:378
  114.0 3.3 %collective-permute-start.7 = (f32[6,32,256]{2,1,0:T(8,128)S(1)}, f32[6,32,256]{2,1,0:T(8,128)S(1)}, u32[]{:S(2)}, u32[]{:S(2)}) collective-permute-start(f32[6,32,256]{2,1,0:T(8,128)S(1)} %convert_add_fusion.own), channel_id=1, source_target_pairs={{0,96},{32,0},{64,32},{96,64},{1,97},{33,1},{65,33},{97,65},{2,98}... | collective-permute-start | bytes 589832 | tf_op jit(solution)/shard_map/ppermute | solution.py:391
  117.2 3.4 %collective-permute-start.6 = (f32[6,32,256]{2,1,0:T(8,128)S(1)}, f32[6,32,256]{2,1,0:T(8,128)S(1)}, u32[]{:S(2)}, u32[]{:S(2)}) collective-permute-start(f32[6,32,256]{2,1,0:T(8,128)S(1)} %convert_add_fusion.own), channel_id=1, source_target_pairs={{0,64},{32,96},{64,0},{96,32},{1,65},{33,97},{65,1},{97,33},{2,66}... | collective-permute-start | bytes 589832 | tf_op jit(solution)/shard_map/ppermute | solution.py:391
  120.7 3.3 %collective-permute-start.5 = (f32[6,32,256]{2,1,0:T(8,128)S(1)}, f32[6,32,256]{2,1,0:T(8,128)S(1)}, u32[]{:S(2)}, u32[]{:S(2)}) collective-permute-start(f32[6,32,256]{2,1,0:T(8,128)S(1)} %convert_add_fusion.own), channel_id=1, source_target_pairs={{0,32},{32,64},{64,96},{96,0},{1,33},{33,65},{65,97},{97,1},{2,34}... | collective-permute-start | bytes 589832 | tf_op jit(solution)/shard_map/ppermute | solution.py:391
  124.0 1.8 %collective-permute-done.7.three = f32[6,32,256]{2,1,0:T(8,128)S(1)} collective-permute-done((f32[6,32,256]{2,1,0:T(8,128)S(1)}, f32[6,32,256]{2,1,0:T(8,128)S(1)}, u32[]{:S(2)}, u32[]{:S(2)}) %collective-permute-start.7) | collective-permute-done | bytes 196640 | tf_op jit(solution)/shard_map/ppermute | solution.py:391
  125.8 2.6 %collective-permute-done.6.two = f32[6,32,256]{2,1,0:T(8,128)S(1)} collective-permute-done((f32[6,32,256]{2,1,0:T(8,128)S(1)}, f32[6,32,256]{2,1,0:T(8,128)S(1)}, u32[]{:S(2)}, u32[]{:S(2)}) %collective-permute-start.6) | collective-permute-done | bytes 196640 | tf_op jit(solution)/shard_map/ppermute | solution.py:391
  128.4 3.0 %collective-permute-done.5.one = f32[6,32,256]{2,1,0:T(8,128)S(1)} collective-permute-done((f32[6,32,256]{2,1,0:T(8,128)S(1)}, f32[6,32,256]{2,1,0:T(8,128)S(1)}, u32[]{:S(2)}, u32[]{:S(2)}) %collective-permute-start.5) | collective-permute-done | bytes 196640 | tf_op jit(solution)/shard_map/ppermute | solution.py:391
  131.4 0.0 copy-done.2
  131.4 0.0 copy-done
  131.4 0.0 copy-done.1
  131.4 2.2 %adam.1 = (f32[768,256]{1,0:T(8,128)}, f32[768,256]{1,0:T(8,128)}, f32[768,256]{1,0:T(8,128)}) custom-call(s32[4]{0:T(128)S(1)} %pad_add_fusion.place, f32[6,32,256]{2,1,0:T(8,128)S(1)} %convert_add_fusion.own, f32[6,32,256]{2,1,0:T(8,128)S(1)} %collective-permute-done.5.one, f32[6,32,256]{2,1,0:T(8,128)S(1)} %collective-permute-done.6.two, ...), custom_call_target="tpu_custom_call" | custom-call | tf_op jit(solution)/shard_map/adam/pallas_call | solution.py:393
  133.6 0.0 all-to-all-done.2.parts
  133.6 1.3 query_sum.1
  (2 shorter events, 0.1 us)
Async XLA Ops:
  3.3 27.1 %copy-start.3 = (bf16[528,256]{1,0:T(8,128)(2,1)S(1)}, bf16[528,256]{1,0:T(8,128)(2,1)}, u32[]{:S(2)}) copy-start(bf16[528,256]{1,0:T(8,128)(2,1)} %get-tuple-element.19.own) | copy-start | bytes 811012
  3.3 16.4 %all-to-all-start = ((bf16[4,144,256]{2,1,0:T(8,128)(2,1)}), bf16[4,144,256]{2,1,0:T(8,128)(2,1)S(1)}, u32[]{:S(2)}, u32[]{:S(2)}) async-start(bf16[4,144,256]{2,1,0:T(8,128)(2,1)} %get-tuple-element.20), calls=%async_computation | async-start | bytes 589824 | tf_op jit(solution)/shard_map/all_to_all | solution.py:319
  11.8 10.9 %collective-permute-start.2 = (bf16[528,256]{1,0:T(8,128)(2,1)}, bf16[528,256]{1,0:T(8,128)(2,1)S(1)}, u32[]{:S(2)}, u32[]{:S(2)}) collective-permute-start(bf16[528,256]{1,0:T(8,128)(2,1)} %get-tuple-element.19.own), channel_id=1, source_target_pairs={{0,24},{8,0},{16,8},{24,16},{1,25},{9,1},{17,9},{25,17},{2,26},{10... | collective-permute-start | bytes 811016 | tf_op jit(solution)/shard_map/ppermute | solution.py:322
  13.8 13.0 %collective-permute-start.1 = (bf16[528,256]{1,0:T(8,128)(2,1)}, bf16[528,256]{1,0:T(8,128)(2,1)S(1)}, u32[]{:S(2)}, u32[]{:S(2)}) collective-permute-start(bf16[528,256]{1,0:T(8,128)(2,1)} %get-tuple-element.19.own), channel_id=1, source_target_pairs={{0,16},{8,24},{16,0},{24,8},{1,17},{9,25},{17,1},{25,9},{2,18},{10... | collective-permute-start | bytes 811016 | tf_op jit(solution)/shard_map/ppermute | solution.py:322
  16.3 14.1 %collective-permute-start = (bf16[528,256]{1,0:T(8,128)(2,1)}, bf16[528,256]{1,0:T(8,128)(2,1)S(1)}, u32[]{:S(2)}, u32[]{:S(2)}) collective-permute-start(bf16[528,256]{1,0:T(8,128)(2,1)} %get-tuple-element.19.own), channel_id=1, source_target_pairs={{0,8},{8,16},{16,24},{24,0},{1,9},{9,17},{17,25},{25,1},{2,10},{10... | collective-permute-start | bytes 811016 | tf_op jit(solution)/shard_map/ppermute | solution.py:322
  47.5 26.2 %all-to-all-start.3 = ((bf16[16,144,256]{2,1,0:T(8,128)(2,1)}), bf16[16,144,256]{2,1,0:T(8,128)(2,1)S(1)}, u32[]{:S(2)}, u32[]{:S(2)}) async-start(bf16[16,144,256]{2,1,0:T(8,128)(2,1)} %get-tuple-element.29), calls=%async_computation.3 | async-start | bytes 2359296 | tf_op jit(solution)/shard_map/all_to_all | solution.py:356
  73.7 57.7 %copy-start.2 = (f32[768,256]{1,0:T(8,128)S(1)}, f32[768,256]{1,0:T(8,128)}, u32[]{:S(2)}) copy-start(f32[768,256]{1,0:T(8,128)} %second.1) | copy-start | bytes 2359300
  73.7 59.9 %all-to-all-start.2 = ((bf16[8,272,128]{2,1,0:T(8,128)(2,1)}), bf16[8,272,128]{2,1,0:T(8,128)(2,1)S(1)}, u32[]{:S(2)}, u32[]{:S(2)}) async-start(bf16[8,272,128]{2,1,0:T(8,128)(2,1)} %query_parts.1), calls=%async_computation.2 | async-start | bytes 1114112 | tf_op jit(solution)/shard_map/all_to_all | solution.py:380
  78.0 53.4 %copy-start = (f32[768,256]{1,0:T(8,128)S(1)}, f32[768,256]{1,0:T(8,128)}, u32[]{:S(2)}) copy-start(f32[768,256]{1,0:T(8,128)} %table.3) | copy-start | bytes 2359300
  78.0 53.4 %copy-start.1 = (f32[768,256]{1,0:T(8,128)S(1)}, f32[768,256]{1,0:T(8,128)}, u32[]{:S(2)}) copy-start(f32[768,256]{1,0:T(8,128)} %first.1) | copy-start | bytes 2359300
  78.3 25.2 %collective-permute-start.3 = (bf16[6,32,256]{2,1,0:T(8,128)(2,1)S(1)}, bf16[6,32,256]{2,1,0:T(8,128)(2,1)S(1)}, u32[]{:S(2)}, u32[]{:S(2)}) collective-permute-start(bf16[6,32,256]{2,1,0:T(8,128)(2,1)S(1)} %gather_parts.1), channel_id=1, source_target_pairs={{0,128},{128,0},{256,384},{384,256},{1,129},{129,1},{257,385},{385... | collective-permute-start | bytes 294920 | tf_op jit(solution)/shard_map/ppermute | solution.py:376
  103.5 10.4 %collective-permute-start.4 = (bf16[6,32,256]{2,1,0:T(8,128)(2,1)S(1)}, bf16[6,32,256]{2,1,0:T(8,128)(2,1)S(1)}, u32[]{:S(2)}, u32[]{:S(2)}) collective-permute-start(bf16[6,32,256]{2,1,0:T(8,128)(2,1)S(1)} %add_convert_fusion), channel_id=1, source_target_pairs={{128,256},{256,128},{384,0},{0,384},{129,257},{257,129},{385,1},{1... | collective-permute-start | bytes 294920 | tf_op jit(solution)/shard_map/ppermute | solution.py:378
  114.0 11.8 %collective-permute-start.7 = (f32[6,32,256]{2,1,0:T(8,128)S(1)}, f32[6,32,256]{2,1,0:T(8,128)S(1)}, u32[]{:S(2)}, u32[]{:S(2)}) collective-permute-start(f32[6,32,256]{2,1,0:T(8,128)S(1)} %convert_add_fusion.own), channel_id=1, source_target_pairs={{0,96},{32,0},{64,32},{96,64},{1,97},{33,1},{65,33},{97,65},{2,98}... | collective-permute-start | bytes 589832 | tf_op jit(solution)/shard_map/ppermute | solution.py:391
  117.2 11.2 %collective-permute-start.6 = (f32[6,32,256]{2,1,0:T(8,128)S(1)}, f32[6,32,256]{2,1,0:T(8,128)S(1)}, u32[]{:S(2)}, u32[]{:S(2)}) collective-permute-start(f32[6,32,256]{2,1,0:T(8,128)S(1)} %convert_add_fusion.own), channel_id=1, source_target_pairs={{0,64},{32,96},{64,0},{96,32},{1,65},{33,97},{65,1},{97,33},{2,66}... | collective-permute-start | bytes 589832 | tf_op jit(solution)/shard_map/ppermute | solution.py:391
  120.7 10.7 %collective-permute-start.5 = (f32[6,32,256]{2,1,0:T(8,128)S(1)}, f32[6,32,256]{2,1,0:T(8,128)S(1)}, u32[]{:S(2)}, u32[]{:S(2)}) collective-permute-start(f32[6,32,256]{2,1,0:T(8,128)S(1)} %convert_add_fusion.own), channel_id=1, source_target_pairs={{0,32},{32,64},{64,96},{96,0},{1,33},{33,65},{65,97},{97,1},{2,34}... | collective-permute-start | bytes 589832 | tf_op jit(solution)/shard_map/ppermute | solution.py:391

commit v5 on v4

--- a/solution.py
+++ b/solution.py
@@ -373,10 +373,19 @@
         compiler_params=limit(4),
         name="gather_parts",
     )(item_parts)
-    other = lax.ppermute(part, "zh", [(0, 1), (1, 0), (2, 3), (3, 2)])
-    part = lax.optimization_barrier((part.astype(f32) + other.astype(f32)).astype(bf16))
-    other = lax.ppermute(part, "zh", [(1, 2), (2, 1), (3, 0), (0, 3)])
-    part = part.astype(f32) + other.astype(f32)
+    halves = [part[: BLOCKS_DEV // 2], part[BLOCKS_DEV // 2 :]]
+    inner, outer = [(0, 1), (1, 0), (2, 3), (3, 2)], [(1, 2), (2, 1), (3, 0), (0, 3)]
+    others = []
+    for n, turn in enumerate((inner, outer)):
+        others.append(lax.ppermute(halves[n], "zh", turn))
+    halves = [
+        lax.optimization_barrier((mine.astype(f32) + other.astype(f32)).astype(bf16))
+        for mine, other in zip(halves, others)
+    ]
+    others = []
+    for n, turn in enumerate((outer, inner)):
+        others.append(lax.ppermute(halves[n], "zh", turn))
+    part = jnp.concatenate([mine.astype(f32) + other.astype(f32) for mine, other in zip(halves, others)])
     query_parts = lax.all_to_all(query_parts, QROWS, 0, 0, tiled=True)
     loss, query_grad = pl.pallas_call(
         query_sum_kernel,

time: 136 us -> 139 us (1.022)
  starting transfers between devices: 47.7 us -> 61.7 us
  waiting for transfers between devices: 56.6 us -> 45.5 us
    ppermute x2 -> x4, starting transfers between devices: 12.1 us -> 28 us  [step(): others.append(lax.ppermute(halves[n], 'zh', turn))]
    ppermute x2 -> x4, waiting for transfers between devices: 23.5 us -> 12.3 us  [step(): others.append(lax.ppermute(halves[n], 'zh', turn))]
    ppermute x3, starting transfers between devices: 10 us -> 8.31 us  [step(): lax.ppermute(part, 'y', [(i, (i + k) % NY) for i in range(NY)])]
  transfers between devices with their start and end apart: 11 -> 13, of which waited for: 9 -> 9; matrix products, arithmetic and copies ran while one was open for 0% -> 0% of each run, Pallas kernels for 5% -> 5%
where the time goes in v5:
time: 139 us; the launch traced here: 138 us
  starting transfers between devices  61.7 us (44%)
  waiting for transfers between devices  45.5 us (33%)
  Pallas kernels  17.3 us (12%)
  blocking collectives  11.8 us (8%)
  between operations  1.47 us (1%)
    ppermute x4, starting transfers between devices, step(): others.append(lax.ppermute(halves[n], 'zh', turn))  28 us
    all_to_all x1, waiting for transfers between devices, step(): item_parts = lax.all_to_all(item_parts, ('y', 'x'), 0, 0, tiled=True)  17.2 us
    ppermute x4, waiting for transfers between devices, step(): others.append(lax.ppermute(halves[n], 'zh', turn))  12.3 us
    all_to_all x1, blocking collectives, step(): stats = lax.all_to_all(stats, QROWS, 0, 0, tiled=True)  9.63 us
    all_to_all x1, starting transfers between devices, step(): every_query = lax.all_to_all(query_rows, 'zl', 0, 0, tiled=True)  8.55 us
    ppermute x3, waiting for transfers between devices, step(): lax.ppermute(items, 'x', [(i, (i + k) % NX) for i in range(NX)])  8.49 us
    ppermute x3, starting transfers between devices, step(): lax.ppermute(part, 'y', [(i, (i + k) % NY) for i in range(NY)])  8.31 us
    ppermute x3, starting transfers between devices, step(): lax.ppermute(items, 'x', [(i, (i + k) % NX) for i in range(NX)])  7.75 us
  transfers between devices with their start and end apart: 13, of which 9 were waited for; matrix products, arithmetic and copies ran while one was open for 0% of the time, Pallas kernels for 5%

profile of v5, /device:TPU:64, one launch (start us, length us, event | category | flops | bytes accessed | tf_op | source)
XLA Modules:
  0.0 138.0 jit_solution(14785442056897235926)
XLA Ops:
  1.3 2.0 %pack.1 = (bf16[528,256]{1,0:T(8,128)(2,1)}, bf16[4,144,256]{2,1,0:T(8,128)(2,1)}) custom-call(s32[1,4]{1,0:T(1,128)} %ids.1, s32[1,1]{1,0:T(1,128)S(6)} %copy.13.count, f32[1,4]{1,0:T(1,128)} %logq.1, f32[768,256]{1,0:T(8,128)} %table.3, bf16[1,128,256]{2,1,0:T(8,128)(2,1)} %queries.1, s32[1,128]{1,0:T(1,128)} %targets.1), custom_call_target="tpu_custom_call" | custom-call | tf_op jit(solution)/shard_map/pack/pallas_call | solution.py:311
  3.3 0.0 copy-start.3
  3.3 8.6 %all-to-all-start = ((bf16[4,144,256]{2,1,0:T(8,128)(2,1)}), bf16[4,144,256]{2,1,0:T(8,128)(2,1)S(1)}, u32[]{:S(2)}, u32[]{:S(2)}) async-start(bf16[4,144,256]{2,1,0:T(8,128)(2,1)} %get-tuple-element.20), calls=%async_computation | async-start | bytes 589824 | tf_op jit(solution)/shard_map/all_to_all | solution.py:319
  11.8 1.9 %collective-permute-start.2 = (bf16[528,256]{1,0:T(8,128)(2,1)}, bf16[528,256]{1,0:T(8,128)(2,1)S(1)}, u32[]{:S(2)}, u32[]{:S(2)}) collective-permute-start(bf16[528,256]{1,0:T(8,128)(2,1)} %get-tuple-element.19.own), channel_id=1, source_target_pairs={{0,24},{8,0},{16,8},{24,16},{1,25},{9,1},{17,9},{25,17},{2,26},{10... | collective-permute-start | bytes 811016 | tf_op jit(solution)/shard_map/ppermute | solution.py:322
  13.8 2.6 %collective-permute-start.1 = (bf16[528,256]{1,0:T(8,128)(2,1)}, bf16[528,256]{1,0:T(8,128)(2,1)S(1)}, u32[]{:S(2)}, u32[]{:S(2)}) collective-permute-start(bf16[528,256]{1,0:T(8,128)(2,1)} %get-tuple-element.19.own), channel_id=1, source_target_pairs={{0,16},{8,24},{16,0},{24,8},{1,17},{9,25},{17,1},{25,9},{2,18},{10... | collective-permute-start | bytes 811016 | tf_op jit(solution)/shard_map/ppermute | solution.py:322
  16.3 3.3 %collective-permute-start = (bf16[528,256]{1,0:T(8,128)(2,1)}, bf16[528,256]{1,0:T(8,128)(2,1)S(1)}, u32[]{:S(2)}, u32[]{:S(2)}) collective-permute-start(bf16[528,256]{1,0:T(8,128)(2,1)} %get-tuple-element.19.own), channel_id=1, source_target_pairs={{0,8},{8,16},{16,24},{24,0},{1,9},{9,17},{17,25},{25,1},{2,10},{10... | collective-permute-start | bytes 811016 | tf_op jit(solution)/shard_map/ppermute | solution.py:322
  19.6 0.1 pad_add_fusion.place
  19.7 0.0 all-to-all-done
  19.7 2.2 %all_gather.3.queries = bf16[8,144,256]{2,1,0:T(8,128)(2,1)S(1)} all-gather(bf16[4,144,256]{2,1,0:T(8,128)(2,1)S(1)} %all-to-all-done), channel_id=1, replica_groups=mesh['zh'=4,'y'=4,'x'=4,'zl'=4,'c'=2] {'c'}, dimensions={0}, use_global_device_ids=true | all-gather | bytes 884736 | tf_op jit(solution)/shard_map/all_gather | solution.py:323
  21.9 0.9 collective-permute-done.2.three
  22.8 4.0 %collective-permute-done.1.two = bf16[528,256]{1,0:T(8,128)(2,1)S(1)} collective-permute-done((bf16[528,256]{1,0:T(8,128)(2,1)}, bf16[528,256]{1,0:T(8,128)(2,1)S(1)}, u32[]{:S(2)}, u32[]{:S(2)}) %collective-permute-start.1) | collective-permute-done | bytes 270368 | tf_op jit(solution)/shard_map/ppermute | solution.py:322
  26.7 3.7 %collective-permute-done.one = bf16[528,256]{1,0:T(8,128)(2,1)S(1)} collective-permute-done((bf16[528,256]{1,0:T(8,128)(2,1)}, bf16[528,256]{1,0:T(8,128)(2,1)S(1)}, u32[]{:S(2)}, u32[]{:S(2)}) %collective-permute-start) | collective-permute-done | bytes 270368 | tf_op jit(solution)/shard_map/ppermute | solution.py:322
  30.4 0.0 copy-done.3
  30.4 3.3 %totals.1 = (f32[8,8,128]{2,1,0:T(8,128)S(1)}, bf16[17,128,256]{2,1,0:T(8,128)(2,1)S(1)}, bf16[4,16,256]{2,1,0:T(8,128)(2,1)S(1)}, s32[18]{0:T(128)S(1)}, f32[17]{0:T(128)S(1)}) custom-call(s32[4]{0:T(128)S(1)} %pad_add_fusion.place, bf16[528,256]{1,0:T(8,128)(2,1)S(1)} %copy-done.3, bf16[528,256]{1,0:T(8,128)(2,1)S(1)} %collective-permute-done.one, ...), custom_call_target="tpu_custom_call" | custom-call | tf_op jit(solution)/shard_map/totals/pallas_call | solution.py:326
  33.7 9.6 %all_to_all.20.stats = f32[8,8,128]{2,1,0:T(8,128)S(1)} all-to-all(f32[8,8,128]{2,1,0:T(8,128)S(1)} %get-tuple-element.25), channel_id=1, replica_groups=mesh['zh'=4,'y'=4,'x'=4,'zl'=4,'c'=2] {'c','zl'}, dimensions={0} | all-to-all | bytes 65536 | tf_op jit(solution)/shard_map/all_to_all | solution.py:342
  43.3 4.2 %items.1 = (bf16[16,144,256]{2,1,0:T(8,128)(2,1)}, f32[1,1024]{1,0:T(1,128)S(1)}) custom-call(s32[4]{0:T(128)S(1)} %pad_add_fusion.place, s32[18]{0:T(128)S(1)} %get-tuple-element.21.live, f32[17]{0:T(128)S(1)} %get-tuple-element.22.shifts, bf16[17,128,256]{2,1,0:T(8,128)(2,1)S(1)} %get-tuple-element.23.rows_all, ...), custom_call_target="tpu_custom_call" | custom-call | tf_op jit(solution)/shard_map/items/pallas_call | solution.py:343
  47.5 4.9 %all-to-all-start.3 = ((bf16[16,144,256]{2,1,0:T(8,128)(2,1)}), bf16[16,144,256]{2,1,0:T(8,128)(2,1)S(1)}, u32[]{:S(2)}, u32[]{:S(2)}) async-start(bf16[16,144,256]{2,1,0:T(8,128)(2,1)} %get-tuple-element.29), calls=%async_computation.3 | async-start | bytes 2359296 | tf_op jit(solution)/shard_map/all_to_all | solution.py:356
  52.4 4.1 %query_parts.1 = bf16[8,272,128]{2,1,0:T(8,128)(2,1)} custom-call(s32[18]{0:T(128)S(1)} %get-tuple-element.21.live, f32[17]{0:T(128)S(1)} %get-tuple-element.22.shifts, bf16[17,128,256]{2,1,0:T(8,128)(2,1)S(1)} %get-tuple-element.23.rows_all, bf16[8,144,256]{2,1,0:T(8,128)(2,1)S(1)} %all_gather.3.queries, f32[1,1024]{1,0:T(1,128)S(1)} %get-tuple-element.26.norms), custom_call_target="tpu_custom_call" | custom-call | flops 2147483648 | bytes 6291456 | tf_op jit(solution)/shard_map/query_parts/pallas_call | solution.py:357
  56.5 17.2 %all-to-all-done.3.parts = bf16[16,144,256]{2,1,0:T(8,128)(2,1)S(1)} async-done(((bf16[16,144,256]{2,1,0:T(8,128)(2,1)}), bf16[16,144,256]{2,1,0:T(8,128)(2,1)S(1)}, u32[]{:S(2)}, u32[]{:S(2)}) %all-to-all-start.3) | async-done | bytes 1179680 | tf_op jit(solution)/shard_map/all_to_all | solution.py:356
  73.7 4.2 %all-to-all-start.2 = ((bf16[8,272,128]{2,1,0:T(8,128)(2,1)}), bf16[8,272,128]{2,1,0:T(8,128)(2,1)S(1)}, u32[]{:S(2)}, u32[]{:S(2)}) async-start(bf16[8,272,128]{2,1,0:T(8,128)(2,1)} %query_parts.1), calls=%async_computation.2 | async-start | bytes 1114112 | tf_op jit(solution)/shard_map/all_to_all | solution.py:389
  77.9 0.0 copy-start
  77.9 0.0 copy-start.1
  77.9 0.0 copy-start.2
  77.9 0.2 gather_parts.1
  78.2 9.0 %collective-permute-start.3 = (bf16[3,32,256]{2,1,0:T(8,128)(2,1)S(1)}, bf16[3,32,256]{2,1,0:T(8,128)(2,1)S(1)}, u32[]{:S(2)}, u32[]{:S(2)}) collective-permute-start(bf16[3,32,256]{2,1,0:T(8,128)(2,1)S(1)} %get-tuple-element.35), channel_id=1, source_target_pairs={{0,128},{128,0},{256,384},{384,256},{1,129},{129,1},{257,385},{385... | collective-permute-start | bytes 147464 | tf_op jit(solution)/shard_map/ppermute | solution.py:380
  87.3 6.4 %collective-permute-start.5 = (bf16[3,32,256]{2,1,0:T(8,128)(2,1)S(1)}, bf16[3,32,256]{2,1,0:T(8,128)(2,1)S(1)}, u32[]{:S(2)}, u32[]{:S(2)}) collective-permute-start(bf16[3,32,256]{2,1,0:T(8,128)(2,1)S(1)} %get-tuple-element.36), channel_id=1, source_target_pairs={{128,256},{256,128},{384,0},{0,384},{129,257},{257,129},{385,1},{1... | collective-permute-start | bytes 147464 | tf_op jit(solution)/shard_map/ppermute | solution.py:380
  93.7 8.6 %collective-permute-done.3 = bf16[3,32,256]{2,1,0:T(8,128)(2,1)S(1)} collective-permute-done((bf16[3,32,256]{2,1,0:T(8,128)(2,1)S(1)}, bf16[3,32,256]{2,1,0:T(8,128)(2,1)S(1)}, u32[]{:S(2)}, u32[]{:S(2)}) %collective-permute-start.3) | collective-permute-done | bytes 49184 | tf_op jit(solution)/shard_map/ppermute | solution.py:380
  102.2 0.0 collective-permute-done.5
  102.3 6.4 %collective-permute-start.6 = (bf16[3,32,256]{2,1,0:T(8,128)(2,1)S(1)}, bf16[3,32,256]{2,1,0:T(8,128)(2,1)S(1)}, u32[]{:S(2)}, u32[]{:S(2)}) collective-permute-start(bf16[3,32,256]{2,1,0:T(8,128)(2,1)S(1)} %get-tuple-element.34), channel_id=1, source_target_pairs={{0,128},{128,0},{256,384},{384,256},{1,129},{129,1},{257,385},{385... | collective-permute-start | bytes 147464 | tf_op jit(solution)/shard_map/ppermute | solution.py:387
  108.7 6.1 %collective-permute-start.4 = (bf16[3,32,256]{2,1,0:T(8,128)(2,1)S(1)}, bf16[3,32,256]{2,1,0:T(8,128)(2,1)S(1)}, u32[]{:S(2)}, u32[]{:S(2)}) collective-permute-start(bf16[3,32,256]{2,1,0:T(8,128)(2,1)S(1)} %get-tuple-element.33), channel_id=1, source_target_pairs={{128,256},{256,128},{384,0},{0,384},{129,257},{257,129},{385,1},{1... | collective-permute-start | bytes 147464 | tf_op jit(solution)/shard_map/ppermute | solution.py:387
  114.8 0.0 collective-permute-done.6
  114.9 3.7 %collective-permute-done.4 = bf16[3,32,256]{2,1,0:T(8,128)(2,1)S(1)} collective-permute-done((bf16[3,32,256]{2,1,0:T(8,128)(2,1)S(1)}, bf16[3,32,256]{2,1,0:T(8,128)(2,1)S(1)}, u32[]{:S(2)}, u32[]{:S(2)}) %collective-permute-start.4) | collective-permute-done | bytes 49184 | tf_op jit(solution)/shard_map/ppermute | solution.py:387
  118.6 3.4 %collective-permute-start.9 = (f32[6,32,256]{2,1,0:T(8,128)S(1)}, f32[6,32,256]{2,1,0:T(8,128)S(1)}, u32[]{:S(2)}, u32[]{:S(2)}) collective-permute-start(f32[6,32,256]{2,1,0:T(8,128)S(1)} %pad_maximum_fusion.own), channel_id=1, source_target_pairs={{0,96},{32,0},{64,32},{96,64},{1,97},{33,1},{65,33},{97,65},{2,98}... | collective-permute-start | bytes 589832 | tf_op jit(solution)/shard_map/ppermute | solution.py:400
  122.0 2.3 %collective-permute-start.8 = (f32[6,32,256]{2,1,0:T(8,128)S(1)}, f32[6,32,256]{2,1,0:T(8,128)S(1)}, u32[]{:S(2)}, u32[]{:S(2)}) collective-permute-start(f32[6,32,256]{2,1,0:T(8,128)S(1)} %pad_maximum_fusion.own), channel_id=1, source_target_pairs={{0,64},{32,96},{64,0},{96,32},{1,65},{33,97},{65,1},{97,33},{2,66}... | collective-permute-start | bytes 589832 | tf_op jit(solution)/shard_map/ppermute | solution.py:400
  124.3 2.6 %collective-permute-start.7 = (f32[6,32,256]{2,1,0:T(8,128)S(1)}, f32[6,32,256]{2,1,0:T(8,128)S(1)}, u32[]{:S(2)}, u32[]{:S(2)}) collective-permute-start(f32[6,32,256]{2,1,0:T(8,128)S(1)} %pad_maximum_fusion.own), channel_id=1, source_target_pairs={{0,32},{32,64},{64,96},{96,0},{1,33},{33,65},{65,97},{97,1},{2,34}... | collective-permute-start | bytes 589832 | tf_op jit(solution)/shard_map/ppermute | solution.py:400
  127.0 0.9 collective-permute-done.9.three
  127.9 5.2 %collective-permute-done.8.two = f32[6,32,256]{2,1,0:T(8,128)S(1)} collective-permute-done((f32[6,32,256]{2,1,0:T(8,128)S(1)}, f32[6,32,256]{2,1,0:T(8,128)S(1)}, u32[]{:S(2)}, u32[]{:S(2)}) %collective-permute-start.8) | collective-permute-done | bytes 196640 | tf_op jit(solution)/shard_map/ppermute | solution.py:400
  133.1 1.4 %collective-permute-done.7.one = f32[6,32,256]{2,1,0:T(8,128)S(1)} collective-permute-done((f32[6,32,256]{2,1,0:T(8,128)S(1)}, f32[6,32,256]{2,1,0:T(8,128)S(1)}, u32[]{:S(2)}, u32[]{:S(2)}) %collective-permute-start.7) | collective-permute-done | bytes 196640 | tf_op jit(solution)/shard_map/ppermute | solution.py:400
  134.5 0.0 copy-done
  134.5 0.0 copy-done.1
  134.5 0.0 copy-done.2
  134.5 2.2 %adam.1 = (f32[768,256]{1,0:T(8,128)}, f32[768,256]{1,0:T(8,128)}, f32[768,256]{1,0:T(8,128)}) custom-call(s32[4]{0:T(128)S(1)} %pad_add_fusion.place, f32[6,32,256]{2,1,0:T(8,128)S(1)} %pad_maximum_fusion.own, f32[6,32,256]{2,1,0:T(8,128)S(1)} %collective-permute-done.7.one, f32[6,32,256]{2,1,0:T(8,128)S(1)} %collective-permute-done.8.two, ...), custom_call_target="tpu_custom_call" | custom-call | tf_op jit(solution)/shard_map/adam/pallas_call | solution.py:402
  136.7 0.0 all-to-all-done.2.parts
  136.7 1.3 query_sum.1
  (5 shorter events, 0.1 us)
Async XLA Ops:
  3.3 27.1 %copy-start.3 = (bf16[528,256]{1,0:T(8,128)(2,1)S(1)}, bf16[528,256]{1,0:T(8,128)(2,1)}, u32[]{:S(2)}) copy-start(bf16[528,256]{1,0:T(8,128)(2,1)} %get-tuple-element.19.own) | copy-start | bytes 811012
  3.3 16.4 %all-to-all-start = ((bf16[4,144,256]{2,1,0:T(8,128)(2,1)}), bf16[4,144,256]{2,1,0:T(8,128)(2,1)S(1)}, u32[]{:S(2)}, u32[]{:S(2)}) async-start(bf16[4,144,256]{2,1,0:T(8,128)(2,1)} %get-tuple-element.20), calls=%async_computation | async-start | bytes 589824 | tf_op jit(solution)/shard_map/all_to_all | solution.py:319
  11.8 10.9 %collective-permute-start.2 = (bf16[528,256]{1,0:T(8,128)(2,1)}, bf16[528,256]{1,0:T(8,128)(2,1)S(1)}, u32[]{:S(2)}, u32[]{:S(2)}) collective-permute-start(bf16[528,256]{1,0:T(8,128)(2,1)} %get-tuple-element.19.own), channel_id=1, source_target_pairs={{0,24},{8,0},{16,8},{24,16},{1,25},{9,1},{17,9},{25,17},{2,26},{10... | collective-permute-start | bytes 811016 | tf_op jit(solution)/shard_map/ppermute | solution.py:322
  13.8 13.0 %collective-permute-start.1 = (bf16[528,256]{1,0:T(8,128)(2,1)}, bf16[528,256]{1,0:T(8,128)(2,1)S(1)}, u32[]{:S(2)}, u32[]{:S(2)}) collective-permute-start(bf16[528,256]{1,0:T(8,128)(2,1)} %get-tuple-element.19.own), channel_id=1, source_target_pairs={{0,16},{8,24},{16,0},{24,8},{1,17},{9,25},{17,1},{25,9},{2,18},{10... | collective-permute-start | bytes 811016 | tf_op jit(solution)/shard_map/ppermute | solution.py:322
  16.3 14.1 %collective-permute-start = (bf16[528,256]{1,0:T(8,128)(2,1)}, bf16[528,256]{1,0:T(8,128)(2,1)S(1)}, u32[]{:S(2)}, u32[]{:S(2)}) collective-permute-start(bf16[528,256]{1,0:T(8,128)(2,1)} %get-tuple-element.19.own), channel_id=1, source_target_pairs={{0,8},{8,16},{16,24},{24,0},{1,9},{9,17},{17,25},{25,1},{2,10},{10... | collective-permute-start | bytes 811016 | tf_op jit(solution)/shard_map/ppermute | solution.py:322
  47.5 26.2 %all-to-all-start.3 = ((bf16[16,144,256]{2,1,0:T(8,128)(2,1)}), bf16[16,144,256]{2,1,0:T(8,128)(2,1)S(1)}, u32[]{:S(2)}, u32[]{:S(2)}) async-start(bf16[16,144,256]{2,1,0:T(8,128)(2,1)} %get-tuple-element.29), calls=%async_computation.3 | async-start | bytes 2359296 | tf_op jit(solution)/shard_map/all_to_all | solution.py:356
  73.7 63.0 %all-to-all-start.2 = ((bf16[8,272,128]{2,1,0:T(8,128)(2,1)}), bf16[8,272,128]{2,1,0:T(8,128)(2,1)S(1)}, u32[]{:S(2)}, u32[]{:S(2)}) async-start(bf16[8,272,128]{2,1,0:T(8,128)(2,1)} %query_parts.1), calls=%async_computation.2 | async-start | bytes 1114112 | tf_op jit(solution)/shard_map/all_to_all | solution.py:389
  77.9 56.6 %copy-start = (f32[768,256]{1,0:T(8,128)S(1)}, f32[768,256]{1,0:T(8,128)}, u32[]{:S(2)}) copy-start(f32[768,256]{1,0:T(8,128)} %table.3) | copy-start | bytes 2359300
  77.9 56.6 %copy-start.1 = (f32[768,256]{1,0:T(8,128)S(1)}, f32[768,256]{1,0:T(8,128)}, u32[]{:S(2)}) copy-start(f32[768,256]{1,0:T(8,128)} %first.1) | copy-start | bytes 2359300
  77.9 56.6 %copy-start.2 = (f32[768,256]{1,0:T(8,128)S(1)}, f32[768,256]{1,0:T(8,128)}, u32[]{:S(2)}) copy-start(f32[768,256]{1,0:T(8,128)} %second.1) | copy-start | bytes 2359300
  78.2 24.0 %collective-permute-start.3 = (bf16[3,32,256]{2,1,0:T(8,128)(2,1)S(1)}, bf16[3,32,256]{2,1,0:T(8,128)(2,1)S(1)}, u32[]{:S(2)}, u32[]{:S(2)}) collective-permute-start(bf16[3,32,256]{2,1,0:T(8,128)(2,1)S(1)} %get-tuple-element.35), channel_id=1, source_target_pairs={{0,128},{128,0},{256,384},{384,256},{1,129},{129,1},{257,385},{385... | collective-permute-start | bytes 147464 | tf_op jit(solution)/shard_map/ppermute | solution.py:380
  87.3 15.0 %collective-permute-start.5 = (bf16[3,32,256]{2,1,0:T(8,128)(2,1)S(1)}, bf16[3,32,256]{2,1,0:T(8,128)(2,1)S(1)}, u32[]{:S(2)}, u32[]{:S(2)}) collective-permute-start(bf16[3,32,256]{2,1,0:T(8,128)(2,1)S(1)} %get-tuple-element.36), channel_id=1, source_target_pairs={{128,256},{256,128},{384,0},{0,384},{129,257},{257,129},{385,1},{1... | collective-permute-start | bytes 147464 | tf_op jit(solution)/shard_map/ppermute | solution.py:380
  102.3 12.5 %collective-permute-start.6 = (bf16[3,32,256]{2,1,0:T(8,128)(2,1)S(1)}, bf16[3,32,256]{2,1,0:T(8,128)(2,1)S(1)}, u32[]{:S(2)}, u32[]{:S(2)}) collective-permute-start(bf16[3,32,256]{2,1,0:T(8,128)(2,1)S(1)} %get-tuple-element.34), channel_id=1, source_target_pairs={{0,128},{128,0},{256,384},{384,256},{1,129},{129,1},{257,385},{385... | collective-permute-start | bytes 147464 | tf_op jit(solution)/shard_map/ppermute | solution.py:387
  108.7 9.9 %collective-permute-start.4 = (bf16[3,32,256]{2,1,0:T(8,128)(2,1)S(1)}, bf16[3,32,256]{2,1,0:T(8,128)(2,1)S(1)}, u32[]{:S(2)}, u32[]{:S(2)}) collective-permute-start(bf16[3,32,256]{2,1,0:T(8,128)(2,1)S(1)} %get-tuple-element.33), channel_id=1, source_target_pairs={{128,256},{256,128},{384,0},{0,384},{129,257},{257,129},{385,1},{1... | collective-permute-start | bytes 147464 | tf_op jit(solution)/shard_map/ppermute | solution.py:387
  118.6 9.3 %collective-permute-start.9 = (f32[6,32,256]{2,1,0:T(8,128)S(1)}, f32[6,32,256]{2,1,0:T(8,128)S(1)}, u32[]{:S(2)}, u32[]{:S(2)}) collective-permute-start(f32[6,32,256]{2,1,0:T(8,128)S(1)} %pad_maximum_fusion.own), channel_id=1, source_target_pairs={{0,96},{32,0},{64,32},{96,64},{1,97},{33,1},{65,33},{97,65},{2,98}... | collective-permute-start | bytes 589832 | tf_op jit(solution)/shard_map/ppermute | solution.py:400
  122.0 11.1 %collective-permute-start.8 = (f32[6,32,256]{2,1,0:T(8,128)S(1)}, f32[6,32,256]{2,1,0:T(8,128)S(1)}, u32[]{:S(2)}, u32[]{:S(2)}) collective-permute-start(f32[6,32,256]{2,1,0:T(8,128)S(1)} %pad_maximum_fusion.own), channel_id=1, source_target_pairs={{0,64},{32,96},{64,0},{96,32},{1,65},{33,97},{65,1},{97,33},{2,66}... | collective-permute-start | bytes 589832 | tf_op jit(solution)/shard_map/ppermute | solution.py:400
  124.3 10.1 %collective-permute-start.7 = (f32[6,32,256]{2,1,0:T(8,128)S(1)}, f32[6,32,256]{2,1,0:T(8,128)S(1)}, u32[]{:S(2)}, u32[]{:S(2)}) collective-permute-start(f32[6,32,256]{2,1,0:T(8,128)S(1)} %pad_maximum_fusion.own), channel_id=1, source_target_pairs={{0,32},{32,64},{64,96},{96,0},{1,33},{33,65},{65,97},{97,1},{2,34}... | collective-permute-start | bytes 589832 | tf_op jit(solution)/shard_map/ppermute | solution.py:400

commit v6 on v4

--- a/solution.py
+++ b/solution.py
@@ -17,7 +17,7 @@
 NQ = NZ * NC
 SLOTS = NX * SLOTS_DEV
 PART = BLOCK // NY
-META = 16
+META = 8
 CHUNK = 256
 CHUNKS = NQ * BLOCK // CHUNK
 TOGETHER = 4
@@ -120,20 +120,21 @@
     tops[...] = jnp.full(tops.shape, floor_value, f32)
     sums[...] = jnp.zeros(sums.shape, f32)
 
-    def score(p, carry):
-        rows = rows_all[pl.ds(2 * p, 2)].reshape(2 * BLOCK, D)
+    def score(g, carry):
+        rows = rows_all[pl.ds(g * TOGETHER, TOGETHER)].reshape(TOGETHER * BLOCK, D)
         for b in range(CHUNKS):
             cols = pl.ds(b * CHUNK, CHUNK)
             doubled = pair_products(rows, queries, b)
             top = tops[:, cols]
-            for h in range(2):
-                half = doubled[h * BLOCK : (h + 1) * BLOCK]
-                scores[2 * p + h, :, cols] = half
-                top = jnp.maximum(top, jnp.max(half.reshape(BLOCK // 8, 8, CHUNK), axis=0) - shifts[2 * p + h])
+            for h in range(TOGETHER):
+                i = g * TOGETHER + h
+                block = doubled[h * BLOCK : (h + 1) * BLOCK]
+                scores[i, :, cols] = block
+                top = jnp.maximum(top, jnp.max(block.reshape(BLOCK // 8, 8, CHUNK), axis=0) - shifts[i])
             tops[:, cols] = top
         return carry
 
-    lax.fori_loop(0, pairs, score, 0)
+    lax.fori_loop(0, (number + TOGETHER - 1) // TOGETHER, score, 0)
     top_row = jnp.max(tops[...], axis=0, keepdims=True)
 
     def weigh(p, carry):

time: 136 us -> 134 us (0.985)
  waiting for transfers between devices: 56.6 us -> 53.9 us
  starting transfers between devices: 47.7 us -> 49.3 us
  Pallas kernels: 17.3 us -> 15.9 us
    all_to_all x1, waiting for transfers between devices: 17.2 us -> 15.2 us  [step(): item_parts = lax.all_to_all(item_parts, ('y', 'x'), 0, 0, tiled=True)]
    ppermute x1, starting transfers between devices: 3.08 us -> 4.68 us  [step(): other = lax.ppermute(part, 'zh', [(1, 2), (2, 1), (3, 0), (0, 3)])]
    ppermute x1, waiting for transfers between devices: 16.2 us -> 14.7 us  [step(): other = lax.ppermute(part, 'zh', [(0, 1), (1, 0), (2, 3), (3, 2)])]
where the time goes in v6:
time: 134 us; the launch traced here: 133 us
  waiting for transfers between devices  53.9 us (40%)
  starting transfers between devices  49.3 us (37%)
  Pallas kernels  15.9 us (12%)
  blocking collectives  11.8 us (9%)
  between operations  1.43 us (1%)
    all_to_all x1, waiting for transfers between devices, step(): item_parts = lax.all_to_all(item_parts, ('y', 'x'), 0, 0, tiled=True)  15.2 us
    ppermute x1, waiting for transfers between devices, step(): other = lax.ppermute(part, 'zh', [(0, 1), (1, 0), (2, 3), (3, 2)])  14.7 us
    ppermute x1, starting transfers between devices, step(): other = lax.ppermute(part, 'zh', [(0, 1), (1, 0), (2, 3), (3, 2)])  9.74 us
    all_to_all x1, blocking collectives, step(): stats = lax.all_to_all(stats, QROWS, 0, 0, tiled=True)  9.56 us
    ppermute x3, starting transfers between devices, step(): lax.ppermute(part, 'y', [(i, (i + k) % NY) for i in range(NY)])  8.9 us
    all_to_all x1, starting transfers between devices, step(): every_query = lax.all_to_all(query_rows, 'zl', 0, 0, tiled=True)  8.55 us
    ppermute x3, waiting for transfers between devices, step(): lax.ppermute(items, 'x', [(i, (i + k) % NX) for i in range(NX)])  8.34 us
    ppermute x3, waiting for transfers between devices, step(): lax.ppermute(part, 'y', [(i, (i + k) % NY) for i in range(NY)])  8.19 us
  transfers between devices with their start and end apart: 11, of which 9 were waited for; matrix products, arithmetic and copies ran while one was open for 0% of the time, Pallas kernels for 5%

profile of v6, /device:TPU:64, one launch (start us, length us, event | category | flops | bytes accessed | tf_op | source)
XLA Modules:
  0.0 133.5 jit_solution(6638723561960422235)
XLA Ops:
  1.3 2.0 %pack.1 = (bf16[520,256]{1,0:T(8,128)(2,1)}, bf16[4,136,256]{2,1,0:T(8,128)(2,1)}) custom-call(s32[1,4]{1,0:T(1,128)} %ids.1, s32[1,1]{1,0:T(1,128)S(6)} %copy.13.count, f32[1,4]{1,0:T(1,128)} %logq.1, f32[768,256]{1,0:T(8,128)} %table.3, bf16[1,128,256]{2,1,0:T(8,128)(2,1)} %queries.1, s32[1,128]{1,0:T(1,128)} %targets.1), custom_call_target="tpu_custom_call" | custom-call | tf_op jit(solution)/shard_map/pack/pallas_call | solution.py:312
  3.3 0.0 copy-start.4
  3.3 8.6 %all-to-all-start = ((bf16[4,136,256]{2,1,0:T(8,128)(2,1)}), bf16[4,136,256]{2,1,0:T(8,128)(2,1)S(1)}, u32[]{:S(2)}, u32[]{:S(2)}) async-start(bf16[4,136,256]{2,1,0:T(8,128)(2,1)} %get-tuple-element.20), calls=%async_computation | async-start | bytes 557056 | tf_op jit(solution)/shard_map/all_to_all | solution.py:320
  11.8 1.9 %collective-permute-start.2 = (bf16[520,256]{1,0:T(8,128)(2,1)}, bf16[520,256]{1,0:T(8,128)(2,1)S(1)}, u32[]{:S(2)}, u32[]{:S(2)}) collective-permute-start(bf16[520,256]{1,0:T(8,128)(2,1)} %get-tuple-element.19.own), channel_id=1, source_target_pairs={{0,24},{8,0},{16,8},{24,16},{1,25},{9,1},{17,9},{25,17},{2,26},{10... | collective-permute-start | bytes 798728 | tf_op jit(solution)/shard_map/ppermute | solution.py:323
  13.8 2.6 %collective-permute-start.1 = (bf16[520,256]{1,0:T(8,128)(2,1)}, bf16[520,256]{1,0:T(8,128)(2,1)S(1)}, u32[]{:S(2)}, u32[]{:S(2)}) collective-permute-start(bf16[520,256]{1,0:T(8,128)(2,1)} %get-tuple-element.19.own), channel_id=1, source_target_pairs={{0,16},{8,24},{16,0},{24,8},{1,17},{9,25},{17,1},{25,9},{2,18},{10... | collective-permute-start | bytes 798728 | tf_op jit(solution)/shard_map/ppermute | solution.py:323
  16.3 3.3 %collective-permute-start = (bf16[520,256]{1,0:T(8,128)(2,1)}, bf16[520,256]{1,0:T(8,128)(2,1)S(1)}, u32[]{:S(2)}, u32[]{:S(2)}) collective-permute-start(bf16[520,256]{1,0:T(8,128)(2,1)} %get-tuple-element.19.own), channel_id=1, source_target_pairs={{0,8},{8,16},{16,24},{24,0},{1,9},{9,17},{17,25},{25,1},{2,10},{10... | collective-permute-start | bytes 798728 | tf_op jit(solution)/shard_map/ppermute | solution.py:323
  19.6 0.1 pad_add_fusion.place
  19.7 0.0 all-to-all-done
  19.7 2.2 %all_gather.3.queries = bf16[8,136,256]{2,1,0:T(8,128)(2,1)S(1)} all-gather(bf16[4,136,256]{2,1,0:T(8,128)(2,1)S(1)} %all-to-all-done), channel_id=1, replica_groups=mesh['zh'=4,'y'=4,'x'=4,'zl'=4,'c'=2] {'c'}, dimensions={0}, use_global_device_ids=true | all-gather | bytes 835584 | tf_op jit(solution)/shard_map/all_gather | solution.py:324
  21.9 0.8 collective-permute-done.2.three
  22.7 3.9 %collective-permute-done.1.two = bf16[520,256]{1,0:T(8,128)(2,1)S(1)} collective-permute-done((bf16[520,256]{1,0:T(8,128)(2,1)}, bf16[520,256]{1,0:T(8,128)(2,1)S(1)}, u32[]{:S(2)}, u32[]{:S(2)}) %collective-permute-start.1) | collective-permute-done | bytes 266272 | tf_op jit(solution)/shard_map/ppermute | solution.py:323
  26.6 3.6 %collective-permute-done.one = bf16[520,256]{1,0:T(8,128)(2,1)S(1)} collective-permute-done((bf16[520,256]{1,0:T(8,128)(2,1)}, bf16[520,256]{1,0:T(8,128)(2,1)S(1)}, u32[]{:S(2)}, u32[]{:S(2)}) %collective-permute-start) | collective-permute-done | bytes 266272 | tf_op jit(solution)/shard_map/ppermute | solution.py:323
  30.2 0.0 copy-done.4
  30.2 2.9 %totals.1 = (f32[8,8,128]{2,1,0:T(8,128)S(1)}, bf16[17,128,256]{2,1,0:T(8,128)(2,1)S(1)}, bf16[4,8,256]{2,1,0:T(8,128)(2,1)S(1)}, s32[18]{0:T(128)S(1)}, f32[17]{0:T(128)S(1)}) custom-call(s32[4]{0:T(128)S(1)} %pad_add_fusion.place, bf16[520,256]{1,0:T(8,128)(2,1)S(1)} %copy-done.4, bf16[520,256]{1,0:T(8,128)(2,1)S(1)} %collective-permute-done.one, ...), custom_call_target="tpu_custom_call" | custom-call | tf_op jit(solution)/shard_map/totals/pallas_call | solution.py:327
  33.1 9.6 %all_to_all.20.stats = f32[8,8,128]{2,1,0:T(8,128)S(1)} all-to-all(f32[8,8,128]{2,1,0:T(8,128)S(1)} %get-tuple-element.25), channel_id=1, replica_groups=mesh['zh'=4,'y'=4,'x'=4,'zl'=4,'c'=2] {'c','zl'}, dimensions={0} | all-to-all | bytes 65536 | tf_op jit(solution)/shard_map/all_to_all | solution.py:343
  42.7 3.1 %items.1 = (bf16[16,136,256]{2,1,0:T(8,128)(2,1)S(1)}, f32[1,1024]{1,0:T(1,128)S(1)}) custom-call(s32[4]{0:T(128)S(1)} %pad_add_fusion.place, s32[18]{0:T(128)S(1)} %get-tuple-element.21.live, f32[17]{0:T(128)S(1)} %get-tuple-element.22.shifts, bf16[17,128,256]{2,1,0:T(8,128)(2,1)S(1)} %get-tuple-element.23.rows_all, ...), custom_call_target="tpu_custom_call" | custom-call | tf_op jit(solution)/shard_map/items/pallas_call | solution.py:344
  45.8 0.0 copy-start.1
  45.8 1.0 copy-done.1
  46.8 5.1 %all-to-all-start.3 = ((bf16[16,136,256]{2,1,0:T(8,128)(2,1)}), bf16[16,136,256]{2,1,0:T(8,128)(2,1)S(1)}, u32[]{:S(2)}, u32[]{:S(2)}) async-start(bf16[16,136,256]{2,1,0:T(8,128)(2,1)} %copy-done.1), calls=%async_computation.3 | async-start | bytes 2228224 | tf_op jit(solution)/shard_map/all_to_all | solution.py:357
  51.9 4.1 %query_parts.1 = bf16[8,264,128]{2,1,0:T(8,128)(2,1)} custom-call(s32[18]{0:T(128)S(1)} %get-tuple-element.21.live, f32[17]{0:T(128)S(1)} %get-tuple-element.22.shifts, bf16[17,128,256]{2,1,0:T(8,128)(2,1)S(1)} %get-tuple-element.23.rows_all, bf16[8,136,256]{2,1,0:T(8,128)(2,1)S(1)} %all_gather.3.queries, f32[1,1024]{1,0:T(1,128)S(1)} %get-tuple-element.26.norms), custom_call_target="tpu_custom_call" | custom-call | flops 2147483648 | bytes 6291456 | tf_op jit(solution)/shard_map/query_parts/pallas_call | solution.py:358
  56.0 15.2 %all-to-all-done.3.parts = bf16[16,136,256]{2,1,0:T(8,128)(2,1)S(1)} async-done(((bf16[16,136,256]{2,1,0:T(8,128)(2,1)}), bf16[16,136,256]{2,1,0:T(8,128)(2,1)S(1)}, u32[]{:S(2)}, u32[]{:S(2)}) %all-to-all-start.3) | async-done | bytes 1114144 | tf_op jit(solution)/shard_map/all_to_all | solution.py:357
  71.3 0.0 copy-start.3
  71.3 4.6 %all-to-all-start.2 = ((bf16[8,264,128]{2,1,0:T(8,128)(2,1)}), bf16[8,264,128]{2,1,0:T(8,128)(2,1)S(1)}, u32[]{:S(2)}, u32[]{:S(2)}) async-start(bf16[8,264,128]{2,1,0:T(8,128)(2,1)} %query_parts.1), calls=%async_computation.2 | async-start | bytes 1081344 | tf_op jit(solution)/shard_map/all_to_all | solution.py:381
  75.9 0.0 copy-start
  75.9 0.0 copy-start.2
  75.9 0.2 gather_parts.1
  76.2 9.7 %collective-permute-start.3 = (bf16[6,32,256]{2,1,0:T(8,128)(2,1)S(1)}, bf16[6,32,256]{2,1,0:T(8,128)(2,1)S(1)}, u32[]{:S(2)}, u32[]{:S(2)}) collective-permute-start(bf16[6,32,256]{2,1,0:T(8,128)(2,1)S(1)} %gather_parts.1), channel_id=1, source_target_pairs={{0,128},{128,0},{256,384},{384,256},{1,129},{129,1},{257,385},{385... | collective-permute-start | bytes 294920 | tf_op jit(solution)/shard_map/ppermute | solution.py:377
  85.9 14.7 %collective-permute-done.3 = bf16[6,32,256]{2,1,0:T(8,128)(2,1)S(1)} collective-permute-done((bf16[6,32,256]{2,1,0:T(8,128)(2,1)S(1)}, bf16[6,32,256]{2,1,0:T(8,128)(2,1)S(1)}, u32[]{:S(2)}, u32[]{:S(2)}) %collective-permute-start.3) | collective-permute-done | bytes 98336 | tf_op jit(solution)/shard_map/ppermute | solution.py:377
  100.6 4.7 %collective-permute-start.4 = (bf16[6,32,256]{2,1,0:T(8,128)(2,1)S(1)}, bf16[6,32,256]{2,1,0:T(8,128)(2,1)S(1)}, u32[]{:S(2)}, u32[]{:S(2)}) collective-permute-start(bf16[6,32,256]{2,1,0:T(8,128)(2,1)S(1)} %add_convert_fusion), channel_id=1, source_target_pairs={{128,256},{256,128},{384,0},{0,384},{129,257},{257,129},{385,1},{1... | collective-permute-start | bytes 294920 | tf_op jit(solution)/shard_map/ppermute | solution.py:379
  105.3 7.5 %collective-permute-done.4 = bf16[6,32,256]{2,1,0:T(8,128)(2,1)S(1)} collective-permute-done((bf16[6,32,256]{2,1,0:T(8,128)(2,1)S(1)}, bf16[6,32,256]{2,1,0:T(8,128)(2,1)S(1)}, u32[]{:S(2)}, u32[]{:S(2)}) %collective-permute-start.4) | collective-permute-done | bytes 98336 | tf_op jit(solution)/shard_map/ppermute | solution.py:379
  112.8 3.4 %collective-permute-start.7 = (f32[6,32,256]{2,1,0:T(8,128)S(1)}, f32[6,32,256]{2,1,0:T(8,128)S(1)}, u32[]{:S(2)}, u32[]{:S(2)}) collective-permute-start(f32[6,32,256]{2,1,0:T(8,128)S(1)} %convert_add_fusion.own), channel_id=1, source_target_pairs={{0,96},{32,0},{64,32},{96,64},{1,97},{33,1},{65,33},{97,65},{2,98}... | collective-permute-start | bytes 589832 | tf_op jit(solution)/shard_map/ppermute | solution.py:392
  116.2 2.6 %collective-permute-start.6 = (f32[6,32,256]{2,1,0:T(8,128)S(1)}, f32[6,32,256]{2,1,0:T(8,128)S(1)}, u32[]{:S(2)}, u32[]{:S(2)}) collective-permute-start(f32[6,32,256]{2,1,0:T(8,128)S(1)} %convert_add_fusion.own), channel_id=1, source_target_pairs={{0,64},{32,96},{64,0},{96,32},{1,65},{33,97},{65,1},{97,33},{2,66}... | collective-permute-start | bytes 589832 | tf_op jit(solution)/shard_map/ppermute | solution.py:392
  118.8 3.0 %collective-permute-start.5 = (f32[6,32,256]{2,1,0:T(8,128)S(1)}, f32[6,32,256]{2,1,0:T(8,128)S(1)}, u32[]{:S(2)}, u32[]{:S(2)}) collective-permute-start(f32[6,32,256]{2,1,0:T(8,128)S(1)} %convert_add_fusion.own), channel_id=1, source_target_pairs={{0,32},{32,64},{64,96},{96,0},{1,33},{33,65},{65,97},{97,1},{2,34}... | collective-permute-start | bytes 589832 | tf_op jit(solution)/shard_map/ppermute | solution.py:392
  121.7 0.4 collective-permute-done.7.three
  122.1 5.1 %collective-permute-done.6.two = f32[6,32,256]{2,1,0:T(8,128)S(1)} collective-permute-done((f32[6,32,256]{2,1,0:T(8,128)S(1)}, f32[6,32,256]{2,1,0:T(8,128)S(1)}, u32[]{:S(2)}, u32[]{:S(2)}) %collective-permute-start.6) | collective-permute-done | bytes 196640 | tf_op jit(solution)/shard_map/ppermute | solution.py:392
  127.2 2.7 %collective-permute-done.5.one = f32[6,32,256]{2,1,0:T(8,128)S(1)} collective-permute-done((f32[6,32,256]{2,1,0:T(8,128)S(1)}, f32[6,32,256]{2,1,0:T(8,128)S(1)}, u32[]{:S(2)}, u32[]{:S(2)}) %collective-permute-start.5) | collective-permute-done | bytes 196640 | tf_op jit(solution)/shard_map/ppermute | solution.py:392
  129.9 0.0 copy-done.3
  129.9 0.0 copy-done
  129.9 0.0 copy-done.2
  129.9 2.2 %adam.1 = (f32[768,256]{1,0:T(8,128)}, f32[768,256]{1,0:T(8,128)}, f32[768,256]{1,0:T(8,128)}) custom-call(s32[4]{0:T(128)S(1)} %pad_add_fusion.place, f32[6,32,256]{2,1,0:T(8,128)S(1)} %convert_add_fusion.own, f32[6,32,256]{2,1,0:T(8,128)S(1)} %collective-permute-done.5.one, f32[6,32,256]{2,1,0:T(8,128)S(1)} %collective-permute-done.6.two, ...), custom_call_target="tpu_custom_call" | custom-call | tf_op jit(solution)/shard_map/adam/pallas_call | solution.py:394
  132.1 0.0 all-to-all-done.2.parts
  132.1 1.3 %query_sum.1 = (f32[1,128]{1,0:T(1,128)}, f32[1,128,256]{2,1,0:T(8,128)}) custom-call(s32[4]{0:T(128)S(1)} %pad_add_fusion.place, f32[1,1024]{1,0:T(1,128)S(1)} %get-tuple-element.26.norms, bf16[8,264,128]{2,1,0:T(8,128)(2,1)S(1)} %all-to-all-done.2.parts), custom_call_target="tpu_custom_call" | custom-call | tf_op jit(solution)/shard_map/query_sum/pallas_call | solution.py:382
  (2 shorter events, 0.1 us)
Async XLA Ops:
  3.3 27.0 %copy-start.4 = (bf16[520,256]{1,0:T(8,128)(2,1)S(1)}, bf16[520,256]{1,0:T(8,128)(2,1)}, u32[]{:S(2)}) copy-start(bf16[520,256]{1,0:T(8,128)(2,1)} %get-tuple-element.19.own) | copy-start | bytes 798724
  3.3 16.4 %all-to-all-start = ((bf16[4,136,256]{2,1,0:T(8,128)(2,1)}), bf16[4,136,256]{2,1,0:T(8,128)(2,1)S(1)}, u32[]{:S(2)}, u32[]{:S(2)}) async-start(bf16[4,136,256]{2,1,0:T(8,128)(2,1)} %get-tuple-element.20), calls=%async_computation | async-start | bytes 557056 | tf_op jit(solution)/shard_map/all_to_all | solution.py:320
  11.8 10.8 %collective-permute-start.2 = (bf16[520,256]{1,0:T(8,128)(2,1)}, bf16[520,256]{1,0:T(8,128)(2,1)S(1)}, u32[]{:S(2)}, u32[]{:S(2)}) collective-permute-start(bf16[520,256]{1,0:T(8,128)(2,1)} %get-tuple-element.19.own), channel_id=1, source_target_pairs={{0,24},{8,0},{16,8},{24,16},{1,25},{9,1},{17,9},{25,17},{2,26},{10... | collective-permute-start | bytes 798728 | tf_op jit(solution)/shard_map/ppermute | solution.py:323
  13.8 12.9 %collective-permute-start.1 = (bf16[520,256]{1,0:T(8,128)(2,1)}, bf16[520,256]{1,0:T(8,128)(2,1)S(1)}, u32[]{:S(2)}, u32[]{:S(2)}) collective-permute-start(bf16[520,256]{1,0:T(8,128)(2,1)} %get-tuple-element.19.own), channel_id=1, source_target_pairs={{0,16},{8,24},{16,0},{24,8},{1,17},{9,25},{17,1},{25,9},{2,18},{10... | collective-permute-start | bytes 798728 | tf_op jit(solution)/shard_map/ppermute | solution.py:323
  16.3 13.9 %collective-permute-start = (bf16[520,256]{1,0:T(8,128)(2,1)}, bf16[520,256]{1,0:T(8,128)(2,1)S(1)}, u32[]{:S(2)}, u32[]{:S(2)}) collective-permute-start(bf16[520,256]{1,0:T(8,128)(2,1)} %get-tuple-element.19.own), channel_id=1, source_target_pairs={{0,8},{8,16},{16,24},{24,0},{1,9},{9,17},{17,25},{25,1},{2,10},{10... | collective-permute-start | bytes 798728 | tf_op jit(solution)/shard_map/ppermute | solution.py:323
  45.8 1.0 copy-start.1
  46.8 24.5 %all-to-all-start.3 = ((bf16[16,136,256]{2,1,0:T(8,128)(2,1)}), bf16[16,136,256]{2,1,0:T(8,128)(2,1)S(1)}, u32[]{:S(2)}, u32[]{:S(2)}) async-start(bf16[16,136,256]{2,1,0:T(8,128)(2,1)} %copy-done.1), calls=%async_computation.3 | async-start | bytes 2228224 | tf_op jit(solution)/shard_map/all_to_all | solution.py:357
  71.3 58.6 %copy-start.3 = (f32[768,256]{1,0:T(8,128)S(1)}, f32[768,256]{1,0:T(8,128)}, u32[]{:S(2)}) copy-start(f32[768,256]{1,0:T(8,128)} %second.1) | copy-start | bytes 2359300
  71.3 60.8 %all-to-all-start.2 = ((bf16[8,264,128]{2,1,0:T(8,128)(2,1)}), bf16[8,264,128]{2,1,0:T(8,128)(2,1)S(1)}, u32[]{:S(2)}, u32[]{:S(2)}) async-start(bf16[8,264,128]{2,1,0:T(8,128)(2,1)} %query_parts.1), calls=%async_computation.2 | async-start | bytes 1081344 | tf_op jit(solution)/shard_map/all_to_all | solution.py:381
  75.9 54.0 %copy-start = (f32[768,256]{1,0:T(8,128)S(1)}, f32[768,256]{1,0:T(8,128)}, u32[]{:S(2)}) copy-start(f32[768,256]{1,0:T(8,128)} %table.3) | copy-start | bytes 2359300
  75.9 54.0 %copy-start.2 = (f32[768,256]{1,0:T(8,128)S(1)}, f32[768,256]{1,0:T(8,128)}, u32[]{:S(2)}) copy-start(f32[768,256]{1,0:T(8,128)} %first.1) | copy-start | bytes 2359300
  76.2 24.4 %collective-permute-start.3 = (bf16[6,32,256]{2,1,0:T(8,128)(2,1)S(1)}, bf16[6,32,256]{2,1,0:T(8,128)(2,1)S(1)}, u32[]{:S(2)}, u32[]{:S(2)}) collective-permute-start(bf16[6,32,256]{2,1,0:T(8,128)(2,1)S(1)} %gather_parts.1), channel_id=1, source_target_pairs={{0,128},{128,0},{256,384},{384,256},{1,129},{129,1},{257,385},{385... | collective-permute-start | bytes 294920 | tf_op jit(solution)/shard_map/ppermute | solution.py:377
  100.6 12.1 %collective-permute-start.4 = (bf16[6,32,256]{2,1,0:T(8,128)(2,1)S(1)}, bf16[6,32,256]{2,1,0:T(8,128)(2,1)S(1)}, u32[]{:S(2)}, u32[]{:S(2)}) collective-permute-start(bf16[6,32,256]{2,1,0:T(8,128)(2,1)S(1)} %add_convert_fusion), channel_id=1, source_target_pairs={{128,256},{256,128},{384,0},{0,384},{129,257},{257,129},{385,1},{1... | collective-permute-start | bytes 294920 | tf_op jit(solution)/shard_map/ppermute | solution.py:379
  112.8 9.3 %collective-permute-start.7 = (f32[6,32,256]{2,1,0:T(8,128)S(1)}, f32[6,32,256]{2,1,0:T(8,128)S(1)}, u32[]{:S(2)}, u32[]{:S(2)}) collective-permute-start(f32[6,32,256]{2,1,0:T(8,128)S(1)} %convert_add_fusion.own), channel_id=1, source_target_pairs={{0,96},{32,0},{64,32},{96,64},{1,97},{33,1},{65,33},{97,65},{2,98}... | collective-permute-start | bytes 589832 | tf_op jit(solution)/shard_map/ppermute | solution.py:392
  116.2 11.1 %collective-permute-start.6 = (f32[6,32,256]{2,1,0:T(8,128)S(1)}, f32[6,32,256]{2,1,0:T(8,128)S(1)}, u32[]{:S(2)}, u32[]{:S(2)}) collective-permute-start(f32[6,32,256]{2,1,0:T(8,128)S(1)} %convert_add_fusion.own), channel_id=1, source_target_pairs={{0,64},{32,96},{64,0},{96,32},{1,65},{33,97},{65,1},{97,33},{2,66}... | collective-permute-start | bytes 589832 | tf_op jit(solution)/shard_map/ppermute | solution.py:392
  118.8 11.2 %collective-permute-start.5 = (f32[6,32,256]{2,1,0:T(8,128)S(1)}, f32[6,32,256]{2,1,0:T(8,128)S(1)}, u32[]{:S(2)}, u32[]{:S(2)}) collective-permute-start(f32[6,32,256]{2,1,0:T(8,128)S(1)} %convert_add_fusion.own), channel_id=1, source_target_pairs={{0,32},{32,64},{64,96},{96,0},{1,33},{33,65},{65,97},{97,1},{2,34}... | collective-permute-start | bytes 589832 | tf_op jit(solution)/shard_map/ppermute | solution.py:392

commit v7 on v6

--- a/solution.py
+++ b/solution.py
@@ -374,9 +374,12 @@
         compiler_params=limit(4),
         name="gather_parts",
     )(item_parts)
-    other = lax.ppermute(part, "zh", [(0, 1), (1, 0), (2, 3), (3, 2)])
+    inner, outer = (1, 0, 3, 2), (3, 2, 1, 0)
+    first = [(z * NC + c, (inner, outer)[c][z] * NC + c) for z in range(4) for c in range(NC)]
+    second = [(z * NC + c, (outer, inner)[c][z] * NC + c) for z in range(4) for c in range(NC)]
+    other = lax.ppermute(part, ("zh", "c"), first)
     part = lax.optimization_barrier((part.astype(f32) + other.astype(f32)).astype(bf16))
-    other = lax.ppermute(part, "zh", [(1, 2), (2, 1), (3, 0), (0, 3)])
+    other = lax.ppermute(part, ("zh", "c"), second)
     part = part.astype(f32) + other.astype(f32)
     query_parts = lax.all_to_all(query_parts, QROWS, 0, 0, tiled=True)
     loss, query_grad = pl.pallas_call(

time: 134 us -> 134 us (level)
  the two profiles are of different devices: /device:TPU:64 before, /device:TPU:33 now
where the time goes in v7:
time: 134 us
  waiting for transfers between devices  55.1 us (41%)
  starting transfers between devices  45.2 us (34%)
  blocking collectives  15.8 us (12%)
  Pallas kernels  15.1 us (11%)
  between operations  1.43 us (1%)
    all_to_all x1, waiting for transfers between devices, step(): item_parts = lax.all_to_all(item_parts, ('y', 'x'), 0, 0, tiled=True)  15.5 us
    ppermute x1, waiting for transfers between devices, step(): other = lax.ppermute(part, ('zh', 'c'), first)  14.7 us
    ppermute x1, starting transfers between devices, step(): other = lax.ppermute(part, ('zh', 'c'), first)  12 us
    all_to_all x1, blocking collectives, step(): stats = lax.all_to_all(stats, QROWS, 0, 0, tiled=True)  11.5 us
    ppermute x3, waiting for transfers between devices, step(): lax.ppermute(part, 'y', [(i, (i + k) % NY) for i in range(NY)])  10 us
    ppermute x3, starting transfers between devices, step(): lax.ppermute(items, 'x', [(i, (i + k) % NX) for i in range(NX)])  9.32 us
    ppermute x3, waiting for transfers between devices, step(): lax.ppermute(items, 'x', [(i, (i + k) % NX) for i in range(NX)])  7.53 us
    ppermute x1, waiting for transfers between devices, step(): other = lax.ppermute(part, ('zh', 'c'), second)  7.34 us
  transfers between devices with their start and end apart: 11, of which 8 were waited for; matrix products, arithmetic and copies ran while one was open for 0% of the time, Pallas kernels for 5%

profile of v7, /device:TPU:33, one launch (start us, length us, event | category | flops | bytes accessed | tf_op | source)
XLA Modules:
  0.0 133.8 jit_solution(7848497556595080203)
XLA Ops:
  1.3 2.0 %pack.1 = (bf16[520,256]{1,0:T(8,128)(2,1)}, bf16[4,136,256]{2,1,0:T(8,128)(2,1)}) custom-call(s32[1,4]{1,0:T(1,128)} %ids.1, s32[1,1]{1,0:T(1,128)S(6)} %copy.13.count, f32[1,4]{1,0:T(1,128)} %logq.1, f32[768,256]{1,0:T(8,128)} %table.3, bf16[1,128,256]{2,1,0:T(8,128)(2,1)} %queries.1, s32[1,128]{1,0:T(1,128)} %targets.1), custom_call_target="tpu_custom_call" | custom-call | tf_op jit(solution)/shard_map/pack/pallas_call | solution.py:312
  3.3 0.0 copy-start.4
  3.3 5.6 %all-to-all-start = ((bf16[4,136,256]{2,1,0:T(8,128)(2,1)}), bf16[4,136,256]{2,1,0:T(8,128)(2,1)S(1)}, u32[]{:S(2)}, u32[]{:S(2)}) async-start(bf16[4,136,256]{2,1,0:T(8,128)(2,1)} %get-tuple-element.20), calls=%async_computation | async-start | bytes 557056 | tf_op jit(solution)/shard_map/all_to_all | solution.py:320
  8.9 4.4 %collective-permute-start.2 = (bf16[520,256]{1,0:T(8,128)(2,1)}, bf16[520,256]{1,0:T(8,128)(2,1)S(1)}, u32[]{:S(2)}, u32[]{:S(2)}) collective-permute-start(bf16[520,256]{1,0:T(8,128)(2,1)} %get-tuple-element.19.own), channel_id=1, source_target_pairs={{0,24},{8,0},{16,8},{24,16},{1,25},{9,1},{17,9},{25,17},{2,26},{10... | collective-permute-start | bytes 798728 | tf_op jit(solution)/shard_map/ppermute | solution.py:323
  13.2 2.4 %collective-permute-start.1 = (bf16[520,256]{1,0:T(8,128)(2,1)}, bf16[520,256]{1,0:T(8,128)(2,1)S(1)}, u32[]{:S(2)}, u32[]{:S(2)}) collective-permute-start(bf16[520,256]{1,0:T(8,128)(2,1)} %get-tuple-element.19.own), channel_id=1, source_target_pairs={{0,16},{8,24},{16,0},{24,8},{1,17},{9,25},{17,1},{25,9},{2,18},{10... | collective-permute-start | bytes 798728 | tf_op jit(solution)/shard_map/ppermute | solution.py:323
  15.7 2.5 %collective-permute-start = (bf16[520,256]{1,0:T(8,128)(2,1)}, bf16[520,256]{1,0:T(8,128)(2,1)S(1)}, u32[]{:S(2)}, u32[]{:S(2)}) collective-permute-start(bf16[520,256]{1,0:T(8,128)(2,1)} %get-tuple-element.19.own), channel_id=1, source_target_pairs={{0,8},{8,16},{16,24},{24,0},{1,9},{9,17},{17,25},{25,1},{2,10},{10... | collective-permute-start | bytes 798728 | tf_op jit(solution)/shard_map/ppermute | solution.py:323
  18.2 0.1 pad_add_fusion.place
  18.3 0.0 all-to-all-done
  18.3 4.4 %all_gather.3.queries = bf16[8,136,256]{2,1,0:T(8,128)(2,1)S(1)} all-gather(bf16[4,136,256]{2,1,0:T(8,128)(2,1)S(1)} %all-to-all-done), channel_id=1, replica_groups=mesh['zh'=4,'y'=4,'x'=4,'zl'=4,'c'=2] {'c'}, dimensions={0}, use_global_device_ids=true | all-gather | bytes 835584 | tf_op jit(solution)/shard_map/all_gather | solution.py:324
  22.6 0.0 collective-permute-done.2.three
  22.7 0.5 collective-permute-done.1.two
  23.2 7.0 %collective-permute-done.one = bf16[520,256]{1,0:T(8,128)(2,1)S(1)} collective-permute-done((bf16[520,256]{1,0:T(8,128)(2,1)}, bf16[520,256]{1,0:T(8,128)(2,1)S(1)}, u32[]{:S(2)}, u32[]{:S(2)}) %collective-permute-start) | collective-permute-done | bytes 266272 | tf_op jit(solution)/shard_map/ppermute | solution.py:323
  30.2 0.0 copy-done.4
  30.2 2.8 %totals.1 = (f32[8,8,128]{2,1,0:T(8,128)S(1)}, bf16[17,128,256]{2,1,0:T(8,128)(2,1)S(1)}, bf16[4,8,256]{2,1,0:T(8,128)(2,1)S(1)}, s32[18]{0:T(128)S(1)}, f32[17]{0:T(128)S(1)}) custom-call(s32[4]{0:T(128)S(1)} %pad_add_fusion.place, bf16[520,256]{1,0:T(8,128)(2,1)S(1)} %copy-done.4, bf16[520,256]{1,0:T(8,128)(2,1)S(1)} %collective-permute-done.one, ...), custom_call_target="tpu_custom_call" | custom-call | tf_op jit(solution)/shard_map/totals/pallas_call | solution.py:327
  32.9 11.5 %all_to_all.20.stats = f32[8,8,128]{2,1,0:T(8,128)S(1)} all-to-all(f32[8,8,128]{2,1,0:T(8,128)S(1)} %get-tuple-element.25), channel_id=1, replica_groups=mesh['zh'=4,'y'=4,'x'=4,'zl'=4,'c'=2] {'c','zl'}, dimensions={0} | all-to-all | bytes 65536 | tf_op jit(solution)/shard_map/all_to_all | solution.py:343
  44.4 2.5 %items.1 = (bf16[16,136,256]{2,1,0:T(8,128)(2,1)S(1)}, f32[1,1024]{1,0:T(1,128)S(1)}) custom-call(s32[4]{0:T(128)S(1)} %pad_add_fusion.place, s32[18]{0:T(128)S(1)} %get-tuple-element.21.live, f32[17]{0:T(128)S(1)} %get-tuple-element.22.shifts, bf16[17,128,256]{2,1,0:T(8,128)(2,1)S(1)} %get-tuple-element.23.rows_all, ...), custom_call_target="tpu_custom_call" | custom-call | tf_op jit(solution)/shard_map/items/pallas_call | solution.py:344
  46.9 0.0 copy-start.1
  46.9 1.0 copy-done.1
  47.9 5.1 %all-to-all-start.3 = ((bf16[16,136,256]{2,1,0:T(8,128)(2,1)}), bf16[16,136,256]{2,1,0:T(8,128)(2,1)S(1)}, u32[]{:S(2)}, u32[]{:S(2)}) async-start(bf16[16,136,256]{2,1,0:T(8,128)(2,1)} %copy-done.1), calls=%async_computation.3 | async-start | bytes 2228224 | tf_op jit(solution)/shard_map/all_to_all | solution.py:357
  53.1 4.1 %query_parts.1 = bf16[8,264,128]{2,1,0:T(8,128)(2,1)} custom-call(s32[18]{0:T(128)S(1)} %get-tuple-element.21.live, f32[17]{0:T(128)S(1)} %get-tuple-element.22.shifts, bf16[17,128,256]{2,1,0:T(8,128)(2,1)S(1)} %get-tuple-element.23.rows_all, bf16[8,136,256]{2,1,0:T(8,128)(2,1)S(1)} %all_gather.3.queries, f32[1,1024]{1,0:T(1,128)S(1)} %get-tuple-element.26.norms), custom_call_target="tpu_custom_call" | custom-call | flops 2147483648 | bytes 6291456 | tf_op jit(solution)/shard_map/query_parts/pallas_call | solution.py:358
  57.2 15.5 %all-to-all-done.3.parts = bf16[16,136,256]{2,1,0:T(8,128)(2,1)S(1)} async-done(((bf16[16,136,256]{2,1,0:T(8,128)(2,1)}), bf16[16,136,256]{2,1,0:T(8,128)(2,1)S(1)}, u32[]{:S(2)}, u32[]{:S(2)}) %all-to-all-start.3) | async-done | bytes 1114144 | tf_op jit(solution)/shard_map/all_to_all | solution.py:357
  72.7 0.0 copy-start.3
  72.7 3.9 %all-to-all-start.2 = ((bf16[8,264,128]{2,1,0:T(8,128)(2,1)}), bf16[8,264,128]{2,1,0:T(8,128)(2,1)S(1)}, u32[]{:S(2)}, u32[]{:S(2)}) async-start(bf16[8,264,128]{2,1,0:T(8,128)(2,1)} %query_parts.1), calls=%async_computation.2 | async-start | bytes 1081344 | tf_op jit(solution)/shard_map/all_to_all | solution.py:384
  76.7 0.0 copy-start
  76.7 0.0 copy-start.2
  76.7 0.2 gather_parts.1
  76.9 12.0 %collective-permute-start.3 = (bf16[6,32,256]{2,1,0:T(8,128)(2,1)S(1)}, bf16[6,32,256]{2,1,0:T(8,128)(2,1)S(1)}, u32[]{:S(2)}, u32[]{:S(2)}) collective-permute-start(bf16[6,32,256]{2,1,0:T(8,128)(2,1)S(1)} %gather_parts.1), channel_id=1, source_target_pairs={{0,128},{1,385},{128,0},{129,257},{256,384},{257,129},{384,256},{3... | collective-permute-start | bytes 294920 | tf_op jit(solution)/shard_map/ppermute | solution.py:380
  88.9 14.7 %collective-permute-done.3 = bf16[6,32,256]{2,1,0:T(8,128)(2,1)S(1)} collective-permute-done((bf16[6,32,256]{2,1,0:T(8,128)(2,1)S(1)}, bf16[6,32,256]{2,1,0:T(8,128)(2,1)S(1)}, u32[]{:S(2)}, u32[]{:S(2)}) %collective-permute-start.3) | collective-permute-done | bytes 98336 | tf_op jit(solution)/shard_map/ppermute | solution.py:380
  103.6 1.9 %collective-permute-start.4 = (bf16[6,32,256]{2,1,0:T(8,128)(2,1)S(1)}, bf16[6,32,256]{2,1,0:T(8,128)(2,1)S(1)}, u32[]{:S(2)}, u32[]{:S(2)}) collective-permute-start(bf16[6,32,256]{2,1,0:T(8,128)(2,1)S(1)} %add_convert_fusion), channel_id=1, source_target_pairs={{0,384},{1,129},{128,256},{129,1},{256,128},{257,385},{384,0},{385... | collective-permute-start | bytes 294920 | tf_op jit(solution)/shard_map/ppermute | solution.py:382
  105.6 7.3 %collective-permute-done.4 = bf16[6,32,256]{2,1,0:T(8,128)(2,1)S(1)} collective-permute-done((bf16[6,32,256]{2,1,0:T(8,128)(2,1)S(1)}, bf16[6,32,256]{2,1,0:T(8,128)(2,1)S(1)}, u32[]{:S(2)}, u32[]{:S(2)}) %collective-permute-start.4) | collective-permute-done | bytes 98336 | tf_op jit(solution)/shard_map/ppermute | solution.py:382
  112.9 2.8 %collective-permute-start.7 = (f32[6,32,256]{2,1,0:T(8,128)S(1)}, f32[6,32,256]{2,1,0:T(8,128)S(1)}, u32[]{:S(2)}, u32[]{:S(2)}) collective-permute-start(f32[6,32,256]{2,1,0:T(8,128)S(1)} %convert_add_fusion.own), channel_id=1, source_target_pairs={{0,96},{32,0},{64,32},{96,64},{1,97},{33,1},{65,33},{97,65},{2,98}... | collective-permute-start | bytes 589832 | tf_op jit(solution)/shard_map/ppermute | solution.py:395
  115.8 2.5 %collective-permute-start.6 = (f32[6,32,256]{2,1,0:T(8,128)S(1)}, f32[6,32,256]{2,1,0:T(8,128)S(1)}, u32[]{:S(2)}, u32[]{:S(2)}) collective-permute-start(f32[6,32,256]{2,1,0:T(8,128)S(1)} %convert_add_fusion.own), channel_id=1, source_target_pairs={{0,64},{32,96},{64,0},{96,32},{1,65},{33,97},{65,1},{97,33},{2,66}... | collective-permute-start | bytes 589832 | tf_op jit(solution)/shard_map/ppermute | solution.py:395
  118.2 2.0 %collective-permute-start.5 = (f32[6,32,256]{2,1,0:T(8,128)S(1)}, f32[6,32,256]{2,1,0:T(8,128)S(1)}, u32[]{:S(2)}, u32[]{:S(2)}) collective-permute-start(f32[6,32,256]{2,1,0:T(8,128)S(1)} %convert_add_fusion.own), channel_id=1, source_target_pairs={{0,32},{32,64},{64,96},{96,0},{1,33},{33,65},{65,97},{97,1},{2,34}... | collective-permute-start | bytes 589832 | tf_op jit(solution)/shard_map/ppermute | solution.py:395
  120.3 1.2 collective-permute-done.7.three
  121.4 4.6 %collective-permute-done.6.two = f32[6,32,256]{2,1,0:T(8,128)S(1)} collective-permute-done((f32[6,32,256]{2,1,0:T(8,128)S(1)}, f32[6,32,256]{2,1,0:T(8,128)S(1)}, u32[]{:S(2)}, u32[]{:S(2)}) %collective-permute-start.6) | collective-permute-done | bytes 196640 | tf_op jit(solution)/shard_map/ppermute | solution.py:395
  126.0 4.2 %collective-permute-done.5.one = f32[6,32,256]{2,1,0:T(8,128)S(1)} collective-permute-done((f32[6,32,256]{2,1,0:T(8,128)S(1)}, f32[6,32,256]{2,1,0:T(8,128)S(1)}, u32[]{:S(2)}, u32[]{:S(2)}) %collective-permute-start.5) | collective-permute-done | bytes 196640 | tf_op jit(solution)/shard_map/ppermute | solution.py:395
  130.3 0.0 copy-done.3
  130.3 0.0 copy-done
  130.3 0.0 copy-done.2
  130.3 2.2 %adam.1 = (f32[768,256]{1,0:T(8,128)}, f32[768,256]{1,0:T(8,128)}, f32[768,256]{1,0:T(8,128)}) custom-call(s32[4]{0:T(128)S(1)} %pad_add_fusion.place, f32[6,32,256]{2,1,0:T(8,128)S(1)} %convert_add_fusion.own, f32[6,32,256]{2,1,0:T(8,128)S(1)} %collective-permute-done.5.one, f32[6,32,256]{2,1,0:T(8,128)S(1)} %collective-permute-done.6.two, ...), custom_call_target="tpu_custom_call" | custom-call | tf_op jit(solution)/shard_map/adam/pallas_call | solution.py:397
  132.5 0.0 all-to-all-done.2.parts
  132.5 1.3 query_sum.1
  (2 shorter events, 0.1 us)
Async XLA Ops:
  3.3 26.9 %copy-start.4 = (bf16[520,256]{1,0:T(8,128)(2,1)S(1)}, bf16[520,256]{1,0:T(8,128)(2,1)}, u32[]{:S(2)}) copy-start(bf16[520,256]{1,0:T(8,128)(2,1)} %get-tuple-element.19.own) | copy-start | bytes 798724
  3.3 15.0 %all-to-all-start = ((bf16[4,136,256]{2,1,0:T(8,128)(2,1)}), bf16[4,136,256]{2,1,0:T(8,128)(2,1)S(1)}, u32[]{:S(2)}, u32[]{:S(2)}) async-start(bf16[4,136,256]{2,1,0:T(8,128)(2,1)} %get-tuple-element.20), calls=%async_computation | async-start | bytes 557056 | tf_op jit(solution)/shard_map/all_to_all | solution.py:320
  8.9 13.8 %collective-permute-start.2 = (bf16[520,256]{1,0:T(8,128)(2,1)}, bf16[520,256]{1,0:T(8,128)(2,1)S(1)}, u32[]{:S(2)}, u32[]{:S(2)}) collective-permute-start(bf16[520,256]{1,0:T(8,128)(2,1)} %get-tuple-element.19.own), channel_id=1, source_target_pairs={{0,24},{8,0},{16,8},{24,16},{1,25},{9,1},{17,9},{25,17},{2,26},{10... | collective-permute-start | bytes 798728 | tf_op jit(solution)/shard_map/ppermute | solution.py:323
  13.2 9.9 %collective-permute-start.1 = (bf16[520,256]{1,0:T(8,128)(2,1)}, bf16[520,256]{1,0:T(8,128)(2,1)S(1)}, u32[]{:S(2)}, u32[]{:S(2)}) collective-permute-start(bf16[520,256]{1,0:T(8,128)(2,1)} %get-tuple-element.19.own), channel_id=1, source_target_pairs={{0,16},{8,24},{16,0},{24,8},{1,17},{9,25},{17,1},{25,9},{2,18},{10... | collective-permute-start | bytes 798728 | tf_op jit(solution)/shard_map/ppermute | solution.py:323
  15.7 14.5 %collective-permute-start = (bf16[520,256]{1,0:T(8,128)(2,1)}, bf16[520,256]{1,0:T(8,128)(2,1)S(1)}, u32[]{:S(2)}, u32[]{:S(2)}) collective-permute-start(bf16[520,256]{1,0:T(8,128)(2,1)} %get-tuple-element.19.own), channel_id=1, source_target_pairs={{0,8},{8,16},{16,24},{24,0},{1,9},{9,17},{17,25},{25,1},{2,10},{10... | collective-permute-start | bytes 798728 | tf_op jit(solution)/shard_map/ppermute | solution.py:323
  46.9 1.0 copy-start.1
  47.9 24.8 %all-to-all-start.3 = ((bf16[16,136,256]{2,1,0:T(8,128)(2,1)}), bf16[16,136,256]{2,1,0:T(8,128)(2,1)S(1)}, u32[]{:S(2)}, u32[]{:S(2)}) async-start(bf16[16,136,256]{2,1,0:T(8,128)(2,1)} %copy-done.1), calls=%async_computation.3 | async-start | bytes 2228224 | tf_op jit(solution)/shard_map/all_to_all | solution.py:357
  72.7 57.6 %copy-start.3 = (f32[768,256]{1,0:T(8,128)S(1)}, f32[768,256]{1,0:T(8,128)}, u32[]{:S(2)}) copy-start(f32[768,256]{1,0:T(8,128)} %second.1) | copy-start | bytes 2359300
  72.7 59.8 %all-to-all-start.2 = ((bf16[8,264,128]{2,1,0:T(8,128)(2,1)}), bf16[8,264,128]{2,1,0:T(8,128)(2,1)S(1)}, u32[]{:S(2)}, u32[]{:S(2)}) async-start(bf16[8,264,128]{2,1,0:T(8,128)(2,1)} %query_parts.1), calls=%async_computation.2 | async-start | bytes 1081344 | tf_op jit(solution)/shard_map/all_to_all | solution.py:384
  76.7 53.6 %copy-start = (f32[768,256]{1,0:T(8,128)S(1)}, f32[768,256]{1,0:T(8,128)}, u32[]{:S(2)}) copy-start(f32[768,256]{1,0:T(8,128)} %table.3) | copy-start | bytes 2359300
  76.7 53.6 %copy-start.2 = (f32[768,256]{1,0:T(8,128)S(1)}, f32[768,256]{1,0:T(8,128)}, u32[]{:S(2)}) copy-start(f32[768,256]{1,0:T(8,128)} %first.1) | copy-start | bytes 2359300
  76.9 26.7 %collective-permute-start.3 = (bf16[6,32,256]{2,1,0:T(8,128)(2,1)S(1)}, bf16[6,32,256]{2,1,0:T(8,128)(2,1)S(1)}, u32[]{:S(2)}, u32[]{:S(2)}) collective-permute-start(bf16[6,32,256]{2,1,0:T(8,128)(2,1)S(1)} %gather_parts.1), channel_id=1, source_target_pairs={{0,128},{1,385},{128,0},{129,257},{256,384},{257,129},{384,256},{3... | collective-permute-start | bytes 294920 | tf_op jit(solution)/shard_map/ppermute | solution.py:380
  103.6 9.3 %collective-permute-start.4 = (bf16[6,32,256]{2,1,0:T(8,128)(2,1)S(1)}, bf16[6,32,256]{2,1,0:T(8,128)(2,1)S(1)}, u32[]{:S(2)}, u32[]{:S(2)}) collective-permute-start(bf16[6,32,256]{2,1,0:T(8,128)(2,1)S(1)} %add_convert_fusion), channel_id=1, source_target_pairs={{0,384},{1,129},{128,256},{129,1},{256,128},{257,385},{384,0},{385... | collective-permute-start | bytes 294920 | tf_op jit(solution)/shard_map/ppermute | solution.py:382
  112.9 8.5 %collective-permute-start.7 = (f32[6,32,256]{2,1,0:T(8,128)S(1)}, f32[6,32,256]{2,1,0:T(8,128)S(1)}, u32[]{:S(2)}, u32[]{:S(2)}) collective-permute-start(f32[6,32,256]{2,1,0:T(8,128)S(1)} %convert_add_fusion.own), channel_id=1, source_target_pairs={{0,96},{32,0},{64,32},{96,64},{1,97},{33,1},{65,33},{97,65},{2,98}... | collective-permute-start | bytes 589832 | tf_op jit(solution)/shard_map/ppermute | solution.py:395
  115.8 10.3 %collective-permute-start.6 = (f32[6,32,256]{2,1,0:T(8,128)S(1)}, f32[6,32,256]{2,1,0:T(8,128)S(1)}, u32[]{:S(2)}, u32[]{:S(2)}) collective-permute-start(f32[6,32,256]{2,1,0:T(8,128)S(1)} %convert_add_fusion.own), channel_id=1, source_target_pairs={{0,64},{32,96},{64,0},{96,32},{1,65},{33,97},{65,1},{97,33},{2,66}... | collective-permute-start | bytes 589832 | tf_op jit(solution)/shard_map/ppermute | solution.py:395
  118.2 12.0 %collective-permute-start.5 = (f32[6,32,256]{2,1,0:T(8,128)S(1)}, f32[6,32,256]{2,1,0:T(8,128)S(1)}, u32[]{:S(2)}, u32[]{:S(2)}) collective-permute-start(f32[6,32,256]{2,1,0:T(8,128)S(1)} %convert_add_fusion.own), channel_id=1, source_target_pairs={{0,32},{32,64},{64,96},{96,0},{1,33},{33,65},{65,97},{97,1},{2,34}... | collective-permute-start | bytes 589832 | tf_op jit(solution)/shard_map/ppermute | solution.py:395

commit v8 on v7

--- a/solution.py
+++ b/solution.py
@@ -1,3 +1,5 @@
+import functools
+
 import jax
 import jax.numpy as jnp
 from jax import lax
@@ -271,12 +273,12 @@
     out[...] = total[...].astype(bf16)
 
 
-def adam_kernel(place, own, one, two, three, table, first, second, *rest):
-    outs, results, sems = rest[:3], rest[3:6], rest[6]
+def adam_kernel(steps, place, early, late, table, first, second, *rest):
+    outs, results, sems = rest[-7:-4], rest[-4:-1], rest[-1]
     copies = []
     for b in range(BLOCKS_DEV):
-        for k, piece in enumerate((own, one, two, three)):
-            y = (place[3] - k) & (NY - 1)
+        for n, piece in enumerate((early, late)):
+            y = (place[3] - steps[n]) & (NY - 1)
             rows = pl.ds(pl.multiple_of(b * BLOCK + y * PART, PART), PART)
             grad = piece[b]
             first_new = beta_first * first[rows, :] + (1.0 - beta_first) * grad
@@ -286,11 +288,10 @@
             results[0][rows, :] = table[rows, :] - learn_rate * (first_new / bias_first) / (
                 jnp.sqrt(second_new / bias_second) + adam_eps
             )
-        block = pl.ds(b * BLOCK, BLOCK)
-        for n in range(3):
-            copy = pltpu.make_async_copy(results[n].at[block, :], outs[n].at[block, :], sems.at[b, n])
-            copy.start()
-            copies.append(copy)
+            for m in range(3):
+                copy = pltpu.make_async_copy(results[m].at[rows, :], outs[m].at[rows, :], sems.at[b, n, m])
+                copy.start()
+                copies.append(copy)
     for copy in copies:
         copy.wait()
 
@@ -394,15 +395,20 @@
     for k in range(1, NY):
         grads.append(lax.ppermute(part, "y", [(i, (i + k) % NY) for i in range(NY)]))
 
-    new_table, new_first, new_second = pl.pallas_call(
-        adam_kernel,
-        out_shape=(jax.ShapeDtypeStruct(table.shape, f32),) * 3,
-        in_specs=[smem()] + [vmem()] * (NY + 3),
-        out_specs=(hbm(),) * 3,
-        scratch_shapes=[pltpu.VMEM(table.shape, f32)] * 3 + [pltpu.SemaphoreType.DMA((BLOCKS_DEV, 3))],
-        compiler_params=limit(12),
-        name="adam",
-    )(where, *grads, table, first_moment, second_moment)
+    def adam(steps, before):
+        return pl.pallas_call(
+            functools.partial(adam_kernel, steps),
+            out_shape=(jax.ShapeDtypeStruct(table.shape, f32),) * 3,
+            in_specs=[smem()] + [vmem()] * 5 + [hbm()] * len(before),
+            out_specs=(hbm(),) * 3,
+            scratch_shapes=[pltpu.VMEM(table.shape, f32)] * 3 + [pltpu.SemaphoreType.DMA((BLOCKS_DEV, 2, 3))],
+            input_output_aliases={6 + n: n for n in range(len(before))},
+            compiler_params=limit(12),
+            cost_estimate=pl.CostEstimate(flops=1 << 22, bytes_accessed=3 << 20, transcendentals=0),
+        )(where, grads[steps[0]], grads[steps[1]], table, first_moment, second_moment, *before)
+
+    new = adam((0, 2), ())
+    new_table, new_first, new_second = adam((1, 3), new)
     return loss, query_grad, new_table, new_first, new_second
 
 

time: 134 us -> 132 us (0.985)
  waiting for transfers between devices: 55.1 us -> 50.7 us
  Pallas kernels: 15.1 us -> 16.7 us
    ppermute x3, waiting for transfers between devices: 10 us -> 5.64 us  [step(): lax.ppermute(part, 'y', [(i, (i + k) % NY) for i in range(NY)])]
    pallas_call x1 -> x2, Pallas kernels: 2.19 us -> 3.77 us  [adam(): pl.pallas_call(functools.partial(adam_kernel, steps), out_shape=(jax.Shap...]
  transfers between devices with their start and end apart: 11 -> 11, of which waited for: 8 -> 8; matrix products, arithmetic and copies ran while one was open for 0% -> 0% of each run, Pallas kernels for 5% -> 6%
where the time goes in v8:
time: 132 us
  waiting for transfers between devices  50.7 us (38%)
  starting transfers between devices  45.8 us (35%)
  Pallas kernels  16.7 us (13%)
  blocking collectives  15.8 us (12%)
  between operations  1.44 us (1%)
    all_to_all x1, waiting for transfers between devices, step(): item_parts = lax.all_to_all(item_parts, ('y', 'x'), 0, 0, tiled=True)  15.5 us
    ppermute x1, waiting for transfers between devices, step(): other = lax.ppermute(part, ('zh', 'c'), first)  14.7 us
    ppermute x1, starting transfers between devices, step(): other = lax.ppermute(part, ('zh', 'c'), first)  12 us
    all_to_all x1, blocking collectives, step(): stats = lax.all_to_all(stats, QROWS, 0, 0, tiled=True)  11.5 us
    ppermute x3, starting transfers between devices, step(): lax.ppermute(items, 'x', [(i, (i + k) % NX) for i in range(NX)])  9.32 us
    ppermute x3, starting transfers between devices, step(): lax.ppermute(part, 'y', [(i, (i + k) % NY) for i in range(NY)])  7.93 us
    ppermute x3, waiting for transfers between devices, step(): lax.ppermute(items, 'x', [(i, (i + k) % NX) for i in range(NX)])  7.53 us
    ppermute x1, waiting for transfers between devices, step(): other = lax.ppermute(part, ('zh', 'c'), second)  7.34 us
  transfers between devices with their start and end apart: 11, of which 8 were waited for; matrix products, arithmetic and copies ran while one was open for 0% of the time, Pallas kernels for 6%

profile of v8, /device:TPU:33, one launch (start us, length us, event | category | flops | bytes accessed | tf_op | source)
XLA Modules:
  0.0 131.7 jit_solution(7255423456131313530)
XLA Ops:
  1.3 2.0 %pack.1 = (bf16[520,256]{1,0:T(8,128)(2,1)}, bf16[4,136,256]{2,1,0:T(8,128)(2,1)}) custom-call(s32[1,4]{1,0:T(1,128)} %ids.1, s32[1,1]{1,0:T(1,128)S(6)} %copy.19.count, f32[1,4]{1,0:T(1,128)} %logq.1, f32[768,256]{1,0:T(8,128)} %table.5, bf16[1,128,256]{2,1,0:T(8,128)(2,1)} %queries.1, s32[1,128]{1,0:T(1,128)} %targets.1), custom_call_target="tpu_custom_call" | custom-call | tf_op jit(solution)/shard_map/pack/pallas_call | solution.py:313
  3.3 0.0 copy-start.4
  3.3 5.6 %all-to-all-start = ((bf16[4,136,256]{2,1,0:T(8,128)(2,1)}), bf16[4,136,256]{2,1,0:T(8,128)(2,1)S(1)}, u32[]{:S(2)}, u32[]{:S(2)}) async-start(bf16[4,136,256]{2,1,0:T(8,128)(2,1)} %get-tuple-element.23), calls=%async_computation | async-start | bytes 557056 | tf_op jit(solution)/shard_map/all_to_all | solution.py:321
  8.9 4.4 %collective-permute-start.2 = (bf16[520,256]{1,0:T(8,128)(2,1)}, bf16[520,256]{1,0:T(8,128)(2,1)S(1)}, u32[]{:S(2)}, u32[]{:S(2)}) collective-permute-start(bf16[520,256]{1,0:T(8,128)(2,1)} %get-tuple-element.22.own), channel_id=1, source_target_pairs={{0,24},{8,0},{16,8},{24,16},{1,25},{9,1},{17,9},{25,17},{2,26},{10... | collective-permute-start | bytes 798728 | tf_op jit(solution)/shard_map/ppermute | solution.py:324
  13.2 2.4 %collective-permute-start.1 = (bf16[520,256]{1,0:T(8,128)(2,1)}, bf16[520,256]{1,0:T(8,128)(2,1)S(1)}, u32[]{:S(2)}, u32[]{:S(2)}) collective-permute-start(bf16[520,256]{1,0:T(8,128)(2,1)} %get-tuple-element.22.own), channel_id=1, source_target_pairs={{0,16},{8,24},{16,0},{24,8},{1,17},{9,25},{17,1},{25,9},{2,18},{10... | collective-permute-start | bytes 798728 | tf_op jit(solution)/shard_map/ppermute | solution.py:324
  15.7 2.5 %collective-permute-start = (bf16[520,256]{1,0:T(8,128)(2,1)}, bf16[520,256]{1,0:T(8,128)(2,1)S(1)}, u32[]{:S(2)}, u32[]{:S(2)}) collective-permute-start(bf16[520,256]{1,0:T(8,128)(2,1)} %get-tuple-element.22.own), channel_id=1, source_target_pairs={{0,8},{8,16},{16,24},{24,0},{1,9},{9,17},{17,25},{25,1},{2,10},{10... | collective-permute-start | bytes 798728 | tf_op jit(solution)/shard_map/ppermute | solution.py:324
  18.2 0.1 pad_add_fusion.place
  18.3 0.0 all-to-all-done
  18.3 4.4 %all_gather.3.queries = bf16[8,136,256]{2,1,0:T(8,128)(2,1)S(1)} all-gather(bf16[4,136,256]{2,1,0:T(8,128)(2,1)S(1)} %all-to-all-done), channel_id=1, replica_groups=mesh['zh'=4,'y'=4,'x'=4,'zl'=4,'c'=2] {'c'}, dimensions={0}, use_global_device_ids=true | all-gather | bytes 835584 | tf_op jit(solution)/shard_map/all_gather | solution.py:325
  22.6 0.0 collective-permute-done.2.three
  22.7 0.5 collective-permute-done.1.two
  23.2 7.0 %collective-permute-done.one = bf16[520,256]{1,0:T(8,128)(2,1)S(1)} collective-permute-done((bf16[520,256]{1,0:T(8,128)(2,1)}, bf16[520,256]{1,0:T(8,128)(2,1)S(1)}, u32[]{:S(2)}, u32[]{:S(2)}) %collective-permute-start) | collective-permute-done | bytes 266272 | tf_op jit(solution)/shard_map/ppermute | solution.py:324
  30.2 0.0 copy-done.4
  30.2 2.8 %totals.1 = (f32[8,8,128]{2,1,0:T(8,128)S(1)}, bf16[17,128,256]{2,1,0:T(8,128)(2,1)S(1)}, bf16[4,8,256]{2,1,0:T(8,128)(2,1)S(1)}, s32[18]{0:T(128)S(1)}, f32[17]{0:T(128)S(1)}) custom-call(s32[4]{0:T(128)S(1)} %pad_add_fusion.place, bf16[520,256]{1,0:T(8,128)(2,1)S(1)} %copy-done.4, bf16[520,256]{1,0:T(8,128)(2,1)S(1)} %collective-permute-done.one, ...), custom_call_target="tpu_custom_call" | custom-call | tf_op jit(solution)/shard_map/totals/pallas_call | solution.py:328
  32.9 11.5 %all_to_all.20.stats = f32[8,8,128]{2,1,0:T(8,128)S(1)} all-to-all(f32[8,8,128]{2,1,0:T(8,128)S(1)} %get-tuple-element.28), channel_id=1, replica_groups=mesh['zh'=4,'y'=4,'x'=4,'zl'=4,'c'=2] {'c','zl'}, dimensions={0} | all-to-all | bytes 65536 | tf_op jit(solution)/shard_map/all_to_all | solution.py:344
  44.4 2.5 %items.1 = (bf16[16,136,256]{2,1,0:T(8,128)(2,1)S(1)}, f32[1,1024]{1,0:T(1,128)S(1)}) custom-call(s32[4]{0:T(128)S(1)} %pad_add_fusion.place, s32[18]{0:T(128)S(1)} %get-tuple-element.24.live, f32[17]{0:T(128)S(1)} %get-tuple-element.25.shifts, bf16[17,128,256]{2,1,0:T(8,128)(2,1)S(1)} %get-tuple-element.26.rows_all, ...), custom_call_target="tpu_custom_call" | custom-call | tf_op jit(solution)/shard_map/items/pallas_call | solution.py:345
  46.9 0.0 copy-start.3
  46.9 1.0 copy-done.3
  47.9 5.1 %all-to-all-start.3 = ((bf16[16,136,256]{2,1,0:T(8,128)(2,1)}), bf16[16,136,256]{2,1,0:T(8,128)(2,1)S(1)}, u32[]{:S(2)}, u32[]{:S(2)}) async-start(bf16[16,136,256]{2,1,0:T(8,128)(2,1)} %copy-done.3), calls=%async_computation.3 | async-start | bytes 2228224 | tf_op jit(solution)/shard_map/all_to_all | solution.py:358
  53.1 4.1 %query_parts.1 = bf16[8,264,128]{2,1,0:T(8,128)(2,1)} custom-call(s32[18]{0:T(128)S(1)} %get-tuple-element.24.live, f32[17]{0:T(128)S(1)} %get-tuple-element.25.shifts, bf16[17,128,256]{2,1,0:T(8,128)(2,1)S(1)} %get-tuple-element.26.rows_all, bf16[8,136,256]{2,1,0:T(8,128)(2,1)S(1)} %all_gather.3.queries, f32[1,1024]{1,0:T(1,128)S(1)} %get-tuple-element.29.norms), custom_call_target="tpu_custom_call" | custom-call | flops 2147483648 | bytes 6291456 | tf_op jit(solution)/shard_map/query_parts/pallas_call | solution.py:359
  57.2 15.5 %all-to-all-done.3.parts = bf16[16,136,256]{2,1,0:T(8,128)(2,1)S(1)} async-done(((bf16[16,136,256]{2,1,0:T(8,128)(2,1)}), bf16[16,136,256]{2,1,0:T(8,128)(2,1)S(1)}, u32[]{:S(2)}, u32[]{:S(2)}) %all-to-all-start.3) | async-done | bytes 1114144 | tf_op jit(solution)/shard_map/all_to_all | solution.py:358
  72.7 0.0 copy-start.2
  72.7 3.9 %all-to-all-start.2 = ((bf16[8,264,128]{2,1,0:T(8,128)(2,1)}), bf16[8,264,128]{2,1,0:T(8,128)(2,1)S(1)}, u32[]{:S(2)}, u32[]{:S(2)}) async-start(bf16[8,264,128]{2,1,0:T(8,128)(2,1)} %query_parts.1), calls=%async_computation.2 | async-start | bytes 1081344 | tf_op jit(solution)/shard_map/all_to_all | solution.py:385
  76.6 0.0 copy-start
  76.7 0.0 copy-start.1
  76.7 0.2 gather_parts.1
  76.9 12.0 %collective-permute-start.3 = (bf16[6,32,256]{2,1,0:T(8,128)(2,1)S(1)}, bf16[6,32,256]{2,1,0:T(8,128)(2,1)S(1)}, u32[]{:S(2)}, u32[]{:S(2)}) collective-permute-start(bf16[6,32,256]{2,1,0:T(8,128)(2,1)S(1)} %gather_parts.1), channel_id=1, source_target_pairs={{0,128},{1,385},{128,0},{129,257},{256,384},{257,129},{384,256},{3... | collective-permute-start | bytes 294920 | tf_op jit(solution)/shard_map/ppermute | solution.py:381
  88.9 14.7 %collective-permute-done.3 = bf16[6,32,256]{2,1,0:T(8,128)(2,1)S(1)} collective-permute-done((bf16[6,32,256]{2,1,0:T(8,128)(2,1)S(1)}, bf16[6,32,256]{2,1,0:T(8,128)(2,1)S(1)}, u32[]{:S(2)}, u32[]{:S(2)}) %collective-permute-start.3) | collective-permute-done | bytes 98336 | tf_op jit(solution)/shard_map/ppermute | solution.py:381
  103.6 1.9 %collective-permute-start.4 = (bf16[6,32,256]{2,1,0:T(8,128)(2,1)S(1)}, bf16[6,32,256]{2,1,0:T(8,128)(2,1)S(1)}, u32[]{:S(2)}, u32[]{:S(2)}) collective-permute-start(bf16[6,32,256]{2,1,0:T(8,128)(2,1)S(1)} %add_convert_fusion), channel_id=1, source_target_pairs={{0,384},{1,129},{128,256},{129,1},{256,128},{257,385},{384,0},{385... | collective-permute-start | bytes 294920 | tf_op jit(solution)/shard_map/ppermute | solution.py:383
  105.6 7.3 %collective-permute-done.4 = bf16[6,32,256]{2,1,0:T(8,128)(2,1)S(1)} collective-permute-done((bf16[6,32,256]{2,1,0:T(8,128)(2,1)S(1)}, bf16[6,32,256]{2,1,0:T(8,128)(2,1)S(1)}, u32[]{:S(2)}, u32[]{:S(2)}) %collective-permute-start.4) | collective-permute-done | bytes 98336 | tf_op jit(solution)/shard_map/ppermute | solution.py:383
  112.9 2.6 %collective-permute-start.7 = (f32[6,32,256]{2,1,0:T(8,128)S(1)}, f32[6,32,256]{2,1,0:T(8,128)S(1)}, u32[]{:S(2)}, u32[]{:S(2)}) collective-permute-start(f32[6,32,256]{2,1,0:T(8,128)S(1)} %convert_add_fusion.early), channel_id=1, source_target_pairs={{0,64},{32,96},{64,0},{96,32},{1,65},{33,97},{65,1},{97,33},{2,66}... | collective-permute-start | bytes 589832 | tf_op jit(solution)/shard_map/ppermute | solution.py:396
  115.6 3.3 %collective-permute-start.6 = (f32[6,32,256]{2,1,0:T(8,128)S(1)}, f32[6,32,256]{2,1,0:T(8,128)S(1)}, u32[]{:S(2)}, u32[]{:S(2)}) collective-permute-start(f32[6,32,256]{2,1,0:T(8,128)S(1)} %convert_add_fusion.early), channel_id=1, source_target_pairs={{0,96},{32,0},{64,32},{96,64},{1,97},{33,1},{65,33},{97,65},{2,98}... | collective-permute-start | bytes 589832 | tf_op jit(solution)/shard_map/ppermute | solution.py:396
  118.8 2.0 %collective-permute-start.5 = (f32[6,32,256]{2,1,0:T(8,128)S(1)}, f32[6,32,256]{2,1,0:T(8,128)S(1)}, u32[]{:S(2)}, u32[]{:S(2)}) collective-permute-start(f32[6,32,256]{2,1,0:T(8,128)S(1)} %convert_add_fusion.early), channel_id=1, source_target_pairs={{0,32},{32,64},{64,96},{96,0},{1,33},{33,65},{65,97},{97,1},{2,34}... | collective-permute-start | bytes 589832 | tf_op jit(solution)/shard_map/ppermute | solution.py:396
  120.9 1.7 %collective-permute-done.7.late = f32[6,32,256]{2,1,0:T(8,128)S(1)} collective-permute-done((f32[6,32,256]{2,1,0:T(8,128)S(1)}, f32[6,32,256]{2,1,0:T(8,128)S(1)}, u32[]{:S(2)}, u32[]{:S(2)}) %collective-permute-start.7) | collective-permute-done | bytes 196640 | tf_op jit(solution)/shard_map/ppermute | solution.py:396
  122.6 0.0 copy-done.2
  122.6 0.0 copy-done
  122.6 0.0 copy-done.1
  122.6 1.9 %shard_map.119 = (f32[768,256]{1,0:T(8,128)}, f32[768,256]{1,0:T(8,128)}, f32[768,256]{1,0:T(8,128)}) custom-call(s32[4]{0:T(128)S(1)} %pad_add_fusion.place, f32[6,32,256]{2,1,0:T(8,128)S(1)} %convert_add_fusion.early, f32[6,32,256]{2,1,0:T(8,128)S(1)} %collective-permute-done.7.late, f32[768,256]{1,0:T(8,128)S(1)} %copy-done, f32[768,256]{1,0:T(8,128)S(1)} %copy-done.1, ...), custom_call_target="tpu_custom_call" | custom-call | flops 4194304 | bytes 3145728 | tf_op jit(solution)/shard_map/pallas_call | solution.py:399
  124.5 1.3 collective-permute-done.6.late
  125.8 2.6 %collective-permute-done.5.early = f32[6,32,256]{2,1,0:T(8,128)S(1)} collective-permute-done((f32[6,32,256]{2,1,0:T(8,128)S(1)}, f32[6,32,256]{2,1,0:T(8,128)S(1)}, u32[]{:S(2)}, u32[]{:S(2)}) %collective-permute-start.5) | collective-permute-done | bytes 196640 | tf_op jit(solution)/shard_map/ppermute | solution.py:396
  128.4 1.9 %shard_map.120 = (f32[768,256]{1,0:T(8,128)}, f32[768,256]{1,0:T(8,128)}, f32[768,256]{1,0:T(8,128)}) custom-call(s32[4]{0:T(128)S(1)} %pad_add_fusion.place, f32[6,32,256]{2,1,0:T(8,128)S(1)} %collective-permute-done.5.early, f32[6,32,256]{2,1,0:T(8,128)S(1)} %collective-permute-done.6.late, ...), custom_call_target="tpu_custom_call", output_to_operand_aliasing={{0}: (6, {}), {1}: (7, {}), {2}: (8, {})} | custom-call | flops 4194304 | bytes 3145728 | tf_op jit(solution)/shard_map/pallas_call | solution.py:399
  130.3 0.0 all-to-all-done.2.parts
  130.3 1.3 %query_sum.1 = (f32[1,128]{1,0:T(1,128)}, f32[1,128,256]{2,1,0:T(8,128)}) custom-call(s32[4]{0:T(128)S(1)} %pad_add_fusion.place, f32[1,1024]{1,0:T(1,128)S(1)} %get-tuple-element.29.norms, bf16[8,264,128]{2,1,0:T(8,128)(2,1)S(1)} %all-to-all-done.2.parts), custom_call_target="tpu_custom_call" | custom-call | tf_op jit(solution)/shard_map/query_sum/pallas_call | solution.py:386
  (2 shorter events, 0.1 us)
Async XLA Ops:
  3.3 26.9 %copy-start.4 = (bf16[520,256]{1,0:T(8,128)(2,1)S(1)}, bf16[520,256]{1,0:T(8,128)(2,1)}, u32[]{:S(2)}) copy-start(bf16[520,256]{1,0:T(8,128)(2,1)} %get-tuple-element.22.own) | copy-start | bytes 798724
  3.3 15.0 %all-to-all-start = ((bf16[4,136,256]{2,1,0:T(8,128)(2,1)}), bf16[4,136,256]{2,1,0:T(8,128)(2,1)S(1)}, u32[]{:S(2)}, u32[]{:S(2)}) async-start(bf16[4,136,256]{2,1,0:T(8,128)(2,1)} %get-tuple-element.23), calls=%async_computation | async-start | bytes 557056 | tf_op jit(solution)/shard_map/all_to_all | solution.py:321
  8.9 13.8 %collective-permute-start.2 = (bf16[520,256]{1,0:T(8,128)(2,1)}, bf16[520,256]{1,0:T(8,128)(2,1)S(1)}, u32[]{:S(2)}, u32[]{:S(2)}) collective-permute-start(bf16[520,256]{1,0:T(8,128)(2,1)} %get-tuple-element.22.own), channel_id=1, source_target_pairs={{0,24},{8,0},{16,8},{24,16},{1,25},{9,1},{17,9},{25,17},{2,26},{10... | collective-permute-start | bytes 798728 | tf_op jit(solution)/shard_map/ppermute | solution.py:324
  13.2 9.9 %collective-permute-start.1 = (bf16[520,256]{1,0:T(8,128)(2,1)}, bf16[520,256]{1,0:T(8,128)(2,1)S(1)}, u32[]{:S(2)}, u32[]{:S(2)}) collective-permute-start(bf16[520,256]{1,0:T(8,128)(2,1)} %get-tuple-element.22.own), channel_id=1, source_target_pairs={{0,16},{8,24},{16,0},{24,8},{1,17},{9,25},{17,1},{25,9},{2,18},{10... | collective-permute-start | bytes 798728 | tf_op jit(solution)/shard_map/ppermute | solution.py:324
  15.7 14.5 %collective-permute-start = (bf16[520,256]{1,0:T(8,128)(2,1)}, bf16[520,256]{1,0:T(8,128)(2,1)S(1)}, u32[]{:S(2)}, u32[]{:S(2)}) collective-permute-start(bf16[520,256]{1,0:T(8,128)(2,1)} %get-tuple-element.22.own), channel_id=1, source_target_pairs={{0,8},{8,16},{16,24},{24,0},{1,9},{9,17},{17,25},{25,1},{2,10},{10... | collective-permute-start | bytes 798728 | tf_op jit(solution)/shard_map/ppermute | solution.py:324
  46.9 1.0 copy-start.3
  47.9 24.8 %all-to-all-start.3 = ((bf16[16,136,256]{2,1,0:T(8,128)(2,1)}), bf16[16,136,256]{2,1,0:T(8,128)(2,1)S(1)}, u32[]{:S(2)}, u32[]{:S(2)}) async-start(bf16[16,136,256]{2,1,0:T(8,128)(2,1)} %copy-done.3), calls=%async_computation.3 | async-start | bytes 2228224 | tf_op jit(solution)/shard_map/all_to_all | solution.py:358
  72.7 49.9 %copy-start.2 = (f32[768,256]{1,0:T(8,128)S(1)}, f32[768,256]{1,0:T(8,128)}, u32[]{:S(2)}) copy-start(f32[768,256]{1,0:T(8,128)} %second.3) | copy-start | bytes 2359300
  72.7 57.6 %all-to-all-start.2 = ((bf16[8,264,128]{2,1,0:T(8,128)(2,1)}), bf16[8,264,128]{2,1,0:T(8,128)(2,1)S(1)}, u32[]{:S(2)}, u32[]{:S(2)}) async-start(bf16[8,264,128]{2,1,0:T(8,128)(2,1)} %query_parts.1), calls=%async_computation.2 | async-start | bytes 1081344 | tf_op jit(solution)/shard_map/all_to_all | solution.py:385
  76.6 46.0 %copy-start = (f32[768,256]{1,0:T(8,128)S(1)}, f32[768,256]{1,0:T(8,128)}, u32[]{:S(2)}) copy-start(f32[768,256]{1,0:T(8,128)} %table.5) | copy-start | bytes 2359300
  76.7 46.0 %copy-start.1 = (f32[768,256]{1,0:T(8,128)S(1)}, f32[768,256]{1,0:T(8,128)}, u32[]{:S(2)}) copy-start(f32[768,256]{1,0:T(8,128)} %first.3) | copy-start | bytes 2359300
  76.9 26.7 %collective-permute-start.3 = (bf16[6,32,256]{2,1,0:T(8,128)(2,1)S(1)}, bf16[6,32,256]{2,1,0:T(8,128)(2,1)S(1)}, u32[]{:S(2)}, u32[]{:S(2)}) collective-permute-start(bf16[6,32,256]{2,1,0:T(8,128)(2,1)S(1)} %gather_parts.1), channel_id=1, source_target_pairs={{0,128},{1,385},{128,0},{129,257},{256,384},{257,129},{384,256},{3... | collective-permute-start | bytes 294920 | tf_op jit(solution)/shard_map/ppermute | solution.py:381
  103.6 9.3 %collective-permute-start.4 = (bf16[6,32,256]{2,1,0:T(8,128)(2,1)S(1)}, bf16[6,32,256]{2,1,0:T(8,128)(2,1)S(1)}, u32[]{:S(2)}, u32[]{:S(2)}) collective-permute-start(bf16[6,32,256]{2,1,0:T(8,128)(2,1)S(1)} %add_convert_fusion), channel_id=1, source_target_pairs={{0,384},{1,129},{128,256},{129,1},{256,128},{257,385},{384,0},{385... | collective-permute-start | bytes 294920 | tf_op jit(solution)/shard_map/ppermute | solution.py:383
  112.9 9.7 %collective-permute-start.7 = (f32[6,32,256]{2,1,0:T(8,128)S(1)}, f32[6,32,256]{2,1,0:T(8,128)S(1)}, u32[]{:S(2)}, u32[]{:S(2)}) collective-permute-start(f32[6,32,256]{2,1,0:T(8,128)S(1)} %convert_add_fusion.early), channel_id=1, source_target_pairs={{0,64},{32,96},{64,0},{96,32},{1,65},{33,97},{65,1},{97,33},{2,66}... | collective-permute-start | bytes 589832 | tf_op jit(solution)/shard_map/ppermute | solution.py:396
  115.6 10.2 %collective-permute-start.6 = (f32[6,32,256]{2,1,0:T(8,128)S(1)}, f32[6,32,256]{2,1,0:T(8,128)S(1)}, u32[]{:S(2)}, u32[]{:S(2)}) collective-permute-start(f32[6,32,256]{2,1,0:T(8,128)S(1)} %convert_add_fusion.early), channel_id=1, source_target_pairs={{0,96},{32,0},{64,32},{96,64},{1,97},{33,1},{65,33},{97,65},{2,98}... | collective-permute-start | bytes 589832 | tf_op jit(solution)/shard_map/ppermute | solution.py:396
  118.8 9.6 %collective-permute-start.5 = (f32[6,32,256]{2,1,0:T(8,128)S(1)}, f32[6,32,256]{2,1,0:T(8,128)S(1)}, u32[]{:S(2)}, u32[]{:S(2)}) collective-permute-start(f32[6,32,256]{2,1,0:T(8,128)S(1)} %convert_add_fusion.early), channel_id=1, source_target_pairs={{0,32},{32,64},{64,96},{96,0},{1,33},{33,65},{65,97},{97,1},{2,34}... | collective-permute-start | bytes 589832 | tf_op jit(solution)/shard_map/ppermute | solution.py:396
